TPU v7x, 32 devices: a whole 2x2x4 slice. The times are simulated.
32 devices in a mesh: groups: 2 (over y), row: 2 (over x), col: 4 (over z), dp: 2 (over core).
Axes of the slice: x: 2, y: 2, z: 4, core: 2. Of those that a mesh axis runs over, the one named last changes fastest.
Arguments:
- features: bfloat16 [4, 512, 6144], P(('groups', 'dp'), 'row', 'col'), parts along dimension 0, may hold values from -6 to 6
- output_gradient: bfloat16 [4, 512, 6144], P(('groups', 'dp'), 'row', 'col'), parts along dimension 0, may hold values from -6 to 6
- value_weight: bfloat16 [6144, 6144], P('row', 'col'), may hold values from -0.109375 to 0.109375
- gate_weight: bfloat16 [6144, 6144], P('row', 'col'), may hold values from -1 to 1
- mixer_weight: bfloat16 [6144, 6144], P('row', 'col'), may hold values from -0.109375 to 0.109375
- conv_kernel: float32 [31, 6144], P(None, 'col'), may hold values from -1 to 1
- layer_norm_gain: float32 [6144], replicated, may hold values from 0.3 to 4.2
Outputs:
- module_out: bfloat16 [4, 512, 6144], P(('groups', 'dp'), 'row', 'col'), parts along dimension 0
- input_gradient: bfloat16 [4, 512, 6144], P(('groups', 'dp'), 'row', 'col'), parts along dimension 0
- value_weight_grad: float32 [12288, 6144], P(('groups', 'row', 'dp'), 'col'), parts along dimension 0
- gate_weight_grad: float32 [12288, 6144], P(('groups', 'row', 'dp'), 'col'), parts along dimension 0
- mixer_weight_grad: float32 [12288, 6144], P(('groups', 'row', 'dp'), 'col'), parts along dimension 0
- kernel_grad: float32 [62, 6144], P('groups', 'col'), parts along dimension 0
- norm_gain_gradient: float32 [12288], P(('groups', 'col')), parts along dimension 0
There are 2 independent parts, one for each index of `groups`. A program takes and returns all parts, laid end to end along the dimension named above; an argument that names none is the same for every part. Nothing has to cross between parts.
All inputs are finite; a program needn't handle non-finite values.
Results may differ from a plain program's by a relative error of at most 0.02.
Values may be sent and summed in bfloat16 or wider, within the bound.
A program may use at most 320 MiB of HBM per device.

v0:
```python
import jax
import jax.numpy as jnp
from jax import lax
from jax.sharding import PartitionSpec as P

EPS = 1e-05
CONTRACT_LAST = (((1,), (1,)), ((), ()))
CONTRACT_FIRST = (((0,), (0,)), ((), ()))
BF16 = jnp.bfloat16
F32 = jnp.float32


def ring(count, shift):
    return [(i, (i + shift) % count) for i in range(count)]


def gather_over(x, axis):
    count, me = lax.axis_size(axis), lax.axis_index(axis)
    pieces = [x] + [lax.ppermute(x, axis, ring(count, s)) for s in range(1, count)]
    ordered = []
    for j in range(count):
        back = (me - j) % count
        block = pieces[0]
        for s in range(1, count):
            block = jnp.where(back == s, pieces[s], block)
        ordered.append(block)
    return ordered


def scatter_over(part, axis, dim, dtype):
    count, me = lax.axis_size(axis), lax.axis_index(axis)
    width = part.shape[dim] // count
    total = lax.dynamic_slice_in_dim(part, me * width, width, dim)
    for s in range(1, count):
        sent = lax.dynamic_slice_in_dim(part, ((me + s) % count) * width, width, dim)
        total = total + lax.ppermute(sent.astype(dtype), axis, ring(count, s)).astype(F32)
    return total


def spread_over(x, axis, dim):
    count, me = lax.axis_size(axis), lax.axis_index(axis)
    width = x.shape[dim] // count
    blocks = [lax.dynamic_slice_in_dim(x, me * width, width, dim)]
    for s in range(1, count):
        sent = lax.dynamic_slice_in_dim(x, ((me + s) % count) * width, width, dim)
        blocks.append(lax.ppermute(sent, axis, ring(count, s)))
    return jnp.concatenate(blocks, axis=0)


def collect_over(x, axis):
    count = lax.axis_size(axis)
    return jnp.concatenate(
        [x] + [lax.ppermute(x, axis, ring(count, s)) for s in range(1, count)], axis=0
    )


def shards(
    features, output_gradient, value_weight, gate_weight, mixer_weight, conv_kernel, layer_norm_gain
):
    utts, frames, width = features.shape
    taps = conv_kernel.shape[0]
    half = taps // 2
    model = layer_norm_gain.shape[0]
    n_row, n_col = lax.axis_size("row"), lax.axis_size("col")
    row, col = lax.axis_index("row"), lax.axis_index("col")
    per_row = n_col // n_row
    depth = per_row * width
    narrow = width // n_row
    span = n_row * frames
    cells = utts * span
    turned = [
        (r * n_col + h * per_row + i, h * n_col + r * per_row + i)
        for r in range(n_row)
        for h in range(n_row)
        for i in range(per_row)
    ]

    def turn(x):
        return lax.ppermute(x, ("row", "col"), turned)

    own = features.astype(F32)
    block_mean = jnp.mean(own, -1)
    block_square = jnp.sum((own - block_mean[..., None]) ** 2, -1)
    stats = lax.all_gather(jnp.stack([block_mean, block_square]), ("row", "col"), axis=0)
    stats = stats.reshape(n_row, n_col, 2, utts, frames)
    mean = jnp.mean(stats[:, :, 0], 1)
    square = jnp.sum(stats[:, :, 1] + width * (stats[:, :, 0] - mean[:, None]) ** 2, 1)
    inverse = lax.rsqrt(square / model + EPS)
    mean_own = lax.dynamic_index_in_dim(mean, row, 0, keepdims=False)[..., None]
    inverse_own = lax.dynamic_index_in_dim(inverse, row, 0, keepdims=False)[..., None]
    mean_all, inverse_all = (
        jnp.swapaxes(s, 0, 1)[:, :, :, None, None] for s in (mean, inverse)
    )

    inputs = lax.all_gather(turn(features), "col", axis=0)
    inputs = inputs.reshape(n_row, per_row, utts, frames, width).transpose(2, 0, 3, 1, 4)
    gain_rows = lax.dynamic_slice_in_dim(layer_norm_gain, row * depth, depth, 0)
    normed = (
        ((inputs.astype(F32) - mean_all) * inverse_all * gain_rows.reshape(per_row, width))
        .astype(BF16)
        .reshape(cells, depth)
    )
    gate_part = jnp.dot(normed, gate_weight, preferred_element_type=F32)
    gate = scatter_over(gate_part, "row", 1, GATE_DTYPE)
    value_part = jnp.dot(normed, value_weight, preferred_element_type=F32)
    value = scatter_over(value_part, "row", 1, BF16)

    grad_rows = jnp.stack(gather_over(output_gradient, "row"), axis=1).reshape(cells, width)
    mixed_part = lax.dot_general(
        grad_rows, mixer_weight, CONTRACT_LAST, preferred_element_type=F32
    ).astype(BF16)
    mixed_part = mixed_part.reshape(cells, per_row, n_row, narrow).transpose(2, 1, 0, 3)
    mixed_grad = turn(
        lax.psum_scatter(
            mixed_part.reshape(n_col * cells, narrow), "col", scatter_dimension=0, tiled=True
        )
    )
    mixed_grad = mixed_grad.astype(F32).reshape(utts, span, narrow)

    kernel_own = lax.dynamic_slice_in_dim(conv_kernel, row * narrow, narrow, 1)
    sig_gate = jax.nn.sigmoid(gate)
    glu = (value * sig_gate).astype(BF16).reshape(utts, span, narrow)
    glu_pad = jnp.pad(glu, ((0, 0), (half, half), (0, 0)))
    conv = jnp.zeros((utts, span, narrow), F32)
    for tap in range(taps):
        conv = conv + kernel_own[tap] * glu_pad[:, tap : tap + span].astype(F32)
    sig_conv = jax.nn.sigmoid(conv)
    mixed = (conv * sig_conv).astype(BF16)
    conv_grad = (mixed_grad * (sig_conv * (1.0 + conv * (1.0 - sig_conv)))).astype(BF16)

    grad_pad = jnp.pad(conv_grad, ((0, 0), (half, half), (0, 0)))
    conv_grad_float = conv_grad.astype(F32)
    glu_grad = jnp.zeros((utts, span, narrow), F32)
    kernel_rows = []
    for tap in range(taps):
        back = 2 * half - tap
        glu_grad = glu_grad + kernel_own[tap] * grad_pad[:, back : back + span].astype(F32)
        kernel_rows.append(
            jnp.sum(glu_pad[:, tap : tap + span].astype(F32) * conv_grad_float, axis=(0, 1))
        )
    glu_grad = glu_grad.reshape(cells, narrow)
    value_grad = (glu_grad * sig_gate).astype(BF16)
    gate_grad = (glu_grad * value * sig_gate * (1.0 - sig_gate)).astype(BF16)
    value_grad, gate_grad = (
        jnp.concatenate(gather_over(g, "row"), axis=1) for g in (value_grad, gate_grad)
    )

    normed_part = (
        lax.dot_general(value_grad, value_weight, CONTRACT_LAST, preferred_element_type=F32)
        + lax.dot_general(gate_grad, gate_weight, CONTRACT_LAST, preferred_element_type=F32)
    ).astype(BF16)
    normed_part = normed_part.reshape(utts, n_row, frames, per_row, width).transpose(1, 3, 0, 2, 4)
    normed_grad = turn(
        lax.psum_scatter(
            normed_part.reshape(n_col * utts * frames, width),
            "col",
            scatter_dimension=0,
            tiled=True,
        )
    )
    normed_grad = normed_grad.astype(F32).reshape(utts, frames, width)

    mixed_rows = lax.all_gather(turn(mixed), "col", axis=0)
    mixed_rows = (
        mixed_rows.reshape(n_row, per_row, utts, span, narrow)
        .transpose(2, 3, 1, 0, 4)
        .reshape(cells, depth)
    )
    projected = jnp.dot(mixed_rows, mixer_weight, preferred_element_type=F32)
    projected = scatter_over(projected.reshape(utts, span, width), "row", 1, BF16)
    module_out = (own + projected).astype(BF16)

    normed_cells = spread_over(normed, "dp", 1)
    value_weight_grad, gate_weight_grad = (
        lax.dot_general(
            normed_cells, collect_over(g, "dp"), CONTRACT_FIRST, preferred_element_type=F32
        )
        for g in (value_grad, gate_grad)
    )
    mixer_weight_grad = lax.dot_general(
        spread_over(mixed_rows, "dp", 1),
        collect_over(grad_rows, "dp"),
        CONTRACT_FIRST,
        preferred_element_type=F32,
    )
    kernel_parts = lax.all_gather(jnp.stack(kernel_rows), ("row", "dp"), axis=0)
    kernel_parts = kernel_parts.reshape(n_row, -1, taps, narrow)
    kernel_grad = jnp.sum(kernel_parts, 1).transpose(1, 0, 2).reshape(taps, width)

    standardized = (own - mean_own) * inverse_own
    gain_own = lax.dynamic_slice_in_dim(layer_norm_gain, col * width, width, 0)
    scaled = normed_grad * gain_own
    sums = lax.psum(jnp.stack([jnp.sum(scaled, -1), jnp.sum(scaled * standardized, -1)]), "col")
    input_gradient = (
        output_gradient.astype(F32)
        + (scaled - sums[0][..., None] / model - standardized * (sums[1][..., None] / model))
        * inverse_own
    ).astype(BF16)
    norm_gain_gradient = lax.psum(jnp.sum(normed_grad * standardized, axis=(0, 1)), ("row", "dp"))
    return (
        module_out,
        input_gradient,
        value_weight_grad,
        gate_weight_grad,
        mixer_weight_grad,
        kernel_grad,
        norm_gain_gradient,
    )


GATE_DTYPE = F32


def solution(mesh):
    placed = (
        P(("groups", "dp"), "row", "col"),
        P(("groups", "dp"), "row", "col"),
        P("row", "col"),
        P("row", "col"),
        P("row", "col"),
        P(None, "col"),
        P(),
    )
    return jax.shard_map(
        shards,
        mesh=mesh,
        in_specs=placed,
        out_specs=(
            P(("groups", "dp"), "row", "col"),
            P(("groups", "dp"), "row", "col"),
            P(("groups", "row", "dp"), "col"),
            P(("groups", "row", "dp"), "col"),
            P(("groups", "row", "dp"), "col"),
            P("groups", "col"),
            P(("groups", "col")),
        ),
        check_vma=False,
    )
```

profile of v0, /device:TPU:0, one launch (start us, length us, event | category | flops | bytes accessed | tf_op | source)
XLA Modules:
  0.0 470.7 jit_solution(16571329316580543862)
XLA Ops:
  10.0 41.2 %collective-permute-start.5 = (bf16[1,256,1536]{2,1,0:T(8,128)(2,1)}, bf16[1,256,1536]{2,1,0:T(8,128)(2,1)S(1)}, u32[]{:S(2)}, u32[]{:S(2)}) collective-permute-start(bf16[1,256,1536]{2,1,0:T(8,128)(2,1)} %param.8), channel_id=1, source_target_pairs={{0,8},{8,0},{1,9},{9,1},{2,10},{10,2},{3,11},{11,3},{4,12},{12,4},... | collective-permute-start | bytes 2359304 | tf_op jit(solution)/shard_map/ppermute | solution.py:19
  51.2 16.9 %collective-permute-done.5 = bf16[1,256,1536]{2,1,0:T(8,128)(2,1)S(1)} collective-permute-done((bf16[1,256,1536]{2,1,0:T(8,128)(2,1)}, bf16[1,256,1536]{2,1,0:T(8,128)(2,1)S(1)}, u32[]{:S(2)}, u32[]{:S(2)}) %collective-permute-start.5) | collective-permute-done | bytes 786464 | tf_op jit(solution)/shard_map/ppermute | solution.py:19
  70.7 10.3 %convolution_convert_fusion = bf16[512,3072]{1,0:T(8,128)(2,1)} fusion(bf16[512,1536]{1,0:T(8,128)(2,1)S(1)} %bitcast.137, bf16[3072,1536]{1,0:T(8,128)(2,1)} %param.11), kind=kOutput, calls=%fused_computation.37 | convolution fusion | flops 4833411072 | bytes 14155776 | tf_op jit(solution)/shard_map/dot_general | solution.py:109
  81.0 7.1 %reshape.322 = bf16[512,2,2,768]{3,2,1,0:T(2,128)(2,1)S(1)} reshape(bf16[512,3072]{1,0:T(8,128)(2,1)} %convolution_convert_fusion) | data formatting | bytes 6291456 | tf_op jit(solution)/shard_map/reshape | solution.py:112
  91.8 27.4 %all-gather.1 = f32[16,1,256]{2,1,0:T(1,128)S(1)} all-gather(f32[2,1,256]{2,1,0:T(1,128)S(1)} %pad_maximum_fusion.6), channel_id=3, replica_groups=mesh['groups'=2,'row'=2,'col'=4,'dp'=2] {'row','col'}, dimensions={0}, use_global_device_ids=true | all-gather | bytes 18432 | tf_op jit(solution)/shard_map/all_gather | solution.py:84
  119.4 3.2 convert.6
  122.6 6.1 %fusion.2 = bf16[2,2,1,256,1536]{4,1,3,0,2:T(2,128)(2,1)S(1)} fusion(f32[2,2,1,256,1536]{4,3,1,0,2:T(8,128)S(1)} %convert.6, f32[2,1536]{1,0:T(2,128)S(1)} %mul.735, f32[2,256]{1,0:T(2,128)S(1)} %add_rsqrt_fusion, f32[2,256]{1,0:T(2,128)S(1)} %broadcast_multiply_fusion), kind=kLoop, calls=%fused_computation.36 | loop fusion | flops 6291456 | bytes 9453568 | tf_op jit(solution)/shard_map/convert.2
  129.6 5.0 %fusion.136 = f32[512,1536]{1,0:T(8,128)S(1)} fusion(bf16[512,3072]{1,0:T(8,128)(2,1)S(1)} %bitcast.129, bf16[3072,1536]{1,0:T(8,128)(2,1)S(1)} %bitcast.157), kind=kOutput, calls=%fused_computation.281 | convolution fusion | flops 4831838208 | bytes 15728640 | tf_op jit(solution)/shard_map/dot_general | solution.py:103
  138.5 5.0 %fusion.135 = f32[512,1536]{1,0:T(8,128)S(1)} fusion(bf16[512,3072]{1,0:T(8,128)(2,1)S(1)} %bitcast.130, bf16[3072,1536]{1,0:T(8,128)(2,1)S(1)} %bitcast.159), kind=kOutput, calls=%fused_computation.280 | convolution fusion | flops 4831838208 | bytes 15728640 | tf_op jit(solution)/shard_map/dot_general | solution.py:105
  145.7 29.8 %reduce-scatter.3.cloned.1.call-done = bf16[512,768]{1,0:T(8,128)(2,1)} async-done(((bf16[2048,768]{1,0:T(8,128)(2,1)}), bf16[512,768]{1,0:T(8,128)(2,1)}) %reduce-scatter.3.cloned.1.call-update) | async-done | bytes 786448 | tf_op jit(solution)/shard_map/reduce_scatter | solution.py:114
  175.5 7.4 %collective-permute-start.6 = (bf16[512,768]{1,0:T(8,128)(2,1)}, bf16[512,768]{1,0:T(8,128)(2,1)}, u32[]{:S(2)}, u32[]{:S(2)}) collective-permute-start(bf16[512,768]{1,0:T(8,128)(2,1)} %reduce-scatter.3.cloned.1.call-done), channel_id=1, source_target_pairs={{0,0},{2,2},{4,8},{6,10},{8,4},{10,6},{12,12},{14,14},{1,1},{3,3},... | collective-permute-start | bytes 2359304 | tf_op jit(solution)/shard_map/ppermute | solution.py:79
  185.9 2.6 multiply_convert_fusion.1
  188.6 10.0 %fusion.114 = (f32[768]{0:T(1024)S(1)}, f32[768]{0:T(1024)S(1)}, f32[768]{0:T(1024)S(1)}, f32[768]{0:T(1024)S(1)}, f32[768]{0:T(1024)S(1)}, /*index=5*/f32[768]{...) fusion(bf16[1,512,768]{2,1,0:T(8,128)(2,1)S(1)} %bitcast.123, ...), kind=kLoop, calls=%fused_computation.188 | loop fusion | flops 51111168 | bytes 4841472 | tf_op jit(solution)/shard_map/reduce_sum | solution.py:139
  201.1 8.5 %fusion.118 = (bf16[512,768]{1,0:T(8,128)(2,1)}, f32[1,512,768]{2,1,0:T(8,128)S(1)}) fusion(f32[512,768]{1,0:T(8,128)S(1)} %collective-permute-done.2, f32[512,1536]{1,0:T(8,128)} %copy-done.3, s32[]{:T(128)S(6)} %select_n.103, f32[768]{0:T(1024)S(1)} %get-tuple-element.70, f32[768]{0:T(1024)S(1)} %get-tuple-element.41, f32[768]{0:T(1024)S(1)} %get-tuple-element.42, ...), kind=kLoop, calls=%fused_computation.198 | loop fusion | flops 38535168 | bytes 6386692 | tf_op jit(solution)/shard_map/convert_element_type | solution.py:142
  209.6 2.7 fusion.121
  212.3 65.0 %collective-permute-start.8 = (bf16[512,768]{1,0:T(8,128)(2,1)}, bf16[512,768]{1,0:T(8,128)(2,1)}, u32[]{:S(2)}, u32[]{:S(2)}) collective-permute-start(bf16[512,768]{1,0:T(8,128)(2,1)} %fusion.121), channel_id=1, source_target_pairs={{0,8},{8,0},{1,9},{9,1},{2,10},{10,2},{3,11},{11,3},{4,12},{12,4},... | collective-permute-start | bytes 2359304 | tf_op jit(solution)/shard_map/ppermute | solution.py:19
  277.5 18.5 %collective-permute-done.8 = bf16[512,768]{1,0:T(8,128)(2,1)} collective-permute-done((bf16[512,768]{1,0:T(8,128)(2,1)}, bf16[512,768]{1,0:T(8,128)(2,1)}, u32[]{:S(2)}, u32[]{:S(2)}) %collective-permute-start.8) | collective-permute-done | bytes 786464 | tf_op jit(solution)/shard_map/ppermute | solution.py:19
  297.4 14.8 %collective-permute-done.7 = bf16[512,768]{1,0:T(8,128)(2,1)} collective-permute-done((bf16[512,768]{1,0:T(8,128)(2,1)}, bf16[512,768]{1,0:T(8,128)(2,1)}, u32[]{:S(2)}, u32[]{:S(2)}) %collective-permute-start.7) | collective-permute-done | bytes 786464 | tf_op jit(solution)/shard_map/ppermute | solution.py:19
  313.9 8.3 %fusion.131 = f32[512,3072]{1,0:T(8,128)S(1)} fusion(bf16[3072,1536]{1,0:T(8,128)(2,1)} %param.10, bf16[512,768]{1,0:T(8,128)(2,1)S(1)} %get-tuple-element.82, bf16[512,768]{1,0:T(8,128)(2,1)S(1)} %get-tuple-element.81), kind=kOutput, calls=%fused_computation.279 | convolution fusion | flops 4834983936 | bytes 17301504 | tf_op jit(solution)/shard_map/dot_general | solution.py:150
  322.2 6.4 %add_convert_fusion = bf16[512,3072]{1,0:T(8,128)(2,1)} fusion(f32[512,3072]{1,0:T(8,128)S(1)} %fusion.131, bf16[3072,1536]{1,0:T(8,128)(2,1)S(1)} %bitcast.161, bf16[512,768]{1,0:T(8,128)(2,1)S(1)} %get-tuple-element.80, bf16[512,768]{1,0:T(8,128)(2,1)S(1)} %get-tuple-element.79), kind=kOutput, calls=%fused_computation.35 | convolution fusion | flops 4838129664 | bytes 20447232 | tf_op jit(solution)/shard_map/dot_general | solution.py:149
  328.7 8.3 %reshape.327 = bf16[1,2,256,2,1536]{4,3,2,1,0:T(2,128)(2,1)} reshape(bf16[512,3072]{1,0:T(8,128)(2,1)} %add_convert_fusion) | data formatting | bytes 6291456 | tf_op jit(solution)/shard_map/reshape | solution.py:152
  337.0 4.1 copy.40
  341.1 3.9 constant_dynamic-slice_fusion.4
  353.6 6.8 %all-gather.4 = f32[4,31,768]{2,1,0:T(8,128)S(1)} all-gather(f32[1,31,768]{2,1,0:T(8,128)S(1)} %bitcast.142), channel_id=5, replica_groups=mesh['groups'=2,'row'=2,'col'=4,'dp'=2] {'row','dp'}, dimensions={0}, use_global_device_ids=true | all-gather | bytes 476160 | tf_op jit(solution)/shard_map/all_gather | solution.py:186
  361.5 13.1 %fusion.3 = f32[1536,1536]{1,0:T(8,128)} fusion(bf16[512,1536]{1,0:T(8,128)(2,1)} %collective-permute-done.11, bf16[512,768]{1,0:T(8,128)(2,1)S(1)} %copy-done.12, bf16[512,768]{1,0:T(8,128)(2,1)S(1)} %copy-done.9, bf16[512,1536]{1,0:T(8,128)(2,1)} %collective-permute-done.10, bf16[512,1536]{1,0:T(8,128)(2,1)} %get-tuple-element.77), kind=kOutput, calls=%fused_computation.39 | convolution fusion | flops 4847566848 | bytes 15728640 | tf_op jit(solution)/shard_map/dot_general | solution.py:175
  374.6 12.3 %fusion.9 = f32[1536,1536]{1,0:T(8,128)} fusion(bf16[512,1536]{1,0:T(8,128)(2,1)} %collective-permute-done.12, bf16[512,768]{1,0:T(8,128)(2,1)S(1)} %get-tuple-element.82, bf16[512,768]{1,0:T(8,128)(2,1)S(1)} %get-tuple-element.81, bf16[512,1536]{1,0:T(8,128)(2,1)} %collective-permute-done.10, bf16[512,1536]{1,0:T(8,128)(2,1)S(1)} %copy-done.18), kind=kOutput, calls=%fused_computation.45 | convolution fusion | flops 4847566848 | bytes 15728640 | tf_op jit(solution)/shard_map/dot_general | solution.py:175
  386.9 3.2 copy.38
  392.3 7.7 %fusion.137 = f32[512,1536]{1,0:T(8,128)S(1)} fusion(bf16[512,3072]{0,1:T(8,128)(2,1)S(1)} %bitcast.133, bf16[3072,1536]{1,0:T(8,128)(2,1)} %param.11), kind=kOutput, calls=%fused_computation.282 | convolution fusion | flops 4831838208 | bytes 15728640 | tf_op jit(solution)/shard_map/dot_general | solution.py:169
  406.1 9.8 %fusion.15 = f32[1536,1536]{1,0:T(8,128)} fusion(bf16[512,1536]{0,1:T(8,128)(2,1)} %collective-permute-done.13, bf16[512,1536]{0,1:T(8,128)(2,1)} %get-tuple-element.75, bf16[512,1536]{1,0:T(8,128)(2,1)} %collective-permute-done.14, bf16[512,1536]{1,0:T(8,128)(2,1)S(1)} %bitcast.139), kind=kOutput, calls=%fused_computation.51 | convolution fusion | flops 4844421120 | bytes 15728640 | tf_op jit(solution)/shard_map/dot_general | solution.py:180
  416.8 37.0 %psum.14 = f32[2,1,256]{2,1,0:T(1,128)S(1)} all-reduce(f32[2,1,256]{2,1,0:T(1,128)S(1)} %pad_maximum_fusion.7), channel_id=1, replica_groups=mesh['groups'=2,'row'=2,'col'=4,'dp'=2] {'col'}, use_global_device_ids=true, to_apply=%region_8.9 | all-reduce | flops 512 | bytes 4096 | tf_op jit(solution)/shard_map/psum | solution.py:193
  453.9 6.4 %psum.15 = f32[1536]{0:T(1024)} all-reduce(f32[1536]{0:T(1024)S(1)} %get-tuple-element.7), channel_id=1, replica_groups=mesh['groups'=2,'row'=2,'col'=4,'dp'=2] {'row','dp'}, use_global_device_ids=true, to_apply=%region_42.43 | all-reduce | flops 1536 | bytes 12288 | tf_op jit(solution)/shard_map/psum | solution.py:199
  460.3 3.7 fusion.62
  (168 shorter events, 43.2 us)
Async XLA Ops:
  7.2 112.2 %all-gather.8.cloned.1.call-start = ((), (), s32[]{:S(2)}) async-start(), calls=%async_computation.4 | async-start | bytes 3932160 | tf_op jit(solution)/shard_map/all_gather | solution.py:95
  7.2 1.8 collective-permute-start
  9.9 165.6 %reduce-scatter.3.cloned.1.call-start = ((), (), s32[]{:S(2)}) async-start(), calls=%async_computation.2 | async-start | bytes 3932160 | tf_op jit(solution)/shard_map/reduce_scatter | solution.py:114
  10.0 58.1 %collective-permute-start.5 = (bf16[1,256,1536]{2,1,0:T(8,128)(2,1)}, bf16[1,256,1536]{2,1,0:T(8,128)(2,1)S(1)}, u32[]{:S(2)}, u32[]{:S(2)}) collective-permute-start(bf16[1,256,1536]{2,1,0:T(8,128)(2,1)} %param.8), channel_id=1, source_target_pairs={{0,8},{8,0},{1,9},{9,1},{2,10},{10,2},{3,11},{11,3},{4,12},{12,4},... | collective-permute-start | bytes 2359304 | tf_op jit(solution)/shard_map/ppermute | solution.py:19
  90.2 296.8 %all-gather.10.cloned.1.call-start = ((), (), s32[]{:S(2)}) async-start(), calls=%async_computation.5 | async-start | bytes 3932160 | tf_op jit(solution)/shard_map/all_gather | solution.py:163
  119.4 10.1 %slice-start = ((s8[9437184]{0:T(1024)(128)(4,1)}), s8[4194304]{0:T(1024)(128)(4,1)S(1)}, s32[]{:S(2)}) async-start(s8[9437184]{0:T(1024)(128)(4,1)} %bitcast.156), calls=%async_computation.6 | async-start | bytes 8388608
  119.4 10.1 %slice-start.1 = ((s8[9437184]{0:T(1024)(128)(4,1)}), s8[4194304]{0:T(1024)(128)(4,1)S(1)}, s32[]{:S(2)}) async-start(s8[9437184]{0:T(1024)(128)(4,1)} %bitcast.156), calls=%async_computation.7 | async-start | bytes 8388608
  128.7 9.8 %slice-start.3 = ((s8[9437184]{0:T(1024)(128)(4,1)}), s8[4194304]{0:T(1024)(128)(4,1)S(1)}, s32[]{:S(2)}) async-start(s8[9437184]{0:T(1024)(128)(4,1)} %bitcast.158), calls=%async_computation.9 | async-start | bytes 8388608
  129.5 9.0 %copy-start = (bf16[64,8,2,1536]{3,1,2,0:T(8,128)(2,1)}, bf16[64,8,2,1536]{3,1,2,0:T(8,128)(2,1)S(1)}, u32[]{:S(2)}) copy-start(bf16[64,8,2,1536]{3,1,2,0:T(8,128)(2,1)S(1)} %copy.43) | copy-start | bytes 9437188
  129.5 9.0 %slice-start.4 = ((s8[9437184]{0:T(1024)(128)(4,1)}), s8[4194304]{0:T(1024)(128)(4,1)S(1)}, s32[]{:S(2)}) async-start(s8[9437184]{0:T(1024)(128)(4,1)} %bitcast.158), calls=%async_computation.10 | async-start | bytes 8388608
  129.6 9.0 %slice-start.5 = ((s8[9437184]{0:T(1024)(128)(4,1)}), s8[1048576]{0:T(1024)(128)(4,1)S(1)}, s32[]{:S(2)}) async-start(s8[9437184]{0:T(1024)(128)(4,1)} %bitcast.158), calls=%async_computation.11 | async-start | bytes 2097152
  136.8 49.1 %collective-permute-start.2 = (f32[512,768]{1,0:T(8,128)}, f32[512,768]{1,0:T(8,128)S(1)}, u32[]{:S(2)}, u32[]{:S(2)}) collective-permute-start(f32[512,768]{1,0:T(8,128)} %constant_dynamic-slice_fusion.7), channel_id=1, source_target_pairs={{0,8},{8,0},{1,9},{9,1},{2,10},{10,2},{3,11},{11,3},{4,12},{12,4},... | collective-permute-start | bytes 4718600 | tf_op jit(solution)/shard_map/ppermute | solution.py:36
  145.3 40.6 %collective-permute-start.1 = (bf16[512,768]{1,0:T(8,128)(2,1)S(1)}, bf16[512,768]{1,0:T(8,128)(2,1)S(1)}, u32[]{:S(2)}, u32[]{:S(2)}) collective-permute-start(bf16[512,768]{1,0:T(8,128)(2,1)S(1)} %dynamic-slice_convert_fusion.1), channel_id=1, source_target_pairs={{0,8},{8,0},{1,9},{9,1},{2,10},{10,2},{3,11},{11,3},{4,12},{12,4},... | collective-permute-start | bytes 2359304 | tf_op jit(solution)/shard_map/ppermute | solution.py:36
  175.5 13.1 %collective-permute-start.6 = (bf16[512,768]{1,0:T(8,128)(2,1)}, bf16[512,768]{1,0:T(8,128)(2,1)}, u32[]{:S(2)}, u32[]{:S(2)}) collective-permute-start(bf16[512,768]{1,0:T(8,128)(2,1)} %reduce-scatter.3.cloned.1.call-done), channel_id=1, source_target_pairs={{0,0},{2,2},{4,8},{6,10},{8,4},{10,6},{12,12},{14,14},{1,1},{3,3},... | collective-permute-start | bytes 2359304 | tf_op jit(solution)/shard_map/ppermute | solution.py:79
  199.0 1.6 collective-permute-start.3
  200.6 203.7 %reduce-scatter.5.cloned.1.call-start = ((), (), s32[]{:S(2)}) async-start(), calls=%async_computation.3 | async-start | bytes 3932160 | tf_op jit(solution)/shard_map/reduce_scatter | solution.py:154
  201.0 8.6 %copy-start.4 = (f32[512,1536]{1,0:T(8,128)S(1)}, f32[512,1536]{1,0:T(8,128)}, u32[]{:S(2)}) copy-start(f32[512,1536]{1,0:T(8,128)} %copy-done.3) | copy-start | bytes 9437188
  201.1 8.6 %copy-start.6 = (f32[512,1536]{1,0:T(8,128)S(1)}, f32[512,1536]{1,0:T(8,128)}, u32[]{:S(2)}) copy-start(f32[512,1536]{1,0:T(8,128)} %copy-done.5) | copy-start | bytes 9437188
  212.3 83.6 %collective-permute-start.8 = (bf16[512,768]{1,0:T(8,128)(2,1)}, bf16[512,768]{1,0:T(8,128)(2,1)}, u32[]{:S(2)}, u32[]{:S(2)}) collective-permute-start(bf16[512,768]{1,0:T(8,128)(2,1)} %fusion.121), channel_id=1, source_target_pairs={{0,8},{8,0},{1,9},{9,1},{2,10},{10,2},{3,11},{11,3},{4,12},{12,4},... | collective-permute-start | bytes 2359304 | tf_op jit(solution)/shard_map/ppermute | solution.py:19
  277.3 34.9 %collective-permute-start.7 = (bf16[512,768]{1,0:T(8,128)(2,1)}, bf16[512,768]{1,0:T(8,128)(2,1)}, u32[]{:S(2)}, u32[]{:S(2)}) collective-permute-start(bf16[512,768]{1,0:T(8,128)(2,1)} %get-tuple-element.73), channel_id=1, source_target_pairs={{0,8},{8,0},{1,9},{9,1},{2,10},{10,2},{3,11},{11,3},{4,12},{12,4},... | collective-permute-start | bytes 2359304 | tf_op jit(solution)/shard_map/ppermute | solution.py:19
  277.4 128.7 %collective-permute-start.14 = (bf16[512,1536]{1,0:T(8,128)(2,1)}, bf16[512,1536]{1,0:T(8,128)(2,1)}, u32[]{:S(2)}, u32[]{:S(2)}) collective-permute-start(bf16[512,1536]{1,0:T(8,128)(2,1)} %bitcast.138), channel_id=1, source_target_pairs={{0,1},{1,0},{2,3},{3,2},{4,5},{5,4},{6,7},{7,6},{8,9},{9,8},{10,11... | collective-permute-start | bytes 4718600 | tf_op jit(solution)/shard_map/ppermute | solution.py:53
  312.2 10.0 %slice-start.6 = ((s8[9437184]{0:T(1024)(128)(4,1)}), s8[4194304]{0:T(1024)(128)(4,1)S(1)}, s32[]{:S(2)}) async-start(s8[9437184]{0:T(1024)(128)(4,1)} %bitcast.160), calls=%async_computation.12 | async-start | bytes 8388608
  313.9 8.3 %slice-start.7 = ((s8[9437184]{0:T(1024)(128)(4,1)}), s8[4194304]{0:T(1024)(128)(4,1)S(1)}, s32[]{:S(2)}) async-start(s8[9437184]{0:T(1024)(128)(4,1)} %bitcast.160), calls=%async_computation.13 | async-start | bytes 8388608
  344.9 16.5 %collective-permute-start.10 = (bf16[512,1536]{1,0:T(8,128)(2,1)}, bf16[512,1536]{1,0:T(8,128)(2,1)}, u32[]{:S(2)}, u32[]{:S(2)}) collective-permute-start(bf16[512,1536]{1,0:T(8,128)(2,1)} %get-tuple-element.78), channel_id=1, source_target_pairs={{0,1},{1,0},{2,3},{3,2},{4,5},{5,4},{6,7},{7,6},{8,9},{9,8},{10,11... | collective-permute-start | bytes 4718600 | tf_op jit(solution)/shard_map/ppermute | solution.py:46
  346.2 15.2 %collective-permute-start.11 = (bf16[512,1536]{1,0:T(8,128)(2,1)}, bf16[512,1536]{1,0:T(8,128)(2,1)}, u32[]{:S(2)}, u32[]{:S(2)}) collective-permute-start(bf16[512,1536]{1,0:T(8,128)(2,1)} %pad_maximum_fusion.4), channel_id=1, source_target_pairs={{0,1},{1,0},{2,3},{3,2},{4,5},{5,4},{6,7},{7,6},{8,9},{9,8},{10,11... | collective-permute-start | bytes 4718600 | tf_op jit(solution)/shard_map/ppermute | solution.py:53
  352.3 22.3 %collective-permute-start.12 = (bf16[512,1536]{1,0:T(8,128)(2,1)}, bf16[512,1536]{1,0:T(8,128)(2,1)}, u32[]{:S(2)}, u32[]{:S(2)}) collective-permute-start(bf16[512,1536]{1,0:T(8,128)(2,1)} %pad_maximum_fusion.5), channel_id=1, source_target_pairs={{0,1},{1,0},{2,3},{3,2},{4,5},{5,4},{6,7},{7,6},{8,9},{9,8},{10,11... | collective-permute-start | bytes 4718600 | tf_op jit(solution)/shard_map/ppermute | solution.py:53
  361.4 13.1 %copy-start.18 = (bf16[512,1536]{1,0:T(8,128)(2,1)S(1)}, bf16[512,1536]{1,0:T(8,128)(2,1)}, u32[]{:S(2)}) copy-start(bf16[512,1536]{1,0:T(8,128)(2,1)} %get-tuple-element.77) | copy-start | bytes 4718596
  392.0 14.1 %collective-permute-start.13 = (bf16[512,1536]{0,1:T(8,128)(2,1)}, bf16[512,1536]{0,1:T(8,128)(2,1)}, u32[]{:S(2)}, u32[]{:S(2)}) collective-permute-start(bf16[512,1536]{0,1:T(8,128)(2,1)} %get-tuple-element.76), channel_id=1, source_target_pairs={{0,1},{1,0},{2,3},{3,2},{4,5},{5,4},{6,7},{7,6},{8,9},{9,8},{10,11... | collective-permute-start | bytes 4718600 | tf_op jit(solution)/shard_map/ppermute | solution.py:46
  402.7 57.6 %collective-permute-start.4 = (bf16[1,256,1536]{2,1,0:T(8,128)(2,1)}, bf16[1,256,1536]{2,1,0:T(8,128)(2,1)}, u32[]{:S(2)}, u32[]{:S(2)}) collective-permute-start(bf16[1,256,1536]{2,1,0:T(8,128)(2,1)} %fusion.122), channel_id=1, source_target_pairs={{0,8},{8,0},{1,9},{9,1},{2,10},{10,2},{3,11},{11,3},{4,12},{12,4},... | collective-permute-start | bytes 2359304 | tf_op jit(solution)/shard_map/ppermute | solution.py:36
  404.3 11.6 %collective-permute-start.9 = (bf16[256,1536]{1,0:T(8,128)(2,1)}, bf16[256,1536]{1,0:T(8,128)(2,1)S(1)}, u32[]{:S(2)}, u32[]{:S(2)}) collective-permute-start(bf16[256,1536]{1,0:T(8,128)(2,1)} %reduce-scatter.5.cloned.1.call-done), channel_id=1, source_target_pairs={{0,0},{2,2},{4,8},{6,10},{8,4},{10,6},{12,12},{14,14},{1,1},{3,3},... | collective-permute-start | bytes 2359304 | tf_op jit(solution)/shard_map/ppermute | solution.py:79
  406.1 10.1 %copy-start.2 = (bf16[1,256,1536]{2,1,0:T(8,128)(2,1)S(1)}, bf16[1,256,1536]{2,1,0:T(8,128)(2,1)}, u32[]{:S(2)}) copy-start(bf16[1,256,1536]{2,1,0:T(8,128)(2,1)} %param.7) | copy-start | bytes 2359300
  415.9 44.4 %copy-start.13 = (bf16[1,256,1536]{2,1,0:T(8,128)(2,1)S(1)}, bf16[1,256,1536]{2,1,0:T(8,128)(2,1)}, u32[]{:S(2)}) copy-start(bf16[1,256,1536]{2,1,0:T(8,128)(2,1)} %param.8) | copy-start | bytes 2359300
  (17 other events, 72.7 us)
Sparse Core Ops, SparseCore 0:
  10.1 103.4 all-gather.7
  116.5 58.8 reduce-scatter.2
  200.7 126.0 all-gather.9
  341.2 59.5 reduce-scatter.4
where the time goes:
time: 477 us; the launch traced here: 471 us
  starting transfers between devices  124 us (26%)
  waiting for transfers between devices  80.1 us (17%)
  matrix products  78.1 us (16%)
  blocking collectives  77.7 us (16%)
  other arithmetic  50.8 us (11%)
  local copies, waits for them, and re-layouts  45.2 us (9%)
  between operations  14.8 us (3%)
    ppermute x3, starting transfers between devices, gather_over(): lax.ppermute(x, axis, ring(count, s))  106 us
    ppermute x3, waiting for transfers between devices, gather_over(): lax.ppermute(x, axis, ring(count, s))  50.2 us
    psum x1, blocking collectives, shards(): lax.psum(jnp.stack([jnp.sum(scaled, -1), jnp.sum(scaled * standardized, -...  37 us
    reduce_scatter x1, waiting for transfers between devices, shards(): lax.psum_scatter(mixed_part.reshape(n_col * cells, narrow), 'col', scatte...  29.8 us
    all_gather x1, blocking collectives, shards(): lax.all_gather(jnp.stack([block_mean, block_square]), ('row', 'col'), axi...  27.4 us
    dot_general x2, matrix products, shards(): lax.dot_general(normed_cells, collect_over(g, 'dp'), CONTRACT_FIRST, pref...  25.4 us
    reduce_sum x4, other arithmetic, shards(): jnp.sum(glu_pad[:, tap:tap + span].astype(F32) * conv_grad_float, axis=(0...  15 us
    ppermute x4, starting transfers between devices, turn(): return lax.ppermute(x, ('row', 'col'), turned)  12.5 us
  transfers between devices with their start and end apart: 19, of which 4 were waited for; matrix products, arithmetic and copies ran while one was open for 32% of the time, Pallas kernels for 0%

commit v1 on v0

v1 whole, which is shorter than its diff:
```python
import functools

import jax
import jax.numpy as jnp
from jax import lax
from jax.experimental import pallas as pl
from jax.experimental.pallas import tpu as pltpu
from jax.sharding import PartitionSpec as P

EPS = 1e-05
CONTRACT_LAST = (((1,), (1,)), ((), ()))
CONTRACT_FIRST = (((0,), (0,)), ((), ()))
BF16 = jnp.bfloat16
F32 = jnp.float32
PARTS = 1
CONV_ROWS = 64


def ring(count, shift):
    return [(i, (i + shift) % count) for i in range(count)]


def by_source(pieces, axis):
    count, me = lax.axis_size(axis), lax.axis_index(axis)
    ordered = []
    for j in range(count):
        back = (me - j) % count
        block = pieces[0]
        for s in range(1, count):
            block = jnp.where(back == s, pieces[s], block)
        ordered.append(block)
    return ordered


def exchange(pick, axis):
    count, me = lax.axis_size(axis), lax.axis_index(axis)
    return [pick(me)] + [
        lax.ppermute(pick((me + s) % count), axis, ring(count, s)) for s in range(1, count)
    ]


def send_sum(pick, axis, dtype):
    count, me = lax.axis_size(axis), lax.axis_index(axis)
    sent = [
        lax.ppermute(pick((me + s) % count).astype(dtype), axis, ring(count, s))
        for s in range(1, count)
    ]
    total = pick(me)
    for piece in sent:
        total = total + piece.astype(F32)
    return total


def sum_over(x, axis):
    pieces = exchange(lambda i: x, axis)
    return sum(pieces[1:], pieces[0])


def conv_body(taps, span, value_ref, value_in_ref, gate_ref, gate_in_ref, grad_ref, kernel_ref,
              mixed_ref, value_grad_ref, gate_grad_ref, taps_ref, glu_pad, grad_pad, partial):
    half = taps // 2
    lead = 16
    lanes = glu_pad.shape[1]
    chunk = CONV_ROWS
    zeros = jnp.zeros((lead, lanes), F32)
    for pad in (glu_pad, grad_pad):
        pad[pl.ds(0, lead)] = zeros
        pad[pl.ds(lead + span, lead)] = zeros
    partial[...] = jnp.zeros_like(partial)

    def rows(i):
        return pl.ds(pl.multiple_of(i * chunk, chunk), chunk)

    def padded(i, shift):
        return pl.ds(i * chunk + (lead + shift), chunk)

    @pl.loop(0, span // chunk)
    def _(i):
        gate = gate_ref[rows(i)] + gate_in_ref[rows(i)]
        value = value_ref[rows(i)] + value_in_ref[rows(i)].astype(F32)
        glu_pad[pl.ds(pl.multiple_of(i * chunk + lead, 8), chunk)] = (
            (value * jax.nn.sigmoid(gate)).astype(BF16).astype(F32)
        )

    @pl.loop(0, span // chunk)
    def _(i):
        conv = jnp.zeros((chunk, lanes), F32)
        for tap in range(taps):
            conv = conv + kernel_ref[pl.ds(tap, 1)] * glu_pad[padded(i, tap - half)]
        sig = jax.nn.sigmoid(conv)
        mixed_ref[rows(i)] = (conv * sig).astype(BF16)
        slope = sig * (1.0 + conv * (1.0 - sig))
        grad = (grad_ref[rows(i)].astype(F32) * slope).astype(BF16).astype(F32)
        grad_pad[pl.ds(pl.multiple_of(i * chunk + lead, 8), chunk)] = grad

    @pl.loop(0, span // chunk)
    def _(i):
        grad = grad_pad[pl.ds(pl.multiple_of(i * chunk + lead, 8), chunk)]
        total = jnp.zeros((chunk, lanes), F32)
        for tap in range(taps):
            total = total + kernel_ref[pl.ds(tap, 1)] * grad_pad[padded(i, half - tap)]
            product = glu_pad[padded(i, tap - half)] * grad
            partial[pl.ds(8 * tap, 8)] += sum(
                product[8 * j : 8 * j + 8] for j in range(chunk // 8)
            )
        gate = gate_ref[rows(i)] + gate_in_ref[rows(i)]
        value = value_ref[rows(i)] + value_in_ref[rows(i)].astype(F32)
        sig = jax.nn.sigmoid(gate)
        value_grad_ref[rows(i)] = (total * sig).astype(BF16)
        gate_grad_ref[rows(i)] = (total * value * sig * (1.0 - sig)).astype(BF16)

    for tap in range(taps):
        taps_ref[pl.ds(tap, 1)] = jnp.sum(partial[pl.ds(8 * tap, 8)], 0, keepdims=True)


def conv_block(value, value_in, gate, gate_in, mixed_grad, kernel, utts):
    cells, narrow = value.shape
    span, taps = cells // utts, kernel.shape[0]
    lanes = 128 if narrow % 128 == 0 else narrow
    tall = pl.BlockSpec((span, lanes), lambda u, j: (u, j))
    short = pl.BlockSpec((taps, lanes), lambda u, j: (0, j))
    work = cells * narrow
    mixed, value_grad, gate_grad, kernel_rows = pl.pallas_call(
        functools.partial(conv_body, taps, span),
        grid=(utts, narrow // lanes),
        in_specs=[tall] * 5 + [short],
        out_specs=[tall] * 3 + [pl.BlockSpec((None, taps, lanes), lambda u, j: (u, 0, j))],
        out_shape=[jax.ShapeDtypeStruct((cells, narrow), BF16)] * 3
        + [jax.ShapeDtypeStruct((utts, taps, narrow), F32)],
        scratch_shapes=[
            pltpu.VMEM((span + 32, lanes), F32),
            pltpu.VMEM((span + 32, lanes), F32),
            pltpu.VMEM((8 * taps, lanes), F32),
        ],
        compiler_params=pltpu.CompilerParams(vmem_limit_bytes=24 << 20),
        cost_estimate=pl.CostEstimate(
            flops=6 * taps * work, bytes_accessed=20 * work, transcendentals=3 * work
        ),
        name="conv_block",
    )(value, value_in, gate, gate_in, mixed_grad, kernel)
    return mixed, value_grad, gate_grad, jnp.sum(kernel_rows, 0)


def shards(
    features, output_gradient, value_weight, gate_weight, mixer_weight, conv_kernel, layer_norm_gain
):
    utts, frames, width = features.shape
    taps = conv_kernel.shape[0]
    half = taps // 2
    model = layer_norm_gain.shape[0]
    n_row, n_col, n_dp = lax.axis_size("row"), lax.axis_size("col"), lax.axis_size("dp")
    row, col, dp = lax.axis_index("row"), lax.axis_index("col"), lax.axis_index("dp")
    per_row = n_col // n_row
    depth = per_row * width
    narrow = width // n_row
    span = n_row * frames
    cells = utts * span
    part = frames // PARTS

    mixer_rows = mixer_weight.reshape(per_row, n_row, narrow, width)
    grad_pieces = exchange(lambda i: output_gradient, "row")
    grad_rows = jnp.stack(by_source(grad_pieces, "row"), axis=1).reshape(cells, width)

    def mixed_part(i):
        rows = lax.dynamic_index_in_dim(mixer_rows, i, 1, keepdims=False)
        return jnp.stack(
            [
                lax.dot_general(
                    grad_rows, rows[p], CONTRACT_LAST, preferred_element_type=F32
                ).astype(BF16)
                for p in range(per_row)
            ]
        )

    mixed_parts = by_source(exchange(mixed_part, "row"), "row")
    mixed_grad = lax.psum_scatter(
        jnp.concatenate(mixed_parts).reshape(n_col * cells, narrow),
        "col",
        scatter_dimension=0,
        tiled=True,
    )

    gain_cols = layer_norm_gain.reshape(n_col, 1, 1, width)
    standard, inverses, crossed = [], [], []
    for i in range(PARTS):
        block = lax.all_gather(features[:, i * part : (i + 1) * part], "col", axis=0).astype(F32)
        mean = jnp.mean(block, (0, 3))[None, :, :, None]
        centered = block - mean
        inverse = lax.rsqrt(jnp.mean(centered * centered, (0, 3)) + EPS)[None, :, :, None]
        xhat = centered * inverse
        standard.append(xhat)
        inverses.append(inverse[0])
        normed_all = (xhat * gain_cols).astype(BF16)

        def channels(j):
            piece = lax.dynamic_slice_in_dim(normed_all, j * per_row, per_row, 0)
            return piece.transpose(1, 2, 0, 3).reshape(utts, part, depth)

        crossed.append(jnp.stack(by_source(exchange(channels, "row"), "row"), axis=1))
    normed = jnp.concatenate(crossed, axis=2).reshape(cells, depth)

    def send_half(x, dtype):
        def columns(i):
            return lax.dynamic_slice_in_dim(x, i * narrow, narrow, 1)

        sent = [
            lax.ppermute(columns((row + s) % n_row).astype(dtype), "row", ring(n_row, s))
            for s in range(1, n_row)
        ]
        return columns(row), sum([p.astype(F32) for p in sent[1:]], sent[0])

    gate_part = jnp.dot(normed, gate_weight, preferred_element_type=F32)
    value_part = jnp.dot(normed, value_weight, preferred_element_type=F32)
    gate, gate_in = send_half(gate_part, F32)
    value, value_in = send_half(value_part, BF16)
    kernel_own = lax.dynamic_slice_in_dim(conv_kernel, row * narrow, narrow, 1)
    mixed, value_grad, gate_grad, kernel_rows = conv_block(
        value, value_in, gate, gate_in, mixed_grad, kernel_own, utts
    )
    mixed = mixed.reshape(utts, span, narrow)
    value_grad, gate_grad = (
        jnp.concatenate(by_source(exchange(lambda i: g, "row"), "row"), axis=1)
        for g in (value_grad, gate_grad)
    )

    value_frames, gate_frames = (
        g.reshape(utts, n_row, PARTS, part, width) for g in (value_grad, gate_grad)
    )
    normed_grads, sums, gain_sums = [], [], []
    for i in range(PARTS):

        def normed_part(j):
            v, g = (
                lax.dynamic_index_in_dim(x[:, :, i], j, 1, keepdims=False).reshape(-1, width)
                for x in (value_frames, gate_frames)
            )
            part_sum = lax.dot_general(
                v, value_weight, CONTRACT_LAST, preferred_element_type=F32
            ) + lax.dot_general(g, gate_weight, CONTRACT_LAST, preferred_element_type=F32)
            part_sum = part_sum.astype(BF16)
            return jnp.stack(
                [part_sum[:, p * width : (p + 1) * width] for p in range(per_row)]
            )

        parts = jnp.concatenate(by_source(exchange(normed_part, "row"), "row"))
        summed = lax.psum_scatter(
            parts.reshape(n_col * utts * part, width), "col", scatter_dimension=0, tiled=True
        )
        normed_grads.append(summed.astype(F32).reshape(utts, part, width))
        wide = parts.astype(F32).reshape(n_col, utts, part, width)
        along = wide * standard[i]
        sums.append(
            jnp.stack([jnp.sum(wide * gain_cols, (0, 3)), jnp.sum(along * gain_cols, (0, 3))])
        )
        gain_sums.append(jnp.sum(along, (1, 2)))
    normed_grad = jnp.concatenate(normed_grads, axis=1)
    sums = sum_over(jnp.concatenate(sums, axis=2), "col")
    gain_sum = sum_over(sum_over(sum(gain_sums), "dp"), "row")
    gain_pieces = exchange(
        lambda j: lax.dynamic_index_in_dim(gain_sum, j, 0, keepdims=False), "col"
    )
    norm_gain_gradient = sum(gain_pieces[1:], gain_pieces[0])

    mixed_gathered = lax.all_gather(mixed, "col", axis=0)
    mixed_pieces = by_source(
        exchange(
            lambda j: lax.dynamic_slice_in_dim(mixed_gathered, j * per_row, per_row, 0), "row"
        ),
        "row",
    )
    mixed_rows = (
        jnp.stack(mixed_pieces, axis=1).transpose(2, 3, 0, 1, 4).reshape(cells, depth)
    )
    projected = jnp.dot(mixed_rows, mixer_weight, preferred_element_type=F32)
    projected = projected.reshape(utts, span, width)
    projected = send_sum(
        lambda j: lax.dynamic_slice_in_dim(projected, j * frames, frames, 1), "row", BF16
    )
    module_out = (features.astype(F32) + projected).astype(BF16)

    share = depth // n_dp

    def spread(x):
        return jnp.concatenate(
            exchange(lambda j: lax.dynamic_slice_in_dim(x, j * share, share, 1), "dp")
        )

    def collect(x):
        return jnp.concatenate(exchange(lambda j: x, "dp"))

    def weight_grad(left, right):
        return lax.dot_general(left, right, CONTRACT_FIRST, preferred_element_type=F32)

    normed_cells = spread(normed)
    value_weight_grad = weight_grad(normed_cells, collect(value_grad))
    gate_weight_grad = weight_grad(normed_cells, collect(gate_grad))
    mixer_weight_grad = weight_grad(spread(mixed_rows), collect(grad_rows))

    kernel_sum = sum_over(kernel_rows, "dp")
    kernel_grad = jnp.concatenate(by_source(exchange(lambda j: kernel_sum, "row"), "row"), axis=1)

    own_standard = jnp.concatenate(
        [lax.dynamic_index_in_dim(x, col, 0, keepdims=False) for x in standard], axis=1
    )
    inverse_own = jnp.concatenate(inverses, axis=1)
    gain_own = lax.dynamic_slice_in_dim(layer_norm_gain, col * width, width, 0)
    scaled = normed_grad * gain_own
    input_gradient = (
        output_gradient.astype(F32)
        + (scaled - sums[0][..., None] / model - own_standard * (sums[1][..., None] / model))
        * inverse_own
    ).astype(BF16)
    return (
        module_out,
        input_gradient,
        value_weight_grad,
        gate_weight_grad,
        mixer_weight_grad,
        kernel_grad,
        norm_gain_gradient,
    )


def solution(mesh):
    placed = (
        P(("groups", "dp"), "row", "col"),
        P(("groups", "dp"), "row", "col"),
        P("row", "col"),
        P("row", "col"),
        P("row", "col"),
        P(None, "col"),
        P(),
    )
    return jax.shard_map(
        shards,
        mesh=mesh,
        in_specs=placed,
        out_specs=(
            P(("groups", "dp"), "row", "col"),
            P(("groups", "dp"), "row", "col"),
            P(("groups", "row", "dp"), "col"),
            P(("groups", "row", "dp"), "col"),
            P(("groups", "row", "dp"), "col"),
            P("groups", "col"),
            P(("groups", "col")),
        ),
        check_vma=False,
    )
```

time: 477 us -> 401 us (0.84)
  waiting for transfers between devices: 80.1 us -> 183 us
  starting transfers between devices: 124 us -> 25.2 us
  blocking collectives: 77.7 us -> 0 us
  local copies, waits for them, and re-layouts: 45.2 us -> 28.1 us
  other arithmetic: 50.8 us -> 34.6 us
  matrix products: 78.1 us -> 93.5 us
  Pallas kernels: 0 us -> 15.2 us
    ppermute x15 -> x25, waiting for transfers between devices: 50.2 us -> 183 us  [the longest x22 142 us: exchange(): lax.ppermute(pick((me + s) % count), axis, ring(count, s))]
    ppermute x15 -> x25, starting transfers between devices: 123 us -> 24.4 us  [the longest x22 19.7 us: exchange(): lax.ppermute(pick((me + s) % count), axis, ring(count, s))]
    psum x2 -> x0, blocking collectives: 43.5 us -> none  [the longest x1 37 us: shards(): lax.psum(jnp.stack([jnp.sum(scaled, -1), jnp.sum(scaled * standardized, -...]
    all_gather x2 -> x0, blocking collectives: 34.3 us -> none  [the longest x1 27.4 us: shards(): lax.all_gather(jnp.stack([block_mean, block_square]), ('row', 'col'), axi...]
    reduce_scatter x2, waiting for transfers between devices: 29.8 us -> 0.01 us  [the longest x1 0.01 us: shards(): lax.psum_scatter(jnp.concatenate(mixed_parts).reshape(n_col * cells, narr...]
    reshape x4 -> x0, local copies, waits for them, and re-layouts: 21.5 us -> none  [the longest x2 12.3 us: shards(): normed_part.reshape(utts, n_row, frames, per_row, width)]
    pallas_call x0 -> x1, Pallas kernels: none -> 15.2 us  [conv_block(): pl.pallas_call(functools.partial(conv_body, taps, span), grid=(utts, narr...]
    convert_element_type x5 -> x2, other arithmetic: 17.5 us -> 2.52 us  [the longest x1 1.33 us: shards(): normed_all = (xhat * gain_cols).astype(BF16)]
  transfers between devices with their start and end apart: 19 -> 29, of which waited for: 4 -> 13; matrix products, arithmetic and copies ran while one was open for 32% -> 35% of each run, Pallas kernels for 0% -> 0%
where the time goes in v1:
time: 401 us; the launch traced here: 395 us
  waiting for transfers between devices  183 us (46%)
  matrix products  93.5 us (23%)
  other arithmetic  34.6 us (9%)
  local copies, waits for them, and re-layouts  28.1 us (7%)
  starting transfers between devices  25.2 us (6%)
  Pallas kernels  15.2 us (4%)
  between operations  14.6 us (4%)
    ppermute x22, waiting for transfers between devices, exchange(): lax.ppermute(pick((me + s) % count), axis, ring(count, s))  142 us
    ppermute x2, waiting for transfers between devices, send_half(): lax.ppermute(columns((row + s) % n_row).astype(dtype), 'row', ring(n_row,...  40.6 us
    dot_general x3, matrix products, weight_grad(): lax.dot_general(left, right, CONTRACT_FIRST, preferred_element_type=F32)  34 us
    ppermute x22, starting transfers between devices, exchange(): lax.ppermute(pick((me + s) % count), axis, ring(count, s))  19.7 us
    pallas_call x1, Pallas kernels, conv_block(): pl.pallas_call(functools.partial(conv_body, taps, span), grid=(utts, narr...  15.2 us
    unnamed x72, local copies, waits for them, and re-layouts  14 us
    dot_general x2, matrix products, normed_part(): lax.dot_general(g, gate_weight, CONTRACT_LAST, preferred_element_type=F32)  13.3 us
    dot_general x4, matrix products, mixed_part(): lax.dot_general(grad_rows, rows[p], CONTRACT_LAST, preferred_element_type...  13 us
  transfers between devices with their start and end apart: 29, of which 13 were waited for; matrix products, arithmetic and copies ran while one was open for 35% of the time, Pallas kernels for 0%

profile of v1, /device:TPU:0, one launch (start us, length us, event | category | flops | bytes accessed | tf_op | source)
XLA Modules:
  0.0 394.8 jit_solution(589457628551755596)
XLA Ops:
  8.0 3.0 collective-permute-start.3
  11.0 17.8 %collective-permute-done.3 = bf16[1,256,1536]{2,1,0:T(8,128)(2,1)S(1)} collective-permute-done((bf16[1,256,1536]{2,1,0:T(8,128)(2,1)}, bf16[1,256,1536]{2,1,0:T(8,128)(2,1)S(1)}, u32[]{:S(2)}, u32[]{:S(2)}) %collective-permute-start.3) | collective-permute-done | bytes 786464 | tf_op jit(solution)/shard_map/ppermute | solution.py:38
  30.1 3.7 fusion.43
  33.8 3.1 fusion.42
  38.9 3.1 fusion.40
  42.0 3.1 fusion.41
  45.1 27.8 %collective-permute-done.4 = bf16[2,512,768]{2,1,0:T(8,128)(2,1)} collective-permute-done((bf16[2,512,768]{2,1,0:T(8,128)(2,1)S(1)}, bf16[2,512,768]{2,1,0:T(8,128)(2,1)}, u32[]{:S(2)}, u32[]{:S(2)}) %collective-permute-start.4) | collective-permute-done | bytes 1572896 | tf_op jit(solution)/shard_map/ppermute | solution.py:38
  72.9 3.3 broadcast_select_fusion.3
  84.6 3.8 pad_maximum_fusion.1
  89.8 29.4 %collective-permute-done = bf16[1,256,3072]{1,2,0:T(8,128)(2,1)} collective-permute-done((bf16[1,256,3072]{1,2,0:T(8,128)(2,1)}, bf16[1,256,3072]{1,2,0:T(8,128)(2,1)}, u32[]{:S(2)}, u32[]{:S(2)}) %collective-permute-start) | collective-permute-done | bytes 1572896 | tf_op jit(solution)/shard_map/ppermute | solution.py:38
  121.1 3.0 copy.27
  124.1 8.6 %fusion.71 = f32[512,1536]{1,0:T(8,128)S(1)} fusion(bf16[512,3072]{1,0:T(8,128)(2,1)} %bitcast.150, bf16[3072,1536]{1,0:T(8,128)(2,1)} %param.10), kind=kOutput, calls=%fused_computation.146 | convolution fusion | flops 4831838208 | bytes 15728640 | tf_op jit(solution)/shard_map/dot_general | solution.py:212
  134.6 7.6 %fusion.70 = f32[512,1536]{1,0:T(8,128)S(1)} fusion(bf16[512,3072]{1,0:T(8,128)(2,1)S(1)} %bitcast.152, bf16[3072,1536]{1,0:T(8,128)(2,1)} %param.9), kind=kOutput, calls=%fused_computation.145 | convolution fusion | flops 4831838208 | bytes 15728640 | tf_op jit(solution)/shard_map/dot_general | solution.py:213
  144.1 40.6 %collective-permute-done.1.value_in_ref = bf16[512,768]{1,0:T(8,128)(2,1)S(1)} collective-permute-done((bf16[512,768]{1,0:T(8,128)(2,1)S(1)}, bf16[512,768]{1,0:T(8,128)(2,1)S(1)}, u32[]{:S(2)}, u32[]{:S(2)}) %collective-permute-start.1) | collective-permute-done | bytes 786464 | tf_op jit(solution)/shard_map/ppermute | solution.py:207
  190.3 15.2 %conv_block.1 = (bf16[512,768]{1,0:T(8,128)(2,1)}, bf16[512,768]{1,0:T(8,128)(2,1)S(1)}, bf16[512,768]{1,0:T(8,128)(2,1)S(1)}, f32[1,31,768]{2,1,0:T(8,128)S(1)}) custom-call(f32[512,768]{1,0:T(8,128)S(1)} %constant_dynamic-slice_fusion.13.value_ref, bf16[512,768]{1,0:T(8,128)(2,1)S(1)} %copy-done.6, f32[512,768]{1,0:T(8,128)S(1)} %get-tuple-element.36.gate_ref, ...), custom_call_target="tpu_custom_call" | custom-call | flops 73138176 | bytes 7864320 | tf_op jit(solution)/shard_map/conv_block/pallas_call | solution.py:123
  210.2 3.7 constant_dynamic-slice_fusion.7
  215.6 15.0 %collective-permute-done.19 = f32[31,768]{1,0:T(8,128)S(1)} collective-permute-done((f32[31,768]{1,0:T(8,128)S(1)}, f32[31,768]{1,0:T(8,128)S(1)}, u32[]{:S(2)}, u32[]{:S(2)}) %collective-permute-start.19) | collective-permute-done | bytes 95264 | tf_op jit(solution)/shard_map/ppermute | solution.py:38
  233.6 5.5 %fusion.49 = f32[256,3072]{1,0:T(8,128)S(1)} fusion(bf16[3072,1536]{1,0:T(8,128)(2,1)} %param.9, bf16[1,2,256,1536]{3,2,1,0:T(8,128)(2,1)} %bitcast.29, s32[]{:T(128)S(6)} %select_n.257), kind=kOutput, calls=%fused_computation.93 | convolution fusion | flops 2415919104 | bytes 13369348 | tf_op jit(solution)/shard_map/dot_general | solution.py:237
  239.1 7.5 %collective-permute-done.8 = bf16[512,768]{1,0:T(8,128)(2,1)S(1)} collective-permute-done((bf16[512,768]{1,0:T(8,128)(2,1)S(1)}, bf16[512,768]{1,0:T(8,128)(2,1)S(1)}, u32[]{:S(2)}, u32[]{:S(2)}) %collective-permute-start.8) | collective-permute-done | bytes 786464 | tf_op jit(solution)/shard_map/ppermute | solution.py:38
  248.9 6.7 %fusion.6 = bf16[256,3072]{1,0:T(8,128)(2,1)S(1)} fusion(f32[256,3072]{1,0:T(8,128)S(1)} %fusion.49, bf16[3072,1536]{1,0:T(8,128)(2,1)} %param.10, bf16[1,2,256,1536]{3,2,1,0:T(8,128)(2,1)} %bitcast.31, s32[]{:T(128)S(6)} %select_n.257), kind=kOutput, calls=%fused_computation.14 | convolution fusion | flops 2417491968 | bytes 14942212 | tf_op jit(solution)/shard_map/dot_general | solution.py:239
  257.5 3.8 fusion.46
  261.8 6.6 %fusion.7 = bf16[256,3072]{1,0:T(8,128)(2,1)S(1)} fusion(f32[256,3072]{1,0:T(8,128)S(1)} %fusion.46, bf16[3072,1536]{1,0:T(8,128)(2,1)} %param.10, bf16[1,2,256,1536]{3,2,1,0:T(8,128)(2,1)} %bitcast.31, s32[]{:T(128)S(6)} %select_n.258), kind=kOutput, calls=%fused_computation.15 | convolution fusion | flops 2417491968 | bytes 14942212 | tf_op jit(solution)/shard_map/dot_general | solution.py:239
  268.5 23.1 %collective-permute-done.9 = bf16[2,256,1536]{2,1,0:T(8,128)(2,1)S(1)} collective-permute-done((bf16[2,256,1536]{2,1,0:T(8,128)(2,1)S(1)}, bf16[2,256,1536]{2,1,0:T(8,128)(2,1)S(1)}, u32[]{:S(2)}, u32[]{:S(2)}) %collective-permute-start.9) | collective-permute-done | bytes 1572896 | tf_op jit(solution)/shard_map/ppermute | solution.py:38
  294.6 3.8 constant_dynamic-slice_fusion.8
  298.3 3.1 copy.31
  302.7 6.5 %fusion.5 = (f32[4,1536]{1,0:T(4,128)S(1)}, f32[256]{0:T(256)S(1)}, f32[256]{0:T(256)S(1)}, f32[4,1,256,1536]{3,2,0,1:T(8,128)}) fusion(bf16[2,1,256,1536]{3,2,0,1:T(8,128)(2,1)} %bitcast.147, bf16[2,1,256,1536]{3,2,0,1:T(8,128)(2,1)} %bitcast.146, f32[256]{0:T(256)S(1)} %add_rsqrt_fusion, f32[256]{0:T(256)S(1)} %broadcast_multiply_fusion, ...), kind=kLoop, calls=%fused_computation.11 | loop fusion | flops 17294848 | bytes 12636160 | tf_op jit(solution)/shard_map/reduce_sum | solution.py:255
  310.5 12.5 %fusion.8 = f32[1536,1536]{1,0:T(8,128)} fusion(bf16[512,1536]{1,0:T(8,128)(2,1)} %collective-permute-done.14, bf16[512,768]{1,0:T(8,128)(2,1)S(1)} %copy-done.26, bf16[512,768]{1,0:T(8,128)(2,1)S(1)} %copy-done.24, bf16[512,1536]{1,0:T(8,128)(2,1)} %collective-permute-done.13, bf16[512,1536]{1,0:T(8,128)(2,1)S(1)} %copy-done.29), kind=kOutput, calls=%fused_computation.22 | convolution fusion | flops 4847566848 | bytes 15728640 | tf_op jit(solution)/shard_map/dot_general | solution.py:292
  324.5 11.9 %collective-permute-done.5 = bf16[2,1,512,768]{2,3,0,1:T(8,128)(2,1)} collective-permute-done((bf16[2,1,512,768]{2,3,0,1:T(8,128)(2,1)}, bf16[2,1,512,768]{2,3,0,1:T(8,128)(2,1)}, u32[]{:S(2)}, u32[]{:S(2)}) %collective-permute-start.5) | collective-permute-done | bytes 1572896 | tf_op jit(solution)/shard_map/ppermute | solution.py:38
  338.3 7.7 %fusion.72 = f32[512,1536]{1,0:T(8,128)S(1)} fusion(bf16[512,3072]{0,1:T(8,128)(2,1)S(1)} %bitcast.153, bf16[3072,1536]{1,0:T(8,128)(2,1)} %param.11), kind=kOutput, calls=%fused_computation.147 | convolution fusion | flops 4831838208 | bytes 15728640 | tf_op jit(solution)/shard_map/dot_general | solution.py:274
  348.0 12.6 %fusion.14 = f32[1536,1536]{1,0:T(8,128)} fusion(bf16[512,1536]{1,0:T(8,128)(2,1)} %collective-permute-done.15, bf16[512,768]{1,0:T(8,128)(2,1)S(1)} %copy-done.22, bf16[512,768]{1,0:T(8,128)(2,1)S(1)} %copy-done.20, bf16[512,1536]{1,0:T(8,128)(2,1)} %collective-permute-done.13, bf16[512,1536]{1,0:T(8,128)(2,1)S(1)} %copy-done.30), kind=kOutput, calls=%fused_computation.28 | convolution fusion | flops 4847566848 | bytes 15728640 | tf_op jit(solution)/shard_map/dot_general | solution.py:292
  370.9 3.4 collective-permute-done.22
  376.1 8.9 %fusion.20 = f32[1536,1536]{1,0:T(8,128)} fusion(bf16[512,1536]{0,1:T(8,128)(2,1)S(1)} %collective-permute-done.16, bf16[512,1536]{0,1:T(8,128)(2,1)S(1)} %get-tuple-element.23, bf16[512,1536]{1,0:T(8,128)(2,1)} %collective-permute-done.17, bf16[512,1536]{1,0:T(8,128)(2,1)S(1)} %bitcast.163), kind=kOutput, calls=%fused_computation.34 | convolution fusion | flops 4844421120 | bytes 15728640 | tf_op jit(solution)/shard_map/dot_general | solution.py:292
  (168 shorter events, 64.8 us)
Async XLA Ops:
  7.2 136.8 %copy-start = (f32[31,1536]{1,0:T(8,128)S(1)}, f32[31,1536]{1,0:T(8,128)}, u32[]{:S(2)}) copy-start(f32[31,1536]{1,0:T(8,128)} %param.12) | copy-start | bytes 571396
  7.2 69.1 %all-gather.5.cloned.1.call-start = ((), (), s32[]{:S(2)}) async-start(), calls=%async_computation.4 | async-start | bytes 3932160 | tf_op jit(solution)/shard_map/all_gather | solution.py:186
  7.9 178.7 %reduce-scatter.3.cloned.1.call-start = ((), (), s32[]{:S(2)}) async-start(), calls=%async_computation.2 | async-start | bytes 3932160 | tf_op jit(solution)/shard_map/reduce_scatter | solution.py:176
  8.0 20.8 %collective-permute-start.3 = (bf16[1,256,1536]{2,1,0:T(8,128)(2,1)}, bf16[1,256,1536]{2,1,0:T(8,128)(2,1)S(1)}, u32[]{:S(2)}, u32[]{:S(2)}) collective-permute-start(bf16[1,256,1536]{2,1,0:T(8,128)(2,1)} %param.8), channel_id=1, source_target_pairs={{0,8},{8,0},{1,9},{9,1},{2,10},{10,2},{3,11},{11,3},{4,12},{12,4},... | collective-permute-start | bytes 2359304 | tf_op jit(solution)/shard_map/ppermute | solution.py:38
  37.1 35.9 %collective-permute-start.4 = (bf16[2,512,768]{2,1,0:T(8,128)(2,1)S(1)}, bf16[2,512,768]{2,1,0:T(8,128)(2,1)}, u32[]{:S(2)}, u32[]{:S(2)}) collective-permute-start(bf16[2,512,768]{2,1,0:T(8,128)(2,1)S(1)} %pad_maximum_fusion.9), channel_id=1, source_target_pairs={{0,8},{8,0},{1,9},{9,1},{2,10},{10,2},{3,11},{11,3},{4,12},{12,4},... | collective-permute-start | bytes 4718600 | tf_op jit(solution)/shard_map/ppermute | solution.py:38
  83.2 36.0 %collective-permute-start = (bf16[1,256,3072]{1,2,0:T(8,128)(2,1)}, bf16[1,256,3072]{1,2,0:T(8,128)(2,1)}, u32[]{:S(2)}, u32[]{:S(2)}) collective-permute-start(bf16[1,256,3072]{1,2,0:T(8,128)(2,1)} %bitcast.164), channel_id=1, source_target_pairs={{0,8},{8,0},{1,9},{9,1},{2,10},{10,2},{3,11},{11,3},{4,12},{12,4},... | collective-permute-start | bytes 4718600 | tf_op jit(solution)/shard_map/ppermute | solution.py:38
  88.5 206.1 %all-gather.7.cloned.1.call-start = ((), (), s32[]{:S(2)}) async-start(), calls=%async_computation.5 | async-start | bytes 3932160 | tf_op jit(solution)/shard_map/all_gather | solution.py:264
  133.0 52.5 %collective-permute-start.2 = (f32[512,768]{1,0:T(8,128)S(1)}, f32[512,768]{1,0:T(8,128)S(1)}, u32[]{:S(2)}, u32[]{:S(2)}) collective-permute-start(f32[512,768]{1,0:T(8,128)S(1)} %get-tuple-element.35), channel_id=1, source_target_pairs={{0,8},{8,0},{1,9},{9,1},{2,10},{10,2},{3,11},{11,3},{4,12},{12,4},... | collective-permute-start | bytes 4718600 | tf_op jit(solution)/shard_map/ppermute | solution.py:207
  142.4 42.2 %collective-permute-start.1 = (bf16[512,768]{1,0:T(8,128)(2,1)S(1)}, bf16[512,768]{1,0:T(8,128)(2,1)S(1)}, u32[]{:S(2)}, u32[]{:S(2)}) collective-permute-start(bf16[512,768]{1,0:T(8,128)(2,1)S(1)} %dynamic-slice_convert_fusion.1), channel_id=1, source_target_pairs={{0,8},{8,0},{1,9},{9,1},{2,10},{10,2},{3,11},{11,3},{4,12},{12,4},... | collective-permute-start | bytes 2359304 | tf_op jit(solution)/shard_map/ppermute | solution.py:207
  207.3 2.1 collective-permute-start.18
  207.4 168.7 %collective-permute-start.17 = (bf16[512,1536]{1,0:T(8,128)(2,1)}, bf16[512,1536]{1,0:T(8,128)(2,1)}, u32[]{:S(2)}, u32[]{:S(2)}) collective-permute-start(bf16[512,1536]{1,0:T(8,128)(2,1)} %bitcast.162), channel_id=1, source_target_pairs={{0,1},{1,0},{2,3},{3,2},{4,5},{5,4},{6,7},{7,6},{8,9},{9,8},{10,11... | collective-permute-start | bytes 4718600 | tf_op jit(solution)/shard_map/ppermute | solution.py:38
  207.9 23.4 %collective-permute-start.7 = (bf16[512,768]{1,0:T(8,128)(2,1)}, bf16[512,768]{1,0:T(8,128)(2,1)S(1)}, u32[]{:S(2)}, u32[]{:S(2)}) collective-permute-start(bf16[512,768]{1,0:T(8,128)(2,1)} %copy-done.9), channel_id=1, source_target_pairs={{0,8},{8,0},{1,9},{9,1},{2,10},{10,2},{3,11},{11,3},{4,12},{12,4},... | collective-permute-start | bytes 2359304 | tf_op jit(solution)/shard_map/ppermute | solution.py:38
  209.5 21.9 %copy-start.10 = (bf16[512,768]{1,0:T(8,128)(2,1)S(1)}, bf16[512,768]{1,0:T(8,128)(2,1)}, u32[]{:S(2)}) copy-start(bf16[512,768]{1,0:T(8,128)(2,1)} %copy-done.9) | copy-start | bytes 2359300
  209.5 21.2 %collective-permute-start.19 = (f32[31,768]{1,0:T(8,128)S(1)}, f32[31,768]{1,0:T(8,128)S(1)}, u32[]{:S(2)}, u32[]{:S(2)}) collective-permute-start(f32[31,768]{1,0:T(8,128)S(1)} %bitcast_add_fusion.2), channel_id=1, source_target_pairs={{0,8},{8,0},{1,9},{9,1},{2,10},{10,2},{3,11},{11,3},{4,12},{12,4},... | collective-permute-start | bytes 285704 | tf_op jit(solution)/shard_map/ppermute | solution.py:38
  214.0 95.3 %collective-permute-start.13 = (bf16[512,1536]{1,0:T(8,128)(2,1)}, bf16[512,1536]{1,0:T(8,128)(2,1)}, u32[]{:S(2)}, u32[]{:S(2)}) collective-permute-start(bf16[512,1536]{1,0:T(8,128)(2,1)} %get-tuple-element.26), channel_id=1, source_target_pairs={{0,1},{1,0},{2,3},{3,2},{4,5},{5,4},{6,7},{7,6},{8,9},{9,8},{10,11... | collective-permute-start | bytes 4718600 | tf_op jit(solution)/shard_map/ppermute | solution.py:38
  214.0 171.0 %reduce-scatter.5.cloned.1.call-start = ((), (), s32[]{:S(2)}) async-start(), calls=%async_computation.3 | async-start | bytes 3932160 | tf_op jit(solution)/shard_map/reduce_scatter | solution.py:246
  214.2 32.4 %collective-permute-start.8 = (bf16[512,768]{1,0:T(8,128)(2,1)S(1)}, bf16[512,768]{1,0:T(8,128)(2,1)S(1)}, u32[]{:S(2)}, u32[]{:S(2)}) collective-permute-start(bf16[512,768]{1,0:T(8,128)(2,1)S(1)} %copy-done.8), channel_id=1, source_target_pairs={{0,8},{8,0},{1,9},{9,1},{2,10},{10,2},{3,11},{11,3},{4,12},{12,4},... | collective-permute-start | bytes 2359304 | tf_op jit(solution)/shard_map/ppermute | solution.py:38
  255.9 35.7 %collective-permute-start.9 = (bf16[2,256,1536]{2,1,0:T(8,128)(2,1)S(1)}, bf16[2,256,1536]{2,1,0:T(8,128)(2,1)S(1)}, u32[]{:S(2)}, u32[]{:S(2)}) collective-permute-start(bf16[2,256,1536]{2,1,0:T(8,128)(2,1)S(1)} %pad_maximum_fusion.13), channel_id=1, source_target_pairs={{0,8},{8,0},{1,9},{9,1},{2,10},{10,2},{3,11},{11,3},{4,12},{12,4},... | collective-permute-start | bytes 4718600 | tf_op jit(solution)/shard_map/ppermute | solution.py:38
  261.2 49.2 %collective-permute-start.14 = (bf16[512,1536]{1,0:T(8,128)(2,1)}, bf16[512,1536]{1,0:T(8,128)(2,1)}, u32[]{:S(2)}, u32[]{:S(2)}) collective-permute-start(bf16[512,1536]{1,0:T(8,128)(2,1)} %pad_maximum_fusion.11), channel_id=1, source_target_pairs={{0,1},{1,0},{2,3},{3,2},{4,5},{5,4},{6,7},{7,6},{8,9},{9,8},{10,11... | collective-permute-start | bytes 4718600 | tf_op jit(solution)/shard_map/ppermute | solution.py:38
  261.3 86.6 %collective-permute-start.15 = (bf16[512,1536]{1,0:T(8,128)(2,1)}, bf16[512,1536]{1,0:T(8,128)(2,1)}, u32[]{:S(2)}, u32[]{:S(2)}) collective-permute-start(bf16[512,1536]{1,0:T(8,128)(2,1)} %pad_maximum_fusion.12), channel_id=1, source_target_pairs={{0,1},{1,0},{2,3},{3,2},{4,5},{5,4},{6,7},{7,6},{8,9},{9,8},{10,11... | collective-permute-start | bytes 4718600 | tf_op jit(solution)/shard_map/ppermute | solution.py:38
  301.4 35.0 %collective-permute-start.5 = (bf16[2,1,512,768]{2,3,0,1:T(8,128)(2,1)}, bf16[2,1,512,768]{2,3,0,1:T(8,128)(2,1)}, u32[]{:S(2)}, u32[]{:S(2)}) collective-permute-start(bf16[2,1,512,768]{2,3,0,1:T(8,128)(2,1)} %copy.31), channel_id=1, source_target_pairs={{0,8},{8,0},{1,9},{9,1},{2,10},{10,2},{3,11},{11,3},{4,12},{12,4},... | collective-permute-start | bytes 4718600 | tf_op jit(solution)/shard_map/ppermute | solution.py:38
  309.2 51.6 %collective-permute-start.12 = (f32[2,1,256]{2,1,0:T(1,128)S(1)}, f32[2,1,256]{2,1,0:T(1,128)S(1)}, u32[]{:S(2)}, u32[]{:S(2)}) collective-permute-start(f32[2,1,256]{2,1,0:T(1,128)S(1)} %pad_maximum_fusion.16), channel_id=1, source_target_pairs={{0,6},{2,0},{4,2},{6,4},{1,7},{3,1},{5,3},{7,5},{8,14},{10,8},{12,... | collective-permute-start | bytes 6152 | tf_op jit(solution)/shard_map/ppermute | solution.py:38
  310.5 12.5 %collective-permute-start.20 = (f32[4,1536]{1,0:T(4,128)S(1)}, f32[4,1536]{1,0:T(4,128)S(1)}, u32[]{:S(2)}, u32[]{:S(2)}) collective-permute-start(f32[4,1536]{1,0:T(4,128)S(1)} %get-tuple-element.15), channel_id=1, source_target_pairs={{0,1},{1,0},{2,3},{3,2},{4,5},{5,4},{6,7},{7,6},{8,9},{9,8},{10,11... | collective-permute-start | bytes 73736 | tf_op jit(solution)/shard_map/ppermute | solution.py:38
  323.0 37.7 %collective-permute-start.21 = (f32[4,1536]{1,0:T(4,128)S(1)}, f32[4,1536]{1,0:T(4,128)S(1)}, u32[]{:S(2)}, u32[]{:S(2)}) collective-permute-start(f32[4,1536]{1,0:T(4,128)S(1)} %add.218), channel_id=1, source_target_pairs={{0,8},{8,0},{1,9},{9,1},{2,10},{10,2},{3,11},{11,3},{4,12},{12,4},... | collective-permute-start | bytes 73736 | tf_op jit(solution)/shard_map/ppermute | solution.py:38
  346.1 28.7 %collective-permute-start.6 = (bf16[1,256,1536]{2,1,0:T(8,128)(2,1)S(1)}, bf16[1,256,1536]{2,1,0:T(8,128)(2,1)S(1)}, u32[]{:S(2)}, u32[]{:S(2)}) collective-permute-start(bf16[1,256,1536]{2,1,0:T(8,128)(2,1)S(1)} %fusion.44), channel_id=1, source_target_pairs={{0,8},{8,0},{1,9},{9,1},{2,10},{10,2},{3,11},{11,3},{4,12},{12,4},... | collective-permute-start | bytes 2359304 | tf_op jit(solution)/shard_map/ppermute | solution.py:45
  347.9 27.0 %copy-start.17 = (bf16[1,256,1536]{2,1,0:T(8,128)(2,1)S(1)}, bf16[1,256,1536]{2,1,0:T(8,128)(2,1)}, u32[]{:S(2)}) copy-start(bf16[1,256,1536]{2,1,0:T(8,128)(2,1)} %param.7) | copy-start | bytes 2359300
  347.9 28.2 %collective-permute-start.16 = (bf16[512,1536]{0,1:T(8,128)(2,1)S(1)}, bf16[512,1536]{0,1:T(8,128)(2,1)S(1)}, u32[]{:S(2)}, u32[]{:S(2)}) collective-permute-start(bf16[512,1536]{0,1:T(8,128)(2,1)S(1)} %get-tuple-element.24), channel_id=1, source_target_pairs={{0,1},{1,0},{2,3},{3,2},{4,5},{5,4},{6,7},{7,6},{8,9},{9,8},{10,11... | collective-permute-start | bytes 4718600 | tf_op jit(solution)/shard_map/ppermute | solution.py:38
  360.7 4.5 %collective-permute-start.11 = (f32[2,1,256]{2,1,0:T(1,128)S(1)}, f32[2,1,256]{2,1,0:T(1,128)S(1)}, u32[]{:S(2)}, u32[]{:S(2)}) collective-permute-start(f32[2,1,256]{2,1,0:T(1,128)S(1)} %pad_maximum_fusion.16), channel_id=1, source_target_pairs={{0,4},{2,6},{4,0},{6,2},{1,5},{3,7},{5,1},{7,3},{8,12},{10,14},{12... | collective-permute-start | bytes 6152 | tf_op jit(solution)/shard_map/ppermute | solution.py:38
  360.9 5.4 %collective-permute-start.10 = (f32[2,1,256]{2,1,0:T(1,128)S(1)}, f32[2,1,256]{2,1,0:T(1,128)S(1)}, u32[]{:S(2)}, u32[]{:S(2)}) collective-permute-start(f32[2,1,256]{2,1,0:T(1,128)S(1)} %pad_maximum_fusion.16), channel_id=1, source_target_pairs={{0,2},{2,4},{4,6},{6,0},{1,3},{3,5},{5,7},{7,1},{8,10},{10,12},{12... | collective-permute-start | bytes 6152 | tf_op jit(solution)/shard_map/ppermute | solution.py:38
  365.2 3.7 collective-permute-start.24
  366.3 4.6 %collective-permute-start.23 = (f32[1536]{0:T(1024)S(1)}, f32[1536]{0:T(1024)S(1)}, u32[]{:S(2)}, u32[]{:S(2)}) collective-permute-start(f32[1536]{0:T(1024)S(1)} %get-tuple-element.20), channel_id=1, source_target_pairs={{0,4},{2,6},{4,0},{6,2},{1,5},{3,7},{5,1},{7,3},{8,12},{10,14},{12... | collective-permute-start | bytes 18440 | tf_op jit(solution)/shard_map/ppermute | solution.py:38
  368.8 5.4 %collective-permute-start.22 = (f32[1536]{0:T(1024)S(1)}, f32[1536]{0:T(1024)S(1)}, u32[]{:S(2)}, u32[]{:S(2)}) collective-permute-start(f32[1536]{0:T(1024)S(1)} %get-tuple-element.18), channel_id=1, source_target_pairs={{0,2},{2,4},{4,6},{6,0},{1,3},{3,5},{5,7},{7,1},{8,10},{10,12},{12... | collective-permute-start | bytes 18440 | tf_op jit(solution)/shard_map/ppermute | solution.py:38
  (32 other events, 150.4 us)
Sparse Core Ops, SparseCore 0:
  9.6 66.1 all-gather.4
  88.6 60.5 reduce-scatter.2
  214.1 62.1 all-gather.6
  294.7 58.9 reduce-scatter.4

commit v2 on v1

v2 whole, which is shorter than its diff:
```python
import functools

import jax
import jax.numpy as jnp
from jax import lax
from jax.experimental import pallas as pl
from jax.experimental.pallas import tpu as pltpu
from jax.sharding import PartitionSpec as P

EPS = 1e-05
CONTRACT_LAST = (((1,), (1,)), ((), ()))
CONTRACT_FIRST = (((0,), (0,)), ((), ()))
BF16 = jnp.bfloat16
F32 = jnp.float32
CONV_ROWS = 64
CONV_VMEM = 56 << 20
NORM_ROWS = 32
BACK_TILE = 512
BACK_VMEM = 40 << 20
NORM_VMEM = 24 << 20
PARTS = 2


def ring(count, shift):
    return [(i, (i + shift) % count) for i in range(count)]


def by_source(pieces, axis):
    count, me = lax.axis_size(axis), lax.axis_index(axis)
    ordered = []
    for j in range(count):
        back = (me - j) % count
        block = pieces[0]
        for s in range(1, count):
            block = jnp.where(back == s, pieces[s], block)
        ordered.append(block)
    return ordered


def exchange(pick, axis):
    count, me = lax.axis_size(axis), lax.axis_index(axis)
    return [pick(me)] + [
        lax.ppermute(pick((me + s) % count), axis, ring(count, s)) for s in range(1, count)
    ]


def after(x, *others):
    return lax.optimization_barrier((x,) + others)[0]


def dot(a, b):
    return jnp.dot(a, b, preferred_element_type=F32)


def dot_last(a, b):
    return lax.dot_general(a, b, CONTRACT_LAST, preferred_element_type=F32)


def sum_over(x, axis):
    pieces = exchange(lambda i: x, axis)
    return sum(pieces[1:], pieces[0])


def conv_body(taps, frames, rows_in, row_ref, *refs):
    parts = [refs[i * rows_in : (i + 1) * rows_in] for i in range(4)]
    grad_ref, kernel_ref, mixed_ref, pair_ref, taps_ref = refs[4 * rows_in : 4 * rows_in + 5]
    glu_pad, grad_pad, partial, value_sum, gate_sum = refs[4 * rows_in + 5 :]
    half = taps // 2
    span = frames * rows_in
    lead = 16
    lanes = glu_pad.shape[1]
    chunk = CONV_ROWS
    per_block = frames // chunk
    row = row_ref[0]
    zeros = jnp.zeros((lead, lanes), F32)
    for pad in (glu_pad, grad_pad):
        pad[pl.ds(0, lead)] = zeros
        pad[pl.ds(lead + span, lead)] = zeros
    partial[...] = jnp.zeros_like(partial)

    def rows(i):
        return pl.ds(pl.multiple_of(i * chunk, chunk), chunk)

    def frame(i):
        block = lax.div(i, per_block)
        place = lax.rem(row - block + rows_in, rows_in)
        return pl.multiple_of(place * frames + (i - block * per_block) * chunk, chunk)

    for k in range(rows_in):
        value_ref, value_in_ref, gate_ref, gate_in_ref = (p[k] for p in parts)

        @pl.loop(0, per_block)
        def _(i, k=k):
            gate = gate_ref[rows(i)] + gate_in_ref[rows(i)]
            value = value_ref[rows(i)] + value_in_ref[rows(i)].astype(F32)
            at = i + k * per_block
            gate_sum[rows(at)] = gate
            value_sum[rows(at)] = value
            glu_pad[pl.ds(pl.multiple_of(frame(at) + lead, 8), chunk)] = (
                (value * jax.nn.sigmoid(gate)).astype(BF16).astype(F32)
            )

    @pl.loop(0, span // chunk)
    def _(i):
        at = frame(i) + lead
        conv = jnp.zeros((chunk, lanes), F32)
        for tap in range(taps):
            conv = conv + kernel_ref[pl.ds(tap, 1)] * glu_pad[pl.ds(at + (tap - half), chunk)]
        sig = jax.nn.sigmoid(conv)
        mixed_ref[rows(i)] = (conv * sig).astype(BF16)
        slope = sig * (1.0 + conv * (1.0 - sig))
        grad = (grad_ref[rows(i)].astype(F32) * slope).astype(BF16).astype(F32)
        grad_pad[pl.ds(pl.multiple_of(at, 8), chunk)] = grad

    @pl.loop(0, span // chunk)
    def _(i):
        at = frame(i) + lead
        grad = grad_pad[pl.ds(pl.multiple_of(at, 8), chunk)]
        total = jnp.zeros((chunk, lanes), F32)
        for tap in range(taps):
            total = total + kernel_ref[pl.ds(tap, 1)] * grad_pad[pl.ds(at + (half - tap), chunk)]
            product = glu_pad[pl.ds(at + (tap - half), chunk)] * grad
            partial[pl.ds(8 * tap, 8)] += sum(
                product[8 * j : 8 * j + 8] for j in range(chunk // 8)
            )
        sig = jax.nn.sigmoid(gate_sum[rows(i)])
        block = lax.div(i, per_block)
        inside = pl.ds(pl.multiple_of((i - block * per_block) * chunk, chunk), chunk)
        pair_ref[block, 0, inside] = (total * sig).astype(BF16)
        pair_ref[block, 1, inside] = (total * value_sum[rows(i)] * sig * (1.0 - sig)).astype(BF16)

    for tap in range(taps):
        taps_ref[pl.ds(tap, 1)] = jnp.sum(partial[pl.ds(8 * tap, 8)], 0, keepdims=True)


def conv_block(row, values, values_in, gates, gates_in, mixed_grad, conv_kernel, frames):
    rows_in = len(values)
    span, narrow = mixed_grad.shape
    taps = conv_kernel.shape[0]
    lanes = 128 if narrow % 128 == 0 else narrow
    steps = narrow // lanes
    if lanes == narrow:
        values, gates, (conv_kernel,) = (
            [lax.dynamic_slice_in_dim(x, row * narrow, narrow, 1) for x in xs]
            for xs in (values, gates, [conv_kernel])
        )

    def at(j, row):
        return (0, j) if lanes == narrow else (0, row[0] * steps + j)

    inner = pl.BlockSpec((frames, lanes), lambda j, row: (0, j))
    outer = pl.BlockSpec((frames, lanes), at)
    tall = pl.BlockSpec((span, lanes), lambda j, row: (0, j))
    work = span * narrow
    return pl.pallas_call(
        functools.partial(conv_body, taps, frames, rows_in),
        grid_spec=pltpu.PrefetchScalarGridSpec(
            num_scalar_prefetch=1,
            grid=(steps,),
            in_specs=[outer] * rows_in
            + [inner] * rows_in
            + [outer] * rows_in
            + [inner] * rows_in
            + [tall, pl.BlockSpec((taps, lanes), at)],
            out_specs=[
                tall,
                pl.BlockSpec((rows_in, 2, frames, lanes), lambda j, row: (0, 0, 0, j)),
                pl.BlockSpec((taps, lanes), lambda j, row: (0, j)),
            ],
            scratch_shapes=[
                pltpu.VMEM((span + 32, lanes), F32),
                pltpu.VMEM((span + 32, lanes), F32),
                pltpu.VMEM((8 * taps, lanes), F32),
                pltpu.VMEM((span, lanes), F32),
                pltpu.VMEM((span, lanes), F32),
            ],
        ),
        out_shape=[
            jax.ShapeDtypeStruct((span, narrow), BF16),
            jax.ShapeDtypeStruct((rows_in, 2, frames, narrow), BF16),
            jax.ShapeDtypeStruct((taps, narrow), F32),
        ],
        compiler_params=pltpu.CompilerParams(vmem_limit_bytes=CONV_VMEM),
        cost_estimate=pl.CostEstimate(
            flops=6 * taps * work, bytes_accessed=20 * work, transcendentals=3 * work
        ),
        name="conv_block",
    )(row.reshape(1), *values, *values_in, *gates, *gates_in, mixed_grad, conv_kernel)


def back_body(value_ref, gate_ref, value_weight_ref, gate_weight_ref, out_ref):
    out_ref[...] = (
        dot_last(value_ref[...], value_weight_ref[...])
        + dot_last(gate_ref[...], gate_weight_ref[...])
    ).astype(BF16)


def back_block(value, gate, value_weight, gate_weight):
    rows, width = value.shape
    depth = value_weight.shape[0]
    tile = BACK_TILE if width % BACK_TILE == 0 else width
    tiles = width // tile
    left = pl.BlockSpec((rows, width), lambda i: (0, 0))
    right = pl.BlockSpec((tile, width), lambda i: (i, 0))
    return pl.pallas_call(
        back_body,
        grid=(depth // tile,),
        in_specs=[left, left, right, right],
        out_specs=pl.BlockSpec((None, rows, tile), lambda i: (i // tiles, 0, i % tiles)),
        out_shape=jax.ShapeDtypeStruct((depth // width, rows, width), BF16),
        compiler_params=pltpu.CompilerParams(vmem_limit_bytes=BACK_VMEM),
        cost_estimate=pl.CostEstimate(
            flops=4 * rows * depth * width,
            bytes_accessed=4 * depth * width + 4 * rows * width + 2 * rows * depth,
            transcendentals=0,
        ),
        name="back_block",
    )(value, gate, value_weight, gate_weight)


def norm_body(per_row, n_row, row_ref, x_ref, gain_ref, *outs):
    n_col, rows, width = x_ref.shape
    mean_ref, inverse_ref = outs[n_row:]
    row = row_ref[0]
    total = sum(x_ref[j].astype(F32) for j in range(n_col))
    mean = jnp.sum(total, -1, keepdims=True) / (n_col * width)
    square = jnp.zeros((rows, width), F32)
    for j in range(n_col):
        centered = x_ref[j].astype(F32) - mean
        square = square + centered * centered
    inverse = lax.rsqrt(jnp.sum(square, -1, keepdims=True) / (n_col * width) + EPS)
    mean_ref[...] = mean
    inverse_ref[...] = inverse
    for s in range(n_row):
        for p in range(per_row):
            j = lax.rem(row + s, n_row) * per_row + p
            xhat = (x_ref[j].astype(F32) - mean) * inverse
            outs[s][:, p * width : (p + 1) * width] = (xhat * gain_ref[j]).astype(BF16)


def norm_block(row, x, gain_cols, n_row):
    n_col, rows, width = x.shape
    per_row = n_col // n_row
    step = NORM_ROWS
    whole = pl.BlockSpec((step, per_row * width), lambda i, row: (i, 0))
    thin = pl.BlockSpec((step, 1), lambda i, row: (i, 0))
    work = n_col * rows * width
    return pl.pallas_call(
        functools.partial(norm_body, per_row, n_row),
        grid_spec=pltpu.PrefetchScalarGridSpec(
            num_scalar_prefetch=1,
            grid=(rows // step,),
            in_specs=[
                pl.BlockSpec((n_col, step, width), lambda i, row: (0, i, 0)),
                pl.BlockSpec((n_col, 1, width), lambda i, row: (0, 0, 0)),
            ],
            out_specs=[whole] * n_row + [thin] * 2,
        ),
        out_shape=[jax.ShapeDtypeStruct((rows, per_row * width), BF16)] * n_row
        + [jax.ShapeDtypeStruct((rows, 1), F32)] * 2,
        compiler_params=pltpu.CompilerParams(vmem_limit_bytes=NORM_VMEM),
        cost_estimate=pl.CostEstimate(
            flops=10 * work, bytes_accessed=4 * work, transcendentals=rows
        ),
        name="norm_block",
    )(row.reshape(1), x, gain_cols)


def shards(
    features, output_gradient, value_weight, gate_weight, mixer_weight, conv_kernel, layer_norm_gain
):
    utts, frames, width = features.shape
    model = layer_norm_gain.shape[0]
    n_row, n_col, n_dp = lax.axis_size("row"), lax.axis_size("col"), lax.axis_size("dp")
    row, col = lax.axis_index("row"), lax.axis_index("col")
    per_row = n_col // n_row
    depth = per_row * width
    narrow = width // n_row
    tokens = utts * frames
    shifts = range(1, n_row)

    def to_row(x, s):
        return lax.ppermute(x, "row", ring(n_row, s))

    def rolled(blocks, s):
        return [blocks[(k - s) % n_row] for k in range(n_row)]

    def placed(pieces):
        buffer = jnp.zeros((n_row,) + pieces[0].shape, pieces[0].dtype)
        for k, piece in enumerate(pieces):
            buffer = lax.dynamic_update_index_in_dim(buffer, piece, (row - k) % n_row, 0)
        return buffer.reshape((-1,) + pieces[0].shape[1:])

    own = features.reshape(tokens, width)
    own_grad = output_gradient.reshape(tokens, width)
    part = tokens // PARTS
    gathered = [
        lax.all_gather(own[i * part : (i + 1) * part], "col", axis=0) for i in range(PARTS)
    ]

    mixer_rows = mixer_weight.reshape(per_row, n_row, narrow, width)
    mixer_of = [
        lax.dynamic_index_in_dim(mixer_rows, (row - k) % n_row, 1, keepdims=False).reshape(
            per_row * narrow, width
        )
        for k in range(n_row)
    ]

    def by_narrow(x):
        return jnp.stack([x[:, p * narrow : (p + 1) * narrow] for p in range(per_row)])

    def mixed_part(rows, s):
        return by_narrow(dot_last(rows, mixer_of[-s % n_row]).astype(BF16))

    grads = [own_grad] + [to_row(own_grad, s) for s in shifts]
    grad_rows = jnp.concatenate(grads)
    mixed_parts = [jnp.concatenate([mixed_part(g, 0) for g in grads], 1)]
    for s in shifts:
        sent = [mixed_part(g, s) for g in grads]
        arrived = [to_row(sent[(k - s) % n_row], s) for k in range(n_row)]
        mixed_parts.append(jnp.concatenate(arrived, 1))
    mixed_parts = jnp.concatenate(by_source(mixed_parts, "row"))

    gain_cols = layer_norm_gain.reshape(n_col, 1, width)
    means, inverses, kept, crossed, sent_out = [], [], [], [], []
    for x in gathered:
        if crossed:
            x = after(x, *crossed[-1])
        *pieces, mean, inverse = norm_block(row, x, gain_cols, n_row)
        kept.append(pieces[0])
        sent_out.append(pieces[1:])
        crossed.append([to_row(x, s) for s, x in zip(shifts, pieces[1:])])
        means.append(mean)
        inverses.append(inverse)
    mean, inverse = jnp.concatenate(means), jnp.concatenate(inverses)
    normed_own = jnp.concatenate(kept)
    normed_in = [jnp.concatenate([c[s - 1] for c in crossed]) for s in shifts]
    normed = jnp.concatenate([normed_own] + normed_in)

    mixed_grad = lax.psum_scatter(
        mixed_parts.reshape(n_col * n_row * tokens, narrow),
        "col",
        scatter_dimension=0,
        tiled=True,
    )

    def columns(x, i):
        return lax.dynamic_slice_in_dim(x, i * narrow, narrow, 1)

    gate_own, value_own = dot(normed_own, gate_weight), dot(normed_own, value_weight)
    rest = jnp.concatenate(normed_in)
    gate_rest, value_rest = dot(rest, gate_weight), dot(rest, value_weight)

    def reduced(first, others, dtype):
        blocks = [first] + [others[k * tokens : (k + 1) * tokens] for k in range(n_row - 1)]
        total = None
        for s in shifts:
            sent = [columns(x, (row + s) % n_row).astype(dtype) for x in blocks]
            sent[0] = after(sent[0], *crossed[-1])
            arrived = [to_row(sent[(k - s) % n_row], s) for k in range(n_row)]
            if total is None:
                total = arrived
            else:
                total = [t.astype(F32) + x.astype(F32) for t, x in zip(total, arrived)]
        return blocks, total

    gate, gate_in = reduced(gate_own, gate_rest, F32)
    value, value_in = reduced(value_own, value_rest, BF16)

    share = depth // n_dp

    def spread(x):
        return jnp.concatenate(
            exchange(lambda j: lax.dynamic_slice_in_dim(x, j * share, share, 1), "dp")
        )

    def collect(x):
        return jnp.concatenate(exchange(lambda j: x, "dp"))

    normed_cells, grad_cells = spread(normed), collect(grad_rows)
    mixed_grad = after(mixed_grad, normed_cells, grad_cells)
    mixed, pair, kernel_rows = conv_block(
        row, value, value_in, gate, gate_in, mixed_grad, conv_kernel, frames
    )

    pair_blocks = [pair[k] for k in range(n_row)]
    first_in, second_in = [], []
    for s in shifts:
        order = rolled(pair_blocks, s)
        first_in.append([to_row(x, s) for x in order[1:]])
    for s in shifts:
        order = rolled(pair_blocks, s)
        second_in.append(to_row(after(order[0], *[x for y in first_in for x in y]), s))
    mixed_all = lax.all_gather(mixed, "col", axis=0)

    pair_kept = [after(x, *[y for z in first_in for y in z]) for x in pair_blocks]

    def wide(i, k):
        pieces = [pair_kept[k]] + [
            second_in[s - 1] if k == 0 else first_in[s - 1][k - 1] for s in shifts
        ]
        return jnp.concatenate(by_source([x[i] for x in pieces], "row"), axis=1)

    value_others = jnp.concatenate([wide(0, k) for k in range(1, n_row)])
    gate_others = jnp.concatenate([wide(1, k) for k in range(1, n_row)])
    part_others = back_block(value_others, gate_others, value_weight, gate_weight)
    part_in = []
    for s in shifts:
        k = n_row - 1 - s
        part_in.append(to_row(part_others[:, k * tokens : (k + 1) * tokens], s))
    second_in = [after(x, part_others) for x in second_in]
    value_mine, gate_mine = wide(0, 0), wide(1, 0)
    part_mine = back_block(value_mine, gate_mine, value_weight, gate_weight)
    def weight_grad(left, right):
        return lax.dot_general(left, right, CONTRACT_FIRST, preferred_element_type=F32)

    value_weight_grad = weight_grad(
        normed_cells, collect(jnp.concatenate([value_mine, value_others]))
    )

    mixed_all = after(mixed_all, value_weight_grad)

    def mixed_piece(j, k):
        return lax.dynamic_slice(
            mixed_all, (j * per_row, k * tokens, 0), (per_row, tokens, narrow)
        )

    mixed_out = [
        jnp.concatenate(
            [mixed_piece((row + s) % n_row, (k - s) % n_row) for k in range(n_row)], axis=1
        )
        for s in shifts
    ]
    part_in = [after(x, *mixed_out) for x in part_in]
    parts = placed([part_mine] + part_in)
    summed = lax.psum_scatter(
        parts.reshape(n_col * tokens, width), "col", scatter_dimension=0, tiled=True
    )

    mixed_in = [to_row(after(x, *part_in), s) for s, x in zip(shifts, mixed_out)]

    def side_by_side(x):
        return jnp.concatenate([x[p] for p in range(per_row)], axis=1)

    mixed_kept = side_by_side(lax.dynamic_slice_in_dim(mixed_all, row * per_row, per_row, 0))
    projected = dot(mixed_kept, mixer_of[0])

    gate_weight_grad = weight_grad(
        after(normed_cells, *part_in), collect(jnp.concatenate([gate_mine, gate_others]))
    )
    parts_wide = after(parts, gate_weight_grad).astype(F32)
    standard = (jnp.concatenate(gathered, axis=1).astype(F32) - mean) * inverse
    along = parts_wide * standard
    sums = jnp.stack([jnp.sum(parts_wide * gain_cols, (0, 2)), jnp.sum(along * gain_cols, (0, 2))])
    gain_sum = jnp.sum(along, 1)
    mixed_blocks = [mixed_kept]
    for s, piece in zip(shifts, mixed_in):
        mixed_blocks.append(side_by_side(after(piece, gate_weight_grad, projected)))
        projected = projected + dot(mixed_blocks[-1], mixer_of[s])
    sums = sum_over(sums, "col")
    gain_sum = sum_over(gain_sum, "dp")
    gain_pieces = exchange(
        lambda j: lax.dynamic_index_in_dim(gain_sum, j, 0, keepdims=False), "col"
    )
    gain_col = sum(gain_pieces[1:], gain_pieces[0])
    norm_gain_gradient = sum_over(after(gain_col, projected), "row")
    projected_blocks = [projected[k * tokens : (k + 1) * tokens] for k in range(n_row)]
    total = own.astype(F32) + projected_blocks[0]
    for s in shifts:
        total = total + to_row(projected_blocks[-s % n_row].astype(BF16), s).astype(F32)
    module_out = total.astype(BF16).reshape(features.shape)

    mixed_sources = by_source(mixed_blocks, "row")
    mixed_rows = jnp.concatenate(
        [
            mixed_sources[h][:, p * narrow : (p + 1) * narrow]
            for p in range(per_row)
            for h in range(n_row)
        ],
        axis=1,
    )
    mixer_weight_grad = weight_grad(spread(mixed_rows), grad_cells)

    kernel_sum = after(sum_over(after(kernel_rows, *part_in), "dp"), projected)
    kernel_grad = jnp.concatenate(by_source(exchange(lambda j: kernel_sum, "row"), "row"), axis=1)

    normed_grad = summed.astype(F32)
    own_standard = (own.astype(F32) - mean) * inverse
    gain_own = lax.dynamic_slice_in_dim(layer_norm_gain, col * width, width, 0)
    scaled = normed_grad * gain_own
    input_gradient = (
        own_grad.astype(F32)
        + (scaled - sums[0][:, None] / model - own_standard * (sums[1][:, None] / model)) * inverse
    )
    input_gradient = input_gradient.astype(BF16).reshape(features.shape)
    return (
        module_out,
        input_gradient,
        value_weight_grad,
        gate_weight_grad,
        mixer_weight_grad,
        kernel_grad,
        norm_gain_gradient,
    )


def solution(mesh):
    placed = (
        P(("groups", "dp"), "row", "col"),
        P(("groups", "dp"), "row", "col"),
        P("row", "col"),
        P("row", "col"),
        P("row", "col"),
        P(None, "col"),
        P(),
    )
    return jax.shard_map(
        shards,
        mesh=mesh,
        in_specs=placed,
        out_specs=(
            P(("groups", "dp"), "row", "col"),
            P(("groups", "dp"), "row", "col"),
            P(("groups", "row", "dp"), "col"),
            P(("groups", "row", "dp"), "col"),
            P(("groups", "row", "dp"), "col"),
            P("groups", "col"),
            P(("groups", "col")),
        ),
        check_vma=False,
    )
```

time: 401 us -> 344 us (0.86)
  waiting for transfers between devices: 183 us -> 118 us
  matrix products: 93.5 us -> 59.8 us
  Pallas kernels: 15.2 us -> 37.8 us
  local copies, waits for them, and re-layouts: 28.1 us -> 46.7 us
  other arithmetic: 34.6 us -> 27 us
  starting transfers between devices: 25.2 us -> 32.7 us
    ppermute x22 -> x15, waiting for transfers between devices: 142 us -> 6.12 us  [exchange(): lax.ppermute(pick((me + s) % count), axis, ring(count, s))]
    ppermute x3 -> x14, waiting for transfers between devices: 40.6 us -> 78.3 us  [to_row(): return lax.ppermute(x, 'row', ring(n_row, s))]
    dot_general x11 -> x10, matrix products: 59.5 us -> 31.1 us  [the longest x6 19.1 us: dot(): return jnp.dot(a, b, preferred_element_type=F32)]
    reduce_scatter x2, waiting for transfers between devices: 0.01 us -> 24.5 us  [the longest x1 24.5 us: shards(): lax.psum_scatter(mixed_parts.reshape(n_col * n_row * tokens, narrow), 'co...]
    pallas_call x1 -> x5, Pallas kernels: 15.2 us -> 37.8 us  [the longest x2 18.2 us: back_block(): pl.pallas_call(back_body, grid=(depth // tile,), in_specs=[left, left, ri...]
    ppermute x3 -> x14, starting transfers between devices: 4.64 us -> 19.6 us  [to_row(): return lax.ppermute(x, 'row', ring(n_row, s))]
    all_gather x2 -> x3, waiting for transfers between devices: 0.02 us -> 9.16 us  [the longest x2 7.09 us: shards(): lax.all_gather(own[i * part:(i + 1) * part], 'col', axis=0)]
    ppermute x22 -> x15, starting transfers between devices: 19.7 us -> 12.7 us  [exchange(): lax.ppermute(pick((me + s) % count), axis, ring(count, s))]
  transfers between devices with their start and end apart: 29 -> 34, of which waited for: 13 -> 17; matrix products, arithmetic and copies ran while one was open for 35% -> 34% of each run, Pallas kernels for 0% -> 6%
where the time goes in v2:
time: 344 us; the launch traced here: 337 us
  waiting for transfers between devices  118 us (34%)
  matrix products  59.8 us (17%)
  local copies, waits for them, and re-layouts  46.7 us (14%)
  Pallas kernels  37.8 us (11%)
  starting transfers between devices  32.7 us (10%)
  other arithmetic  27 us (8%)
  between operations  15.2 us (4%)
    ppermute x14, waiting for transfers between devices, to_row(): return lax.ppermute(x, 'row', ring(n_row, s))  78.3 us
    dot_general x3, matrix products, weight_grad(): lax.dot_general(left, right, CONTRACT_FIRST, preferred_element_type=F32)  28.7 us
    reduce_scatter x1, waiting for transfers between devices, shards(): lax.psum_scatter(mixed_parts.reshape(n_col * n_row * tokens, narrow), 'co...  24.5 us
    ppermute x14, starting transfers between devices, to_row(): return lax.ppermute(x, 'row', ring(n_row, s))  19.6 us
    dot_general x6, matrix products, dot(): return jnp.dot(a, b, preferred_element_type=F32)  19.1 us
    pallas_call x2, Pallas kernels, back_block(): pl.pallas_call(back_body, grid=(depth // tile,), in_specs=[left, left, ri...  18.2 us
    unnamed x108, local copies, waits for them, and re-layouts  17.1 us
    pallas_call x1, Pallas kernels, conv_block(): pl.pallas_call(functools.partial(conv_body, taps, frames, rows_in), grid_...  16.5 us
  transfers between devices with their start and end apart: 34, of which 17 were waited for; matrix products, arithmetic and copies ran while one was open for 34% of the time, Pallas kernels for 6%

profile of v2, /device:TPU:0, one launch (start us, length us, event | category | flops | bytes accessed | tf_op | source)
XLA Modules:
  0.0 337.3 jit_solution(9598849271531890130)
XLA Ops:
  9.3 3.0 collective-permute-start.6
  12.3 6.6 %constant_dynamic-slice_fusion.7 = (bf16[2,1,768,1536]{3,2,1,0:T(8,128)(2,1)S(1)}, bf16[2,1,768,1536]{3,2,1,0:T(8,128)(2,1)}) fusion(bf16[2,2,768,1536]{3,2,1,0:T(8,128)(2,1)} %bitcast.111, s32[]{:T(128)S(6)} %select_n.231, s32[]{:T(128)S(6)} %select_n.232), kind=kLoop, calls=%fused_computation.125 | loop fusion | bytes 18874376 | tf_op jit(solution)/shard_map/jit(dynamic_index_in_dim)/dynamic_slice | solution.py:303
  21.5 3.9 %fusion.28 = bf16[256,1536]{0,1:T(8,128)(2,1)S(1)} fusion(bf16[1536,1536]{1,0:T(8,128)(2,1)} %bitcast.119, bf16[1,256,1536]{2,1,0:T(8,128)(2,1)S(1)} %copy-done.21), kind=kOutput, calls=%fused_computation.41 | convolution fusion | flops 1208352768 | bytes 6291456 | tf_op jit(solution)/shard_map/dot_general | solution.py:56
  25.4 5.6 %collective-permute-done.6 = bf16[256,1536]{1,0:T(8,128)(2,1)} collective-permute-done((bf16[256,1536]{1,0:T(8,128)(2,1)}, bf16[256,1536]{1,0:T(8,128)(2,1)}, u32[]{:S(2)}, u32[]{:S(2)}) %collective-permute-start.6) | collective-permute-done | bytes 786464 | tf_op jit(solution)/shard_map/ppermute | solution.py:283
  36.8 4.0 %fusion.29 = bf16[256,1536]{0,1:T(8,128)(2,1)S(1)} fusion(bf16[1536,1536]{1,0:T(8,128)(2,1)} %bitcast.120, bf16[256,1536]{1,0:T(8,128)(2,1)} %collective-permute-done.6), kind=kOutput, calls=%fused_computation.42 | convolution fusion | flops 1208352768 | bytes 6291456 | tf_op jit(solution)/shard_map/dot_general | solution.py:56
  40.9 23.0 %collective-permute-done.7 = bf16[2,256,768]{1,2,0:T(8,128)(2,1)} collective-permute-done((bf16[2,256,768]{1,2,0:T(8,128)(2,1)S(1)}, bf16[2,256,768]{1,2,0:T(8,128)(2,1)}, u32[]{:S(2)}, u32[]{:S(2)}) %collective-permute-start.7) | collective-permute-done | bytes 786464 | tf_op jit(solution)/shard_map/ppermute | solution.py:283
  71.7 3.4 pad_maximum_fusion
  75.1 4.6 %copy.22 = bf16[4,512,768]{2,1,0:T(8,128)(2,1)} copy(bf16[4,512,768]{1,2,0:T(8,128)(2,1)} %pad_maximum_fusion) | data formatting | bytes 6291456 | tf_op jit(solution)/shard_map/concatenate | solution.py:322
  81.0 7.1 %all-gather.7.cloned.1.call-done.x_ref = bf16[4,128,1536]{2,1,0:T(8,128)(2,1)} async-done(((bf16[1,128,1536]{2,1,0:T(8,128)(2,1)}), bf16[4,128,1536]{2,1,0:T(8,128)(2,1)}) %all-gather.7.cloned.1.call-update) | async-done | bytes 1572880 | tf_op jit(solution)/shard_map/all_gather | solution.py:298
  95.5 6.1 %fusion.53.refs_4_ = f32[256,1536]{1,0:T(8,128)S(1)} fusion(bf16[256,3072]{1,0:T(8,128)(2,1)} %copy-done.34, bf16[3072,1536]{1,0:T(8,128)(2,1)} %gate_weight_ref.3), kind=kOutput, calls=%fused_computation.146 | convolution fusion | flops 2415919104 | bytes 12582912 | tf_op jit(solution)/shard_map/dot_general | solution.py:52
  102.3 2.6 fusion.51.refs_0_
  110.9 2.6 fusion.54.refs_5_
  116.6 2.6 fusion.52.refs_1_
  125.6 24.5 %reduce-scatter.3.cloned.1.call-done.refs_8_ = bf16[512,768]{1,0:T(8,128)(2,1)} async-done(((bf16[2048,768]{1,0:T(8,128)(2,1)}), bf16[512,768]{1,0:T(8,128)(2,1)}) %reduce-scatter.3.cloned.1.call-update) | async-done | bytes 786448 | tf_op jit(solution)/shard_map/reduce_scatter | solution.py:340
  150.1 10.3 %collective-permute-done.2.refs_2_ = bf16[256,768]{1,0:T(8,128)(2,1)S(1)} collective-permute-done((bf16[256,768]{1,0:T(8,128)(2,1)}, bf16[256,768]{1,0:T(8,128)(2,1)S(1)}, u32[]{:S(2)}, u32[]{:S(2)}) %collective-permute-start.2) | collective-permute-done | bytes 393248 | tf_op jit(solution)/shard_map/ppermute | solution.py:283
  160.4 8.0 %collective-permute-done.3.refs_3_ = bf16[256,768]{1,0:T(8,128)(2,1)S(1)} collective-permute-done((bf16[256,768]{1,0:T(8,128)(2,1)}, bf16[256,768]{1,0:T(8,128)(2,1)S(1)}, u32[]{:S(2)}, u32[]{:S(2)}) %collective-permute-start.3) | collective-permute-done | bytes 393248 | tf_op jit(solution)/shard_map/ppermute | solution.py:283
  169.2 16.5 %conv_block.1 = (bf16[512,768]{1,0:T(8,128)(2,1)}, bf16[2,2,256,768]{3,2,1,0:T(8,128)(2,1)}, f32[31,768]{1,0:T(8,128)}) custom-call(s32[1]{0:T(128)} %bitcast.1.row_ref, f32[256,1536]{1,0:T(8,128)} %copy-done.24, f32[256,1536]{1,0:T(8,128)} %copy-done.25, bf16[256,768]{1,0:T(8,128)(2,1)} %copy-done.32, bf16[256,768]{1,0:T(8,128)(2,1)} %copy-done.33, ...), custom_call_target="tpu_custom_call" | custom-call | flops 73138176 | bytes 7864320 | tf_op jit(solution)/shard_map/conv_block/pallas_call | solution.py:155
  192.5 14.8 %collective-permute-done.11 = bf16[2,256,768]{2,1,0:T(8,128)(2,1)} collective-permute-done((bf16[2,256,768]{2,1,0:T(8,128)(2,1)S(1)}, bf16[2,256,768]{2,1,0:T(8,128)(2,1)}, u32[]{:S(2)}, u32[]{:S(2)}) %collective-permute-start.11) | collective-permute-done | bytes 786464 | tf_op jit(solution)/shard_map/ppermute | solution.py:283
  210.4 3.9 %copy-done = bf16[3072,1536]{1,0:T(8,128)(2,1)S(1)} copy-done((bf16[3072,1536]{1,0:T(8,128)(2,1)S(1)}, bf16[3072,1536]{1,0:T(8,128)(2,1)}, u32[]{:S(2)}) %copy-start) | copy-done | bytes 9437208
  214.3 9.6 %back_block.2 = bf16[2,256,1536]{2,1,0:T(8,128)(2,1)S(1)} custom-call(bf16[256,1536]{1,0:T(8,128)(2,1)S(1)} %get-tuple-element.122.value_ref, bf16[256,1536]{1,0:T(8,128)(2,1)S(1)} %get-tuple-element.123.gate_ref, bf16[3072,1536]{1,0:T(8,128)(2,1)S(1)} %copy-done, bf16[3072,1536]{1,0:T(8,128)(2,1)} %gate_weight_ref.3), custom_call_target="tpu_custom_call" | custom-call | flops 4831838208 | bytes 22020096 | tf_op jit(solution)/shard_map/back_block/pallas_call | solution.py:205
  230.1 8.7 %back_block.3 = bf16[2,256,1536]{2,1,0:T(8,128)(2,1)S(1)} custom-call(bf16[256,1536]{1,0:T(8,128)(2,1)S(1)} %pad_maximum_fusion.13.value_ref, bf16[256,1536]{1,0:T(8,128)(2,1)S(1)} %pad_maximum_fusion.14.gate_ref, bf16[3072,1536]{1,0:T(8,128)(2,1)S(1)} %bitcast.105, bf16[3072,1536]{1,0:T(8,128)(2,1)} %gate_weight_ref.3), custom_call_target="tpu_custom_call" | custom-call | flops 4831838208 | bytes 22020096 | tf_op jit(solution)/shard_map/back_block/pallas_call | solution.py:205
  242.0 8.6 %fusion.2 = f32[1536,1536]{1,0:T(8,128)} fusion(bf16[512,1536]{1,0:T(8,128)(2,1)S(1)} %collective-permute-done.13, bf16[256,768]{1,0:T(8,128)(2,1)S(1)} %get-tuple-element.93, bf16[256,768]{1,0:T(8,128)(2,1)S(1)} %get-tuple-element.95, bf16[256,768]{1,0:T(8,128)(2,1)S(1)} %get-tuple-element.89, bf16[256,768]{1,0:T(8,128)(2,1)S(1)} %get-tuple-element.91, ...), kind=kOutput, calls=%fused_computation.9 | convolution fusion | flops 4853858304 | bytes 15728640 | tf_op jit(solution)/shard_map/dot_general | solution.py:415
  255.4 4.2 %collective-permute-done.14 = bf16[2,256,1536]{2,1,0:T(8,128)(2,1)} collective-permute-done((bf16[2,256,1536]{2,1,0:T(8,128)(2,1)S(1)}, bf16[2,256,1536]{2,1,0:T(8,128)(2,1)}, u32[]{:S(2)}, u32[]{:S(2)}) %collective-permute-start.14) | collective-permute-done | bytes 1572896 | tf_op jit(solution)/shard_map/ppermute | solution.py:283
  259.5 2.8 bitcast_dynamic-update-slice_fusion
  264.0 10.9 %fusion.12 = f32[1536,1536]{1,0:T(8,128)} fusion(bf16[1024,1536]{1,0:T(8,128)(2,1)} %pad_maximum_fusion.1, bf16[512,1536]{1,0:T(8,128)(2,1)} %collective-permute-done.16, bf16[256,768]{1,0:T(8,128)(2,1)S(1)} %copy-done.13, bf16[256,768]{1,0:T(8,128)(2,1)S(1)} %copy-done.11, bf16[256,768]{1,0:T(8,128)(2,1)S(1)} %copy-done.17, bf16[256,768]{1,0:T(8,128)(2,1)S(1)} %copy-done.15), kind=kOutput, calls=%fused_computation.19 | convolution fusion | flops 4847566848 | bytes 15728640 | tf_op jit(solution)/shard_map/dot_general | solution.py:415
  274.9 5.7 %fusion.1 = (f32[4,1536]{1,0:T(4,128)S(1)}, f32[256]{0:T(256)S(1)}, f32[256]{0:T(256)S(1)}) fusion(bf16[4,256,1536]{2,1,0:T(8,128)(2,1)} %bitcast.39, f32[256]{0:T(256)S(1)} %bitcast.135, f32[256]{0:T(256)S(1)} %bitcast.133, bf16[4,128,1536]{2,1,0:T(8,128)(2,1)S(1)} %copy-done.4, bf16[4,128,1536]{2,1,0:T(8,128)(2,1)S(1)} %copy-done.2, f32[4,1536]{1,0:T(4,128)S(1)} %mul.91), kind=kLoop, calls=%fused_computation.4 | loop fusion | flops 20440576 | bytes 6344704 | tf_op jit(solution)/shard_map/reduce_sum | solution.py:455
  290.4 2.9 collective-permute-start.27
  293.3 3.7 %collective-permute-done.15 = bf16[2,512,768]{2,1,0:T(8,128)(2,1)S(1)} collective-permute-done((bf16[2,512,768]{2,1,0:T(8,128)(2,1)S(1)}, bf16[2,512,768]{2,1,0:T(8,128)(2,1)S(1)}, u32[]{:S(2)}, u32[]{:S(2)}) %collective-permute-start.15) | collective-permute-done | bytes 1572896 | tf_op jit(solution)/shard_map/ppermute | solution.py:283
  309.3 2.9 collective-permute-done.23
  313.0 9.2 %fusion.22 = f32[1536,1536]{1,0:T(8,128)} fusion(bf16[512,1536]{1,0:T(8,128)(2,1)S(1)} %collective-permute-done.21, bf16[512,1536]{1,0:T(8,128)(2,1)S(1)} %get-tuple-element.70, bf16[512,1536]{1,0:T(8,128)(2,1)} %collective-permute-done.10, bf16[256,1536]{1,0:T(8,128)(2,1)} %collective-permute-done.6, bf16[256,1536]{1,0:T(8,128)(2,1)S(1)} %bitcast.128), kind=kOutput, calls=%fused_computation.31 | convolution fusion | flops 4847566848 | bytes 15728640 | tf_op jit(solution)/shard_map/dot_general | solution.py:415
  322.2 4.5 %collective-permute-done.17 = bf16[256,1536]{1,0:T(8,128)(2,1)S(1)} collective-permute-done((bf16[256,1536]{1,0:T(8,128)(2,1)S(1)}, bf16[256,1536]{1,0:T(8,128)(2,1)S(1)}, u32[]{:S(2)}, u32[]{:S(2)}) %collective-permute-start.17) | collective-permute-done | bytes 786464 | tf_op jit(solution)/shard_map/ppermute | solution.py:283
  326.7 3.6 %fusion.38 = (bf16[1,256,1536]{2,1,0:T(8,128)(2,1)}, bf16[1,256,1536]{2,1,0:T(8,128)(2,1)}) fusion(bf16[256,1536]{1,0:T(8,128)(2,1)} %reduce-scatter.5.cloned.1.call-done, bf16[1,256,1536]{2,1,0:T(8,128)(2,1)S(1)} %copy-done.20, f32[256]{0:T(256)S(1)} %bitcast.138, f32[256]{0:T(256)S(1)} %bitcast.136, f32[256]{0:T(256)S(1)} %bitcast.134, ...), kind=kLoop, calls=%fused_computation.67 | loop fusion | flops 6291456 | bytes 6301696 | tf_op jit(solution)/shard_map/reshape | solution.py:495
  (234 shorter events, 91.8 us)
Async XLA Ops:
  7.2 59.8 %all-gather.5.cloned.1.call-start = ((), (), s32[]{:S(2)}) async-start(), calls=%async_computation.2 | async-start | bytes 1966080 | tf_op jit(solution)/shard_map/all_gather | solution.py:298
  9.3 78.8 %all-gather.7.cloned.1.call-start = ((), (), s32[]{:S(2)}) async-start(), calls=%async_computation.3 | async-start | bytes 1966080 | tf_op jit(solution)/shard_map/all_gather | solution.py:298
  9.3 21.7 %collective-permute-start.6 = (bf16[256,1536]{1,0:T(8,128)(2,1)}, bf16[256,1536]{1,0:T(8,128)(2,1)}, u32[]{:S(2)}, u32[]{:S(2)}) collective-permute-start(bf16[256,1536]{1,0:T(8,128)(2,1)} %bitcast.126), channel_id=1, source_target_pairs={{0,8},{8,0},{1,9},{9,1},{2,10},{10,2},{3,11},{11,3},{4,12},{12,4},... | collective-permute-start | bytes 2359304 | tf_op jit(solution)/shard_map/ppermute | solution.py:283
  21.3 43.8 %collective-permute-start.8 = (bf16[2,256,768]{1,2,0:T(8,128)(2,1)S(1)}, bf16[2,256,768]{1,2,0:T(8,128)(2,1)S(1)}, u32[]{:S(2)}, u32[]{:S(2)}) collective-permute-start(bf16[2,256,768]{1,2,0:T(8,128)(2,1)S(1)} %pad_maximum_fusion.10), channel_id=1, source_target_pairs={{0,8},{8,0},{1,9},{9,1},{2,10},{10,2},{3,11},{11,3},{4,12},{12,4},... | collective-permute-start | bytes 2359304 | tf_op jit(solution)/shard_map/ppermute | solution.py:283
  21.5 128.7 %reduce-scatter.3.cloned.1.call-start = ((), (), s32[]{:S(2)}) async-start(), calls=%async_computation.4 | async-start | bytes 3932160 | tf_op jit(solution)/shard_map/reduce_scatter | solution.py:340
  33.7 30.2 %collective-permute-start.7 = (bf16[2,256,768]{1,2,0:T(8,128)(2,1)S(1)}, bf16[2,256,768]{1,2,0:T(8,128)(2,1)}, u32[]{:S(2)}, u32[]{:S(2)}) collective-permute-start(bf16[2,256,768]{1,2,0:T(8,128)(2,1)S(1)} %pad_maximum_fusion.9), channel_id=1, source_target_pairs={{0,8},{8,0},{1,9},{9,1},{2,10},{10,2},{3,11},{11,3},{4,12},{12,4},... | collective-permute-start | bytes 2359304 | tf_op jit(solution)/shard_map/ppermute | solution.py:283
  69.9 18.9 %collective-permute-start = (bf16[128,3072]{1,0:T(8,128)(2,1)S(1)}, bf16[128,3072]{1,0:T(8,128)(2,1)}, u32[]{:S(2)}, u32[]{:S(2)}) collective-permute-start(bf16[128,3072]{1,0:T(8,128)(2,1)S(1)} %get-tuple-element.35), channel_id=1, source_target_pairs={{0,8},{8,0},{1,9},{9,1},{2,10},{10,2},{3,11},{11,3},{4,12},{12,4},... | collective-permute-start | bytes 2359304 | tf_op jit(solution)/shard_map/ppermute | solution.py:283
  79.8 172.9 %all-gather.9.cloned.1.call-start = ((), (), s32[]{:S(2)}) async-start(), calls=%async_computation.6 | async-start | bytes 3932160 | tf_op jit(solution)/shard_map/all_gather | solution.py:394
  91.8 18.5 %collective-permute-start.1 = (bf16[128,3072]{1,0:T(8,128)(2,1)S(1)}, bf16[128,3072]{1,0:T(8,128)(2,1)S(1)}, u32[]{:S(2)}, u32[]{:S(2)}) collective-permute-start(bf16[128,3072]{1,0:T(8,128)(2,1)S(1)} %get-tuple-element.38), channel_id=1, source_target_pairs={{0,8},{8,0},{1,9},{9,1},{2,10},{10,2},{3,11},{11,3},{4,12},{12,4},... | collective-permute-start | bytes 2359304 | tf_op jit(solution)/shard_map/ppermute | solution.py:283
  110.8 11.7 %collective-permute-start.9 = (bf16[512,1536]{1,0:T(8,128)(2,1)S(1)}, bf16[512,1536]{1,0:T(8,128)(2,1)S(1)}, u32[]{:S(2)}, u32[]{:S(2)}) collective-permute-start(bf16[512,1536]{1,0:T(8,128)(2,1)S(1)} %get-tuple-element.79), channel_id=1, source_target_pairs={{0,1},{1,0},{2,3},{3,2},{4,5},{5,4},{6,7},{7,6},{8,9},{9,8},{10,11... | collective-permute-start | bytes 4718600 | tf_op jit(solution)/shard_map/ppermute | solution.py:43
  114.6 53.8 %collective-permute-start.4 = (f32[256,768]{1,0:T(8,128)}, f32[256,768]{1,0:T(8,128)}, u32[]{:S(2)}, u32[]{:S(2)}) collective-permute-start(f32[256,768]{1,0:T(8,128)} %constant_dynamic-slice_fusion.9), channel_id=1, source_target_pairs={{0,8},{8,0},{1,9},{9,1},{2,10},{10,2},{3,11},{11,3},{4,12},{12,4},... | collective-permute-start | bytes 2359304 | tf_op jit(solution)/shard_map/ppermute | solution.py:283
  116.0 52.4 %collective-permute-start.5 = (f32[256,768]{1,0:T(8,128)}, f32[256,768]{1,0:T(8,128)}, u32[]{:S(2)}, u32[]{:S(2)}) collective-permute-start(f32[256,768]{1,0:T(8,128)} %constant_dynamic-slice_fusion.8), channel_id=1, source_target_pairs={{0,8},{8,0},{1,9},{9,1},{2,10},{10,2},{3,11},{11,3},{4,12},{12,4},... | collective-permute-start | bytes 2359304 | tf_op jit(solution)/shard_map/ppermute | solution.py:283
  120.5 39.9 %collective-permute-start.2 = (bf16[256,768]{1,0:T(8,128)(2,1)}, bf16[256,768]{1,0:T(8,128)(2,1)S(1)}, u32[]{:S(2)}, u32[]{:S(2)}) collective-permute-start(bf16[256,768]{1,0:T(8,128)(2,1)} %dynamic-slice_convert_fusion.1), channel_id=1, source_target_pairs={{0,8},{8,0},{1,9},{9,1},{2,10},{10,2},{3,11},{11,3},{4,12},{12,4},... | collective-permute-start | bytes 1179656 | tf_op jit(solution)/shard_map/ppermute | solution.py:283
  122.0 46.4 %collective-permute-start.3 = (bf16[256,768]{1,0:T(8,128)(2,1)}, bf16[256,768]{1,0:T(8,128)(2,1)S(1)}, u32[]{:S(2)}, u32[]{:S(2)}) collective-permute-start(bf16[256,768]{1,0:T(8,128)(2,1)} %dynamic-slice_convert_fusion), channel_id=1, source_target_pairs={{0,8},{8,0},{1,9},{9,1},{2,10},{10,2},{3,11},{11,3},{4,12},{12,4},... | collective-permute-start | bytes 1179656 | tf_op jit(solution)/shard_map/ppermute | solution.py:283
  188.1 19.2 %collective-permute-start.11 = (bf16[2,256,768]{2,1,0:T(8,128)(2,1)S(1)}, bf16[2,256,768]{2,1,0:T(8,128)(2,1)}, u32[]{:S(2)}, u32[]{:S(2)}) collective-permute-start(bf16[2,256,768]{2,1,0:T(8,128)(2,1)S(1)} %get-tuple-element.46), channel_id=1, source_target_pairs={{0,8},{8,0},{1,9},{9,1},{2,10},{10,2},{3,11},{11,3},{4,12},{12,4},... | collective-permute-start | bytes 2359304 | tf_op jit(solution)/shard_map/ppermute | solution.py:283
  189.7 137.1 %reduce-scatter.5.cloned.1.call-start = ((), (), s32[]{:S(2)}) async-start(), calls=%async_computation.5 | async-start | bytes 3932160 | tf_op jit(solution)/shard_map/reduce_scatter | solution.py:436
  192.1 120.8 %collective-permute-start.10 = (bf16[512,1536]{1,0:T(8,128)(2,1)}, bf16[512,1536]{1,0:T(8,128)(2,1)}, u32[]{:S(2)}, u32[]{:S(2)}) collective-permute-start(bf16[512,1536]{1,0:T(8,128)(2,1)} %pad_maximum_fusion.5), channel_id=1, source_target_pairs={{0,1},{1,0},{2,3},{3,2},{4,5},{5,4},{6,7},{7,6},{8,9},{9,8},{10,11... | collective-permute-start | bytes 4718600 | tf_op jit(solution)/shard_map/ppermute | solution.py:43
  207.3 19.2 %collective-permute-start.12 = (bf16[2,256,768]{2,1,0:T(8,128)(2,1)}, bf16[2,256,768]{2,1,0:T(8,128)(2,1)}, u32[]{:S(2)}, u32[]{:S(2)}) collective-permute-start(bf16[2,256,768]{2,1,0:T(8,128)(2,1)} %get-tuple-element.44), channel_id=1, source_target_pairs={{0,8},{8,0},{1,9},{9,1},{2,10},{10,2},{3,11},{11,3},{4,12},{12,4},... | collective-permute-start | bytes 2359304 | tf_op jit(solution)/shard_map/ppermute | solution.py:283
  223.8 35.7 %collective-permute-start.14 = (bf16[2,256,1536]{2,1,0:T(8,128)(2,1)S(1)}, bf16[2,256,1536]{2,1,0:T(8,128)(2,1)}, u32[]{:S(2)}, u32[]{:S(2)}) collective-permute-start(bf16[2,256,1536]{2,1,0:T(8,128)(2,1)S(1)} %back_block.2), channel_id=1, source_target_pairs={{0,8},{8,0},{1,9},{9,1},{2,10},{10,2},{3,11},{11,3},{4,12},{12,4},... | collective-permute-start | bytes 4718600 | tf_op jit(solution)/shard_map/ppermute | solution.py:283
  228.1 13.9 %collective-permute-start.13 = (bf16[512,1536]{1,0:T(8,128)(2,1)S(1)}, bf16[512,1536]{1,0:T(8,128)(2,1)S(1)}, u32[]{:S(2)}, u32[]{:S(2)}) collective-permute-start(bf16[512,1536]{1,0:T(8,128)(2,1)S(1)} %maximum_maximum_fusion.1), channel_id=1, source_target_pairs={{0,1},{1,0},{2,3},{3,2},{4,5},{5,4},{6,7},{7,6},{8,9},{9,8},{10,11... | collective-permute-start | bytes 4718600 | tf_op jit(solution)/shard_map/ppermute | solution.py:43
  229.4 34.5 %collective-permute-start.16 = (bf16[512,1536]{1,0:T(8,128)(2,1)}, bf16[512,1536]{1,0:T(8,128)(2,1)}, u32[]{:S(2)}, u32[]{:S(2)}) collective-permute-start(bf16[512,1536]{1,0:T(8,128)(2,1)} %maximum_maximum_fusion.2), channel_id=1, source_target_pairs={{0,1},{1,0},{2,3},{3,2},{4,5},{5,4},{6,7},{7,6},{8,9},{9,8},{10,11... | collective-permute-start | bytes 4718600 | tf_op jit(solution)/shard_map/ppermute | solution.py:43
  262.4 34.7 %collective-permute-start.15 = (bf16[2,512,768]{2,1,0:T(8,128)(2,1)S(1)}, bf16[2,512,768]{2,1,0:T(8,128)(2,1)S(1)}, u32[]{:S(2)}, u32[]{:S(2)}) collective-permute-start(bf16[2,512,768]{2,1,0:T(8,128)(2,1)S(1)} %copy-done.27), channel_id=1, source_target_pairs={{0,8},{8,0},{1,9},{9,1},{2,10},{10,2},{3,11},{11,3},{4,12},{12,4},... | collective-permute-start | bytes 4718600 | tf_op jit(solution)/shard_map/ppermute | solution.py:283
  280.6 6.7 %collective-permute-start.19 = (f32[2,256]{1,0:T(2,128)S(1)}, f32[2,256]{1,0:T(2,128)S(1)}, u32[]{:S(2)}, u32[]{:S(2)}) collective-permute-start(f32[2,256]{1,0:T(2,128)S(1)} %pad_maximum_fusion.18), channel_id=1, source_target_pairs={{0,4},{2,6},{4,0},{6,2},{1,5},{3,7},{5,1},{7,3},{8,12},{10,14},{12... | collective-permute-start | bytes 6152 | tf_op jit(solution)/shard_map/ppermute | solution.py:43
  282.2 5.1 %collective-permute-start.20 = (f32[2,256]{1,0:T(2,128)S(1)}, f32[2,256]{1,0:T(2,128)S(1)}, u32[]{:S(2)}, u32[]{:S(2)}) collective-permute-start(f32[2,256]{1,0:T(2,128)S(1)} %pad_maximum_fusion.18), channel_id=1, source_target_pairs={{0,6},{2,0},{4,2},{6,4},{1,7},{3,1},{5,3},{7,5},{8,14},{10,8},{12,... | collective-permute-start | bytes 6152 | tf_op jit(solution)/shard_map/ppermute | solution.py:43
  283.6 5.7 %collective-permute-start.18 = (f32[2,256]{1,0:T(2,128)S(1)}, f32[2,256]{1,0:T(2,128)S(1)}, u32[]{:S(2)}, u32[]{:S(2)}) collective-permute-start(f32[2,256]{1,0:T(2,128)S(1)} %pad_maximum_fusion.18), channel_id=1, source_target_pairs={{0,2},{2,4},{4,6},{6,0},{1,3},{3,5},{5,7},{7,1},{8,10},{10,12},{12... | collective-permute-start | bytes 6152 | tf_op jit(solution)/shard_map/ppermute | solution.py:43
  287.3 14.8 %collective-permute-start.22 = (f32[31,768]{1,0:T(8,128)S(1)}, f32[31,768]{1,0:T(8,128)S(1)}, u32[]{:S(2)}, u32[]{:S(2)}) collective-permute-start(f32[31,768]{1,0:T(8,128)S(1)} %copy-done.36), channel_id=1, source_target_pairs={{0,1},{1,0},{2,3},{3,2},{4,5},{5,4},{6,7},{7,6},{8,9},{9,8},{10,11... | collective-permute-start | bytes 285704 | tf_op jit(solution)/shard_map/ppermute | solution.py:43
  289.4 10.8 %collective-permute-start.25 = (f32[1536]{0:T(1024)S(1)}, f32[1536]{0:T(1024)S(1)}, u32[]{:S(2)}, u32[]{:S(2)}) collective-permute-start(f32[1536]{0:T(1024)S(1)} %get-tuple-element.64), channel_id=1, source_target_pairs={{0,2},{2,4},{4,6},{6,0},{1,3},{3,5},{5,7},{7,1},{8,10},{10,12},{12... | collective-permute-start | bytes 18440 | tf_op jit(solution)/shard_map/ppermute | solution.py:43
  290.4 9.9 %collective-permute-start.27 = (f32[1536]{0:T(1024)S(1)}, f32[1536]{0:T(1024)S(1)}, u32[]{:S(2)}, u32[]{:S(2)}) collective-permute-start(f32[1536]{0:T(1024)S(1)} %get-tuple-element.65), channel_id=1, source_target_pairs={{0,6},{2,0},{4,2},{6,4},{1,7},{3,1},{5,3},{7,5},{8,14},{10,8},{12,... | collective-permute-start | bytes 18440 | tf_op jit(solution)/shard_map/ppermute | solution.py:43
  297.1 5.0 %collective-permute-start.26 = (f32[1536]{0:T(1024)S(1)}, f32[1536]{0:T(1024)S(1)}, u32[]{:S(2)}, u32[]{:S(2)}) collective-permute-start(f32[1536]{0:T(1024)S(1)} %get-tuple-element.66), channel_id=1, source_target_pairs={{0,4},{2,6},{4,0},{6,2},{1,5},{3,7},{5,1},{7,3},{8,12},{10,14},{12... | collective-permute-start | bytes 18440 | tf_op jit(solution)/shard_map/ppermute | solution.py:43
  300.3 12.7 %collective-permute-start.21 = (bf16[512,1536]{1,0:T(8,128)(2,1)S(1)}, bf16[512,1536]{1,0:T(8,128)(2,1)S(1)}, u32[]{:S(2)}, u32[]{:S(2)}) collective-permute-start(bf16[512,1536]{1,0:T(8,128)(2,1)S(1)} %get-tuple-element.71), channel_id=1, source_target_pairs={{0,1},{1,0},{2,3},{3,2},{4,5},{5,4},{6,7},{7,6},{8,9},{9,8},{10,11... | collective-permute-start | bytes 4718600 | tf_op jit(solution)/shard_map/ppermute | solution.py:43
  306.5 5.7 %collective-permute-start.23 = (f32[31,768]{1,0:T(8,128)S(1)}, f32[31,768]{1,0:T(8,128)S(1)}, u32[]{:S(2)}, u32[]{:S(2)}) collective-permute-start(f32[31,768]{1,0:T(8,128)S(1)} %add.177), channel_id=1, source_target_pairs={{0,8},{8,0},{1,9},{9,1},{2,10},{10,2},{3,11},{11,3},{4,12},{12,4},... | collective-permute-start | bytes 285704 | tf_op jit(solution)/shard_map/ppermute | solution.py:43
  306.9 19.8 %collective-permute-start.17 = (bf16[256,1536]{1,0:T(8,128)(2,1)S(1)}, bf16[256,1536]{1,0:T(8,128)(2,1)S(1)}, u32[]{:S(2)}, u32[]{:S(2)}) collective-permute-start(bf16[256,1536]{1,0:T(8,128)(2,1)S(1)} %slice.183), channel_id=1, source_target_pairs={{0,8},{8,0},{1,9},{9,1},{2,10},{10,2},{3,11},{11,3},{4,12},{12,4},... | collective-permute-start | bytes 2359304 | tf_op jit(solution)/shard_map/ppermute | solution.py:283
  (54 other events, 432.6 us)
Sparse Core Ops, SparseCore 0:
  10.1 39.7 all-gather.4
  52.1 35.9 all-gather.6
  91.0 59.1 reduce-scatter.2
  189.8 62.8 all-gather.8
  262.5 60.9 reduce-scatter.4

commit v3 on v2

--- a/solution.py
+++ b/solution.py
@@ -16,6 +16,7 @@
 CONV_VMEM = 56 << 20
 NORM_ROWS = 32
 BACK_TILE = 512
+HALVES = 2
 BACK_VMEM = 40 << 20
 NORM_VMEM = 24 << 20
 PARTS = 2
@@ -61,10 +62,11 @@
     return sum(pieces[1:], pieces[0])
 
 
-def conv_body(taps, frames, rows_in, row_ref, *refs):
+def conv_body(taps, frames, rows_in, carried, row_ref, *refs):
     parts = [refs[i * rows_in : (i + 1) * rows_in] for i in range(4)]
-    grad_ref, kernel_ref, mixed_ref, pair_ref, taps_ref = refs[4 * rows_in : 4 * rows_in + 5]
-    glu_pad, grad_pad, partial, value_sum, gate_sum = refs[4 * rows_in + 5 :]
+    grad_ref, kernel_ref = refs[4 * rows_in : 4 * rows_in + 2]
+    mixed_ref, pair_ref, taps_ref, *scratch = refs[4 * rows_in + 2 + carried :]
+    glu_pad, grad_pad, partial, value_sum, gate_sum = scratch
     half = taps // 2
     span = frames * rows_in
     lead = 16
@@ -133,12 +135,16 @@
         taps_ref[pl.ds(tap, 1)] = jnp.sum(partial[pl.ds(8 * tap, 8)], 0, keepdims=True)
 
 
-def conv_block(row, values, values_in, gates, gates_in, mixed_grad, conv_kernel, frames):
+def conv_block(
+    row, values, values_in, gates, gates_in, mixed_grad, conv_kernel, frames, count, which, before
+):
     rows_in = len(values)
-    span, narrow = mixed_grad.shape
+    span, whole = mixed_grad.shape
+    narrow = whole // count
     taps = conv_kernel.shape[0]
     lanes = 128 if narrow % 128 == 0 else narrow
     steps = narrow // lanes
+    first = which * steps
     if lanes == narrow:
         values, gates, (conv_kernel,) = (
             [lax.dynamic_slice_in_dim(x, row * narrow, narrow, 1) for x in xs]
@@ -146,14 +152,14 @@
         )
 
     def at(j, row):
-        return (0, j) if lanes == narrow else (0, row[0] * steps + j)
+        return (0, j) if lanes == narrow else (0, row[0] * (count * steps) + (first + j))
 
     inner = pl.BlockSpec((frames, lanes), lambda j, row: (0, j))
     outer = pl.BlockSpec((frames, lanes), at)
-    tall = pl.BlockSpec((span, lanes), lambda j, row: (0, j))
+    tall = pl.BlockSpec((span, lanes), lambda j, row: (0, first + j))
     work = span * narrow
     return pl.pallas_call(
-        functools.partial(conv_body, taps, frames, rows_in),
+        functools.partial(conv_body, taps, frames, rows_in, len(before)),
         grid_spec=pltpu.PrefetchScalarGridSpec(
             num_scalar_prefetch=1,
             grid=(steps,),
@@ -161,11 +167,12 @@
             + [inner] * rows_in
             + [outer] * rows_in
             + [inner] * rows_in
-            + [tall, pl.BlockSpec((taps, lanes), at)],
+            + [tall, pl.BlockSpec((taps, lanes), at)]
+            + [pl.BlockSpec(memory_space=pl.ANY)] * len(before),
             out_specs=[
                 tall,
-                pl.BlockSpec((rows_in, 2, frames, lanes), lambda j, row: (0, 0, 0, j)),
-                pl.BlockSpec((taps, lanes), lambda j, row: (0, j)),
+                pl.BlockSpec((rows_in, 2, frames, lanes), lambda j, row: (0, 0, 0, first + j)),
+                pl.BlockSpec((taps, lanes), lambda j, row: (0, first + j)),
             ],
             scratch_shapes=[
                 pltpu.VMEM((span + 32, lanes), F32),
@@ -176,16 +183,17 @@
             ],
         ),
         out_shape=[
-            jax.ShapeDtypeStruct((span, narrow), BF16),
-            jax.ShapeDtypeStruct((rows_in, 2, frames, narrow), BF16),
-            jax.ShapeDtypeStruct((taps, narrow), F32),
+            jax.ShapeDtypeStruct((span, whole), BF16),
+            jax.ShapeDtypeStruct((rows_in, 2, frames, whole), BF16),
+            jax.ShapeDtypeStruct((taps, whole), F32),
         ],
+        input_output_aliases={4 * rows_in + 3 + i: i for i in range(len(before))},
         compiler_params=pltpu.CompilerParams(vmem_limit_bytes=CONV_VMEM),
         cost_estimate=pl.CostEstimate(
             flops=6 * taps * work, bytes_accessed=20 * work, transcendentals=3 * work
         ),
         name="conv_block",
-    )(row.reshape(1), *values, *values_in, *gates, *gates_in, mixed_grad, conv_kernel)
+    )(row.reshape(1), *values, *values_in, *gates, *gates_in, mixed_grad, conv_kernel, *before)
 
 
 def back_body(value_ref, gate_ref, value_weight_ref, gate_weight_ref, out_ref):
@@ -344,28 +352,36 @@
         tiled=True,
     )
 
-    def columns(x, i):
-        return lax.dynamic_slice_in_dim(x, i * narrow, narrow, 1)
-
+    count = HALVES if narrow % (HALVES * 128) == 0 else 1
+    piece = narrow // count
     gate_own, value_own = dot(normed_own, gate_weight), dot(normed_own, value_weight)
     rest = jnp.concatenate(normed_in)
     gate_rest, value_rest = dot(rest, gate_weight), dot(rest, value_weight)
 
-    def reduced(first, others, dtype):
-        blocks = [first] + [others[k * tokens : (k + 1) * tokens] for k in range(n_row - 1)]
+    def blocks_of(first, others):
+        return [first] + [others[k * tokens : (k + 1) * tokens] for k in range(n_row - 1)]
+
+    def reduced(blocks, q, dtype, *others):
         total = None
         for s in shifts:
-            sent = [columns(x, (row + s) % n_row).astype(dtype) for x in blocks]
-            sent[0] = after(sent[0], *crossed[-1])
+            start = ((row + s) % n_row) * narrow + q * piece
+            sent = [
+                after(lax.dynamic_slice_in_dim(x, start, piece, 1).astype(dtype), *others)
+                for x in blocks
+            ]
             arrived = [to_row(sent[(k - s) % n_row], s) for k in range(n_row)]
             if total is None:
                 total = arrived
             else:
                 total = [t.astype(F32) + x.astype(F32) for t, x in zip(total, arrived)]
-        return blocks, total
-
-    gate, gate_in = reduced(gate_own, gate_rest, F32)
-    value, value_in = reduced(value_own, value_rest, BF16)
+        return total
+
+    gate, value = blocks_of(gate_own, gate_rest), blocks_of(value_own, value_rest)
+    gate_in, value_in = [], []
+    for q in range(count):
+        before = gate_in[-1] + value_in[-1] if q else []
+        gate_in.append(reduced(gate, q, F32, *before))
+        value_in.append(reduced(value, q, BF16, *before))
 
     share = depth // n_dp
 
@@ -379,9 +395,13 @@
 
     normed_cells, grad_cells = spread(normed), collect(grad_rows)
     mixed_grad = after(mixed_grad, normed_cells, grad_cells)
-    mixed, pair, kernel_rows = conv_block(
-        row, value, value_in, gate, gate_in, mixed_grad, conv_kernel, frames
-    )
+    done = []
+    for q in range(count):
+        here = [[after(x, *done) for x in y[q]] for y in (value_in, gate_in)]
+        done = conv_block(
+            row, value, here[0], gate, here[1], mixed_grad, conv_kernel, frames, count, q, done
+        )
+    mixed, pair, kernel_rows = done
 
     pair_blocks = [pair[k] for k in range(n_row)]
     first_in, second_in = [], []

time: 344 us -> 326 us (0.948)
  waiting for transfers between devices: 118 us -> 98.7 us
  starting transfers between devices: 32.7 us -> 37.9 us
  local copies, waits for them, and re-layouts: 46.7 us -> 43 us
    reduce_scatter x1, waiting for transfers between devices: 24.5 us -> 7.27 us  [shards(): lax.psum_scatter(mixed_parts.reshape(n_col * n_row * tokens, narrow), 'co...]
    unnamed x108 -> x100, local copies, waits for them, and re-layouts: 17.1 us -> 12.5 us
    ppermute x14 -> x18, starting transfers between devices: 19.6 us -> 23.7 us  [to_row(): return lax.ppermute(x, 'row', ring(n_row, s))]
    ppermute x14 -> x18, waiting for transfers between devices: 78.3 us -> 74.7 us  [to_row(): return lax.ppermute(x, 'row', ring(n_row, s))]
    pallas_call x1 -> x2, Pallas kernels: 16.5 us -> 18.5 us  [conv_block(): pl.pallas_call(functools.partial(conv_body, taps, frames, rows_in, len(be...]
  transfers between devices with their start and end apart: 34 -> 38, of which waited for: 17 -> 18; matrix products, arithmetic and copies ran while one was open for 34% -> 35% of each run, Pallas kernels for 6% -> 10%
where the time goes in v3:
time: 326 us; the launch traced here: 320 us
  waiting for transfers between devices  98.7 us (30%)
  matrix products  58.6 us (18%)
  local copies, waits for them, and re-layouts  43 us (13%)
  Pallas kernels  39.9 us (12%)
  starting transfers between devices  37.9 us (12%)
  other arithmetic  26.5 us (8%)
  between operations  15.1 us (5%)
    ppermute x18, waiting for transfers between devices, to_row(): return lax.ppermute(x, 'row', ring(n_row, s))  74.7 us
    dot_general x3, matrix products, weight_grad(): lax.dot_general(left, right, CONTRACT_FIRST, preferred_element_type=F32)  28.5 us
    ppermute x18, starting transfers between devices, to_row(): return lax.ppermute(x, 'row', ring(n_row, s))  23.7 us
    dot_general x6, matrix products, dot(): return jnp.dot(a, b, preferred_element_type=F32)  19.4 us
    pallas_call x2, Pallas kernels, conv_block(): pl.pallas_call(functools.partial(conv_body, taps, frames, rows_in, len(be...  18.5 us
    pallas_call x2, Pallas kernels, back_block(): pl.pallas_call(back_body, grid=(depth // tile,), in_specs=[left, left, ri...  18.2 us
    ppermute x15, starting transfers between devices, exchange(): lax.ppermute(pick((me + s) % count), axis, ring(count, s))  13.9 us
    unnamed x100, local copies, waits for them, and re-layouts  12.5 us
  transfers between devices with their start and end apart: 38, of which 18 were waited for; matrix products, arithmetic and copies ran while one was open for 35% of the time, Pallas kernels for 10%

profile of v3, /device:TPU:0, one launch (start us, length us, event | category | flops | bytes accessed | tf_op | source)
XLA Modules:
  0.0 319.7 jit_solution(6621003888777079385)
XLA Ops:
  9.3 3.0 collective-permute-start.7
  12.3 6.6 %constant_dynamic-slice_fusion.9 = (bf16[2,1,768,1536]{3,2,1,0:T(8,128)(2,1)S(1)}, bf16[2,1,768,1536]{3,2,1,0:T(8,128)(2,1)}) fusion(bf16[2,2,768,1536]{3,2,1,0:T(8,128)(2,1)} %bitcast.111, s32[]{:T(128)S(6)} %select_n.238, s32[]{:T(128)S(6)} %select_n.239), kind=kLoop, calls=%fused_computation.129 | loop fusion | bytes 18874376 | tf_op jit(solution)/shard_map/jit(dynamic_index_in_dim)/dynamic_slice | solution.py:311
  22.3 3.9 %fusion.28 = bf16[256,1536]{0,1:T(8,128)(2,1)S(1)} fusion(bf16[1536,1536]{1,0:T(8,128)(2,1)} %bitcast.119, bf16[1,256,1536]{2,1,0:T(8,128)(2,1)S(1)} %copy-done.17), kind=kOutput, calls=%fused_computation.41 | convolution fusion | flops 1208352768 | bytes 6291456 | tf_op jit(solution)/shard_map/dot_general | solution.py:57
  26.2 4.7 %collective-permute-done.7 = bf16[256,1536]{1,0:T(8,128)(2,1)S(1)} collective-permute-done((bf16[256,1536]{1,0:T(8,128)(2,1)}, bf16[256,1536]{1,0:T(8,128)(2,1)S(1)}, u32[]{:S(2)}, u32[]{:S(2)}) %collective-permute-start.7) | collective-permute-done | bytes 786464 | tf_op jit(solution)/shard_map/ppermute | solution.py:291
  35.6 3.8 %fusion.29 = bf16[256,1536]{0,1:T(8,128)(2,1)S(1)} fusion(bf16[1536,1536]{1,0:T(8,128)(2,1)} %bitcast.120, bf16[256,1536]{1,0:T(8,128)(2,1)S(1)} %collective-permute-done.7), kind=kOutput, calls=%fused_computation.42 | convolution fusion | flops 1208352768 | bytes 6291456 | tf_op jit(solution)/shard_map/dot_general | solution.py:57
  40.4 23.4 %collective-permute-done.8 = bf16[2,256,768]{1,2,0:T(8,128)(2,1)S(1)} collective-permute-done((bf16[2,256,768]{1,2,0:T(8,128)(2,1)S(1)}, bf16[2,256,768]{1,2,0:T(8,128)(2,1)S(1)}, u32[]{:S(2)}, u32[]{:S(2)}) %collective-permute-start.8) | collective-permute-done | bytes 786464 | tf_op jit(solution)/shard_map/ppermute | solution.py:291
  73.9 4.6 %copy.25 = bf16[4,512,768]{2,1,0:T(8,128)(2,1)} copy(bf16[4,512,768]{1,2,0:T(8,128)(2,1)} %pad_maximum_fusion) | data formatting | bytes 6291456 | tf_op jit(solution)/shard_map/concatenate | solution.py:330
  79.8 8.3 %all-gather.7.cloned.1.call-done.x_ref = bf16[4,128,1536]{2,1,0:T(8,128)(2,1)} async-done(((bf16[1,128,1536]{2,1,0:T(8,128)(2,1)}), bf16[4,128,1536]{2,1,0:T(8,128)(2,1)}) %all-gather.7.cloned.1.call-update) | async-done | bytes 1572880 | tf_op jit(solution)/shard_map/all_gather | solution.py:306
  93.6 6.4 %fusion.54.refs_4_ = f32[256,1536]{1,0:T(8,128)S(1)} fusion(bf16[256,3072]{1,0:T(8,128)(2,1)S(1)} %get-tuple-element.131, bf16[3072,1536]{1,0:T(8,128)(2,1)} %gate_weight_ref.3), kind=kOutput, calls=%fused_computation.151 | convolution fusion | flops 2415919104 | bytes 12582912 | tf_op jit(solution)/shard_map/dot_general | solution.py:53
  100.2 2.6 fusion.51.refs_0_
  107.7 3.9 %collective-permute-done.1 = bf16[128,3072]{1,0:T(8,128)(2,1)S(1)} collective-permute-done((bf16[128,3072]{1,0:T(8,128)(2,1)S(1)}, bf16[128,3072]{1,0:T(8,128)(2,1)S(1)}, u32[]{:S(2)}, u32[]{:S(2)}) %collective-permute-start.1) | collective-permute-done | bytes 786464 | tf_op jit(solution)/shard_map/ppermute | solution.py:291
  121.3 3.0 collective-permute-done.3.refs_7_
  124.3 11.4 %collective-permute-done.4.refs_2_ = bf16[256,384]{1,0:T(8,128)(2,1)S(1)} collective-permute-done((bf16[256,384]{1,0:T(8,128)(2,1)S(1)}, bf16[256,384]{1,0:T(8,128)(2,1)S(1)}, u32[]{:S(2)}, u32[]{:S(2)}) %collective-permute-start.4) | collective-permute-done | bytes 196640 | tf_op jit(solution)/shard_map/ppermute | solution.py:291
  142.9 7.3 %reduce-scatter.3.cloned.1.call-done.refs_8_ = bf16[512,768]{1,0:T(8,128)(2,1)} async-done(((bf16[2048,768]{1,0:T(8,128)(2,1)}), bf16[512,768]{1,0:T(8,128)(2,1)}) %reduce-scatter.3.cloned.1.call-update) | async-done | bytes 786448 | tf_op jit(solution)/shard_map/reduce_scatter | solution.py:348
  150.1 9.2 %conv_block.2 = (bf16[512,768]{1,0:T(8,128)(2,1)}, bf16[2,2,256,768]{3,2,1,0:T(8,128)(2,1)}, f32[31,768]{1,0:T(8,128)}) custom-call(s32[1]{0:T(128)} %bitcast.1.row_ref, f32[256,1536]{1,0:T(8,128)} %copy-done.8, f32[256,1536]{1,0:T(8,128)} %copy-done.9, bf16[256,384]{1,0:T(8,128)(2,1)} %copy-done.32, bf16[256,384]{1,0:T(8,128)(2,1)} %copy-done.31, ...), custom_call_target="tpu_custom_call" | custom-call | flops 36569088 | bytes 3932160 | tf_op jit(solution)/shard_map/conv_block/pallas_call | solution.py:161
  159.4 3.4 %collective-permute-done.12.refs_3_ = bf16[256,384]{1,0:T(8,128)(2,1)} collective-permute-done((bf16[256,384]{1,0:T(8,128)(2,1)}, bf16[256,384]{1,0:T(8,128)(2,1)}, u32[]{:S(2)}, u32[]{:S(2)}) %collective-permute-start.12) | collective-permute-done | bytes 196640 | tf_op jit(solution)/shard_map/ppermute | solution.py:291
  162.8 9.3 %conv_block.3 = (bf16[512,768]{1,0:T(8,128)(2,1)}, bf16[2,2,256,768]{3,2,1,0:T(8,128)(2,1)}, f32[31,768]{1,0:T(8,128)}) custom-call(s32[1]{0:T(128)} %bitcast.1.row_ref, f32[256,1536]{1,0:T(8,128)} %copy-done.8, f32[256,1536]{1,0:T(8,128)} %copy-done.9, ...), custom_call_target="tpu_custom_call", output_to_operand_aliasing={{0}: (11, {}), {1}: (12, {}), {2}: (13, {})} | custom-call | flops 36569088 | bytes 3932160 | tf_op jit(solution)/shard_map/conv_block/pallas_call | solution.py:161
  178.2 13.3 %collective-permute-done.15 = bf16[2,256,768]{2,1,0:T(8,128)(2,1)} collective-permute-done((bf16[2,256,768]{2,1,0:T(8,128)(2,1)S(1)}, bf16[2,256,768]{2,1,0:T(8,128)(2,1)}, u32[]{:S(2)}, u32[]{:S(2)}) %collective-permute-start.15) | collective-permute-done | bytes 786464 | tf_op jit(solution)/shard_map/ppermute | solution.py:291
  194.3 3.7 %copy-done = bf16[3072,1536]{1,0:T(8,128)(2,1)S(1)} copy-done((bf16[3072,1536]{1,0:T(8,128)(2,1)S(1)}, bf16[3072,1536]{1,0:T(8,128)(2,1)}, u32[]{:S(2)}) %copy-start) | copy-done | bytes 9437208
  198.1 9.6 %back_block.2 = bf16[2,256,1536]{2,1,0:T(8,128)(2,1)S(1)} custom-call(bf16[256,1536]{1,0:T(8,128)(2,1)S(1)} %get-tuple-element.148.value_ref, bf16[256,1536]{1,0:T(8,128)(2,1)S(1)} %get-tuple-element.149.gate_ref, bf16[3072,1536]{1,0:T(8,128)(2,1)S(1)} %copy-done, bf16[3072,1536]{1,0:T(8,128)(2,1)} %gate_weight_ref.3), custom_call_target="tpu_custom_call" | custom-call | flops 4831838208 | bytes 22020096 | tf_op jit(solution)/shard_map/back_block/pallas_call | solution.py:213
  212.9 8.7 %back_block.3 = bf16[2,256,1536]{2,1,0:T(8,128)(2,1)S(1)} custom-call(bf16[256,1536]{1,0:T(8,128)(2,1)S(1)} %pad_maximum_fusion.13.value_ref, bf16[256,1536]{1,0:T(8,128)(2,1)S(1)} %pad_maximum_fusion.14.gate_ref, bf16[3072,1536]{1,0:T(8,128)(2,1)S(1)} %bitcast.105, bf16[3072,1536]{1,0:T(8,128)(2,1)} %gate_weight_ref.3), custom_call_target="tpu_custom_call" | custom-call | flops 4831838208 | bytes 22020096 | tf_op jit(solution)/shard_map/back_block/pallas_call | solution.py:213
  224.8 8.6 %fusion.2 = f32[1536,1536]{1,0:T(8,128)} fusion(bf16[512,1536]{1,0:T(8,128)(2,1)S(1)} %collective-permute-done.17, bf16[256,768]{1,0:T(8,128)(2,1)S(1)} %get-tuple-element.111, bf16[256,768]{1,0:T(8,128)(2,1)S(1)} %get-tuple-element.113, bf16[256,768]{1,0:T(8,128)(2,1)S(1)} %get-tuple-element.107, bf16[256,768]{1,0:T(8,128)(2,1)S(1)} %get-tuple-element.109, ...), kind=kOutput, calls=%fused_computation.9 | convolution fusion | flops 4853858304 | bytes 15728640 | tf_op jit(solution)/shard_map/dot_general | solution.py:435
  233.4 3.5 %all-gather.9.cloned.1.call-done = bf16[2048,768]{1,0:T(8,128)(2,1)} async-done(((bf16[512,768]{1,0:T(8,128)(2,1)}), bf16[2048,768]{1,0:T(8,128)(2,1)}) %all-gather.9.cloned.1.call-update) | async-done | bytes 3145744 | tf_op jit(solution)/shard_map/all_gather | solution.py:414
  241.9 2.8 bitcast_dynamic-update-slice_fusion
  246.3 10.9 %fusion.12 = f32[1536,1536]{1,0:T(8,128)} fusion(bf16[1024,1536]{1,0:T(8,128)(2,1)} %pad_maximum_fusion.1, bf16[512,1536]{1,0:T(8,128)(2,1)} %collective-permute-done.20, bf16[256,768]{1,0:T(8,128)(2,1)S(1)} %get-tuple-element.112, bf16[256,768]{1,0:T(8,128)(2,1)S(1)} %get-tuple-element.110, bf16[256,768]{1,0:T(8,128)(2,1)S(1)} %get-tuple-element.108, ...), kind=kOutput, calls=%fused_computation.19 | convolution fusion | flops 4847566848 | bytes 15728640 | tf_op jit(solution)/shard_map/dot_general | solution.py:435
  257.2 5.6 %fusion.1 = (f32[4,1536]{1,0:T(4,128)S(1)}, f32[256]{0:T(256)S(1)}, f32[256]{0:T(256)S(1)}) fusion(bf16[4,256,1536]{2,1,0:T(8,128)(2,1)} %bitcast.39, f32[256]{0:T(256)S(1)} %bitcast.135, f32[256]{0:T(256)S(1)} %bitcast.133, bf16[4,128,1536]{2,1,0:T(8,128)(2,1)S(1)} %copy-done.4, bf16[4,128,1536]{2,1,0:T(8,128)(2,1)S(1)} %copy-done.2, f32[4,1536]{1,0:T(4,128)S(1)} %mul.91), kind=kLoop, calls=%fused_computation.4 | loop fusion | flops 20440576 | bytes 6344704 | tf_op jit(solution)/shard_map/reduce_sum | solution.py:475
  272.6 2.7 collective-permute-start.31
  275.3 3.3 %collective-permute-done.19 = bf16[2,512,768]{2,1,0:T(8,128)(2,1)S(1)} collective-permute-done((bf16[2,512,768]{2,1,0:T(8,128)(2,1)S(1)}, bf16[2,512,768]{2,1,0:T(8,128)(2,1)S(1)}, u32[]{:S(2)}, u32[]{:S(2)}) %collective-permute-start.19) | collective-permute-done | bytes 1572896 | tf_op jit(solution)/shard_map/ppermute | solution.py:291
  291.4 2.9 collective-permute-done.27
  295.1 9.0 %fusion.22 = f32[1536,1536]{1,0:T(8,128)} fusion(bf16[512,1536]{1,0:T(8,128)(2,1)S(1)} %collective-permute-done.25, bf16[512,1536]{1,0:T(8,128)(2,1)S(1)} %get-tuple-element.88, bf16[512,1536]{1,0:T(8,128)(2,1)} %collective-permute-done.11, bf16[256,1536]{1,0:T(8,128)(2,1)S(1)} %copy-done.25, bf16[256,1536]{1,0:T(8,128)(2,1)S(1)} %bitcast.128), kind=kOutput, calls=%fused_computation.31 | convolution fusion | flops 4847566848 | bytes 15728640 | tf_op jit(solution)/shard_map/dot_general | solution.py:435
  304.1 5.0 %collective-permute-done.21 = bf16[256,1536]{1,0:T(8,128)(2,1)S(1)} collective-permute-done((bf16[256,1536]{1,0:T(8,128)(2,1)S(1)}, bf16[256,1536]{1,0:T(8,128)(2,1)S(1)}, u32[]{:S(2)}, u32[]{:S(2)}) %collective-permute-start.21) | collective-permute-done | bytes 786464 | tf_op jit(solution)/shard_map/ppermute | solution.py:291
  309.1 3.7 %fusion.38 = (bf16[1,256,1536]{2,1,0:T(8,128)(2,1)}, bf16[1,256,1536]{2,1,0:T(8,128)(2,1)}) fusion(bf16[256,1536]{1,0:T(8,128)(2,1)} %reduce-scatter.5.cloned.1.call-done, bf16[1,256,1536]{2,1,0:T(8,128)(2,1)S(1)} %copy-done.16, f32[256]{0:T(256)S(1)} %bitcast.138, f32[256]{0:T(256)S(1)} %bitcast.136, f32[256]{0:T(256)S(1)} %bitcast.134, ...), kind=kLoop, calls=%fused_computation.67 | loop fusion | flops 6291456 | bytes 6301696 | tf_op jit(solution)/shard_map/reshape | solution.py:515
  (235 shorter events, 96.4 us)
Async XLA Ops:
  7.2 57.9 %all-gather.5.cloned.1.call-start = ((), (), s32[]{:S(2)}) async-start(), calls=%async_computation.2 | async-start | bytes 1966080 | tf_op jit(solution)/shard_map/all_gather | solution.py:306
  9.3 78.8 %all-gather.7.cloned.1.call-start = ((), (), s32[]{:S(2)}) async-start(), calls=%async_computation.3 | async-start | bytes 1966080 | tf_op jit(solution)/shard_map/all_gather | solution.py:306
  9.3 21.6 %collective-permute-start.7 = (bf16[256,1536]{1,0:T(8,128)(2,1)}, bf16[256,1536]{1,0:T(8,128)(2,1)S(1)}, u32[]{:S(2)}, u32[]{:S(2)}) collective-permute-start(bf16[256,1536]{1,0:T(8,128)(2,1)} %bitcast.126), channel_id=1, source_target_pairs={{0,8},{8,0},{1,9},{9,1},{2,10},{10,2},{3,11},{11,3},{4,12},{12,4},... | collective-permute-start | bytes 2359304 | tf_op jit(solution)/shard_map/ppermute | solution.py:291
  22.2 41.7 %collective-permute-start.9 = (bf16[2,256,768]{1,2,0:T(8,128)(2,1)}, bf16[2,256,768]{1,2,0:T(8,128)(2,1)}, u32[]{:S(2)}, u32[]{:S(2)}) collective-permute-start(bf16[2,256,768]{1,2,0:T(8,128)(2,1)} %pad_maximum_fusion.10), channel_id=1, source_target_pairs={{0,8},{8,0},{1,9},{9,1},{2,10},{10,2},{3,11},{11,3},{4,12},{12,4},... | collective-permute-start | bytes 2359304 | tf_op jit(solution)/shard_map/ppermute | solution.py:291
  22.3 127.9 %reduce-scatter.3.cloned.1.call-start = ((), (), s32[]{:S(2)}) async-start(), calls=%async_computation.4 | async-start | bytes 3932160 | tf_op jit(solution)/shard_map/reduce_scatter | solution.py:348
  32.5 31.3 %collective-permute-start.8 = (bf16[2,256,768]{1,2,0:T(8,128)(2,1)S(1)}, bf16[2,256,768]{1,2,0:T(8,128)(2,1)S(1)}, u32[]{:S(2)}, u32[]{:S(2)}) collective-permute-start(bf16[2,256,768]{1,2,0:T(8,128)(2,1)S(1)} %pad_maximum_fusion.9), channel_id=1, source_target_pairs={{0,8},{8,0},{1,9},{9,1},{2,10},{10,2},{3,11},{11,3},{4,12},{12,4},... | collective-permute-start | bytes 2359304 | tf_op jit(solution)/shard_map/ppermute | solution.py:291
  68.1 20.0 %collective-permute-start = (bf16[128,3072]{1,0:T(8,128)(2,1)S(1)}, bf16[128,3072]{1,0:T(8,128)(2,1)}, u32[]{:S(2)}, u32[]{:S(2)}) collective-permute-start(bf16[128,3072]{1,0:T(8,128)(2,1)S(1)} %get-tuple-element.44), channel_id=1, source_target_pairs={{0,8},{8,0},{1,9},{9,1},{2,10},{10,2},{3,11},{11,3},{4,12},{12,4},... | collective-permute-start | bytes 2359304 | tf_op jit(solution)/shard_map/ppermute | solution.py:291
  78.5 158.4 %all-gather.9.cloned.1.call-start = ((), (), s32[]{:S(2)}) async-start(), calls=%async_computation.6 | async-start | bytes 3932160 | tf_op jit(solution)/shard_map/all_gather | solution.py:414
  91.1 20.5 %collective-permute-start.1 = (bf16[128,3072]{1,0:T(8,128)(2,1)S(1)}, bf16[128,3072]{1,0:T(8,128)(2,1)S(1)}, u32[]{:S(2)}, u32[]{:S(2)}) collective-permute-start(bf16[128,3072]{1,0:T(8,128)(2,1)S(1)} %get-tuple-element.47), channel_id=1, source_target_pairs={{0,8},{8,0},{1,9},{9,1},{2,10},{10,2},{3,11},{11,3},{4,12},{12,4},... | collective-permute-start | bytes 2359304 | tf_op jit(solution)/shard_map/ppermute | solution.py:291
  103.6 17.7 %collective-permute-start.5 = (bf16[256,384]{1,0:T(8,128)(2,1)S(1)}, bf16[256,384]{1,0:T(8,128)(2,1)S(1)}, u32[]{:S(2)}, u32[]{:S(2)}) collective-permute-start(bf16[256,384]{1,0:T(8,128)(2,1)S(1)} %get-tuple-element.121), channel_id=1, source_target_pairs={{0,8},{8,0},{1,9},{9,1},{2,10},{10,2},{3,11},{11,3},{4,12},{12,4},... | collective-permute-start | bytes 589832 | tf_op jit(solution)/shard_map/ppermute | solution.py:291
  105.0 19.3 %collective-permute-start.3 = (f32[256,384]{1,0:T(8,128)S(1)}, f32[256,384]{1,0:T(8,128)S(1)}, u32[]{:S(2)}, u32[]{:S(2)}) collective-permute-start(f32[256,384]{1,0:T(8,128)S(1)} %get-tuple-element.117), channel_id=1, source_target_pairs={{0,8},{8,0},{1,9},{9,1},{2,10},{10,2},{3,11},{11,3},{4,12},{12,4},... | collective-permute-start | bytes 1179656 | tf_op jit(solution)/shard_map/ppermute | solution.py:291
  112.0 27.7 %collective-permute-start.10 = (bf16[512,1536]{1,0:T(8,128)(2,1)S(1)}, bf16[512,1536]{1,0:T(8,128)(2,1)S(1)}, u32[]{:S(2)}, u32[]{:S(2)}) collective-permute-start(bf16[512,1536]{1,0:T(8,128)(2,1)S(1)} %get-tuple-element.97), channel_id=1, source_target_pairs={{0,1},{1,0},{2,3},{3,2},{4,5},{5,4},{6,7},{7,6},{8,9},{9,8},{10,11... | collective-permute-start | bytes 4718600 | tf_op jit(solution)/shard_map/ppermute | solution.py:44
  115.8 19.9 %collective-permute-start.2 = (f32[256,384]{1,0:T(8,128)S(1)}, f32[256,384]{1,0:T(8,128)S(1)}, u32[]{:S(2)}, u32[]{:S(2)}) collective-permute-start(f32[256,384]{1,0:T(8,128)S(1)} %get-tuple-element.119), channel_id=1, source_target_pairs={{0,8},{8,0},{1,9},{9,1},{2,10},{10,2},{3,11},{11,3},{4,12},{12,4},... | collective-permute-start | bytes 1179656 | tf_op jit(solution)/shard_map/ppermute | solution.py:291
  120.7 14.9 %collective-permute-start.4 = (bf16[256,384]{1,0:T(8,128)(2,1)S(1)}, bf16[256,384]{1,0:T(8,128)(2,1)S(1)}, u32[]{:S(2)}, u32[]{:S(2)}) collective-permute-start(bf16[256,384]{1,0:T(8,128)(2,1)S(1)} %get-tuple-element.122), channel_id=1, source_target_pairs={{0,8},{8,0},{1,9},{9,1},{2,10},{10,2},{3,11},{11,3},{4,12},{12,4},... | collective-permute-start | bytes 589832 | tf_op jit(solution)/shard_map/ppermute | solution.py:291
  135.6 23.7 %collective-permute-start.14 = (f32[256,384]{1,0:T(8,128)}, f32[256,384]{1,0:T(8,128)S(1)}, u32[]{:S(2)}, u32[]{:S(2)}) collective-permute-start(f32[256,384]{1,0:T(8,128)} %get-tuple-element.58), channel_id=1, source_target_pairs={{0,8},{8,0},{1,9},{9,1},{2,10},{10,2},{3,11},{11,3},{4,12},{12,4},... | collective-permute-start | bytes 1179656 | tf_op jit(solution)/shard_map/ppermute | solution.py:291
  137.2 22.2 %collective-permute-start.13 = (f32[256,384]{1,0:T(8,128)}, f32[256,384]{1,0:T(8,128)S(1)}, u32[]{:S(2)}, u32[]{:S(2)}) collective-permute-start(f32[256,384]{1,0:T(8,128)} %get-tuple-element.56), channel_id=1, source_target_pairs={{0,8},{8,0},{1,9},{9,1},{2,10},{10,2},{3,11},{11,3},{4,12},{12,4},... | collective-permute-start | bytes 1179656 | tf_op jit(solution)/shard_map/ppermute | solution.py:291
  137.7 25.1 %collective-permute-start.6 = (bf16[256,384]{1,0:T(8,128)(2,1)}, bf16[256,384]{1,0:T(8,128)(2,1)}, u32[]{:S(2)}, u32[]{:S(2)}) collective-permute-start(bf16[256,384]{1,0:T(8,128)(2,1)} %get-tuple-element.48), channel_id=1, source_target_pairs={{0,8},{8,0},{1,9},{9,1},{2,10},{10,2},{3,11},{11,3},{4,12},{12,4},... | collective-permute-start | bytes 589832 | tf_op jit(solution)/shard_map/ppermute | solution.py:291
  139.2 23.6 %collective-permute-start.12 = (bf16[256,384]{1,0:T(8,128)(2,1)}, bf16[256,384]{1,0:T(8,128)(2,1)}, u32[]{:S(2)}, u32[]{:S(2)}) collective-permute-start(bf16[256,384]{1,0:T(8,128)(2,1)} %get-tuple-element.54), channel_id=1, source_target_pairs={{0,8},{8,0},{1,9},{9,1},{2,10},{10,2},{3,11},{11,3},{4,12},{12,4},... | collective-permute-start | bytes 589832 | tf_op jit(solution)/shard_map/ppermute | solution.py:291
  173.7 17.8 %collective-permute-start.15 = (bf16[2,256,768]{2,1,0:T(8,128)(2,1)S(1)}, bf16[2,256,768]{2,1,0:T(8,128)(2,1)}, u32[]{:S(2)}, u32[]{:S(2)}) collective-permute-start(bf16[2,256,768]{2,1,0:T(8,128)(2,1)S(1)} %get-tuple-element.64), channel_id=1, source_target_pairs={{0,8},{8,0},{1,9},{9,1},{2,10},{10,2},{3,11},{11,3},{4,12},{12,4},... | collective-permute-start | bytes 2359304 | tf_op jit(solution)/shard_map/ppermute | solution.py:291
  175.4 133.7 %reduce-scatter.5.cloned.1.call-start = ((), (), s32[]{:S(2)}) async-start(), calls=%async_computation.5 | async-start | bytes 3932160 | tf_op jit(solution)/shard_map/reduce_scatter | solution.py:456
  177.9 117.2 %collective-permute-start.11 = (bf16[512,1536]{1,0:T(8,128)(2,1)}, bf16[512,1536]{1,0:T(8,128)(2,1)}, u32[]{:S(2)}, u32[]{:S(2)}) collective-permute-start(bf16[512,1536]{1,0:T(8,128)(2,1)} %pad_maximum_fusion.5), channel_id=1, source_target_pairs={{0,1},{1,0},{2,3},{3,2},{4,5},{5,4},{6,7},{7,6},{8,9},{9,8},{10,11... | collective-permute-start | bytes 4718600 | tf_op jit(solution)/shard_map/ppermute | solution.py:44
  191.5 17.8 %collective-permute-start.16 = (bf16[2,256,768]{2,1,0:T(8,128)(2,1)S(1)}, bf16[2,256,768]{2,1,0:T(8,128)(2,1)}, u32[]{:S(2)}, u32[]{:S(2)}) collective-permute-start(bf16[2,256,768]{2,1,0:T(8,128)(2,1)S(1)} %get-tuple-element.62), channel_id=1, source_target_pairs={{0,8},{8,0},{1,9},{9,1},{2,10},{10,2},{3,11},{11,3},{4,12},{12,4},... | collective-permute-start | bytes 2359304 | tf_op jit(solution)/shard_map/ppermute | solution.py:291
  207.6 34.3 %collective-permute-start.18 = (bf16[2,256,1536]{2,1,0:T(8,128)(2,1)S(1)}, bf16[2,256,1536]{2,1,0:T(8,128)(2,1)}, u32[]{:S(2)}, u32[]{:S(2)}) collective-permute-start(bf16[2,256,1536]{2,1,0:T(8,128)(2,1)S(1)} %back_block.2), channel_id=1, source_target_pairs={{0,8},{8,0},{1,9},{9,1},{2,10},{10,2},{3,11},{11,3},{4,12},{12,4},... | collective-permute-start | bytes 4718600 | tf_op jit(solution)/shard_map/ppermute | solution.py:291
  210.9 13.9 %collective-permute-start.17 = (bf16[512,1536]{1,0:T(8,128)(2,1)S(1)}, bf16[512,1536]{1,0:T(8,128)(2,1)S(1)}, u32[]{:S(2)}, u32[]{:S(2)}) collective-permute-start(bf16[512,1536]{1,0:T(8,128)(2,1)S(1)} %maximum_maximum_fusion.1), channel_id=1, source_target_pairs={{0,1},{1,0},{2,3},{3,2},{4,5},{5,4},{6,7},{7,6},{8,9},{9,8},{10,11... | collective-permute-start | bytes 4718600 | tf_op jit(solution)/shard_map/ppermute | solution.py:44
  212.3 34.1 %collective-permute-start.20 = (bf16[512,1536]{1,0:T(8,128)(2,1)}, bf16[512,1536]{1,0:T(8,128)(2,1)}, u32[]{:S(2)}, u32[]{:S(2)}) collective-permute-start(bf16[512,1536]{1,0:T(8,128)(2,1)} %maximum_maximum_fusion.2), channel_id=1, source_target_pairs={{0,1},{1,0},{2,3},{3,2},{4,5},{5,4},{6,7},{7,6},{8,9},{9,8},{10,11... | collective-permute-start | bytes 4718600 | tf_op jit(solution)/shard_map/ppermute | solution.py:44
  244.8 33.9 %collective-permute-start.19 = (bf16[2,512,768]{2,1,0:T(8,128)(2,1)S(1)}, bf16[2,512,768]{2,1,0:T(8,128)(2,1)S(1)}, u32[]{:S(2)}, u32[]{:S(2)}) collective-permute-start(bf16[2,512,768]{2,1,0:T(8,128)(2,1)S(1)} %copy-done.21), channel_id=1, source_target_pairs={{0,8},{8,0},{1,9},{9,1},{2,10},{10,2},{3,11},{11,3},{4,12},{12,4},... | collective-permute-start | bytes 4718600 | tf_op jit(solution)/shard_map/ppermute | solution.py:291
  262.9 7.1 %collective-permute-start.23 = (f32[2,256]{1,0:T(2,128)S(1)}, f32[2,256]{1,0:T(2,128)S(1)}, u32[]{:S(2)}, u32[]{:S(2)}) collective-permute-start(f32[2,256]{1,0:T(2,128)S(1)} %pad_maximum_fusion.18), channel_id=1, source_target_pairs={{0,4},{2,6},{4,0},{6,2},{1,5},{3,7},{5,1},{7,3},{8,12},{10,14},{12... | collective-permute-start | bytes 6152 | tf_op jit(solution)/shard_map/ppermute | solution.py:44
  269.9 13.8 %collective-permute-start.26 = (f32[31,768]{1,0:T(8,128)S(1)}, f32[31,768]{1,0:T(8,128)S(1)}, u32[]{:S(2)}, u32[]{:S(2)}) collective-permute-start(f32[31,768]{1,0:T(8,128)S(1)} %copy-done.26), channel_id=1, source_target_pairs={{0,1},{1,0},{2,3},{3,2},{4,5},{5,4},{6,7},{7,6},{8,9},{9,8},{10,11... | collective-permute-start | bytes 285704 | tf_op jit(solution)/shard_map/ppermute | solution.py:44
  271.4 11.2 %collective-permute-start.29 = (f32[1536]{0:T(1024)S(1)}, f32[1536]{0:T(1024)S(1)}, u32[]{:S(2)}, u32[]{:S(2)}) collective-permute-start(f32[1536]{0:T(1024)S(1)} %get-tuple-element.82), channel_id=1, source_target_pairs={{0,2},{2,4},{4,6},{6,0},{1,3},{3,5},{5,7},{7,1},{8,10},{10,12},{12... | collective-permute-start | bytes 18440 | tf_op jit(solution)/shard_map/ppermute | solution.py:44
  272.6 10.1 %collective-permute-start.31 = (f32[1536]{0:T(1024)S(1)}, f32[1536]{0:T(1024)S(1)}, u32[]{:S(2)}, u32[]{:S(2)}) collective-permute-start(f32[1536]{0:T(1024)S(1)} %get-tuple-element.83), channel_id=1, source_target_pairs={{0,6},{2,0},{4,2},{6,4},{1,7},{3,1},{5,3},{7,5},{8,14},{10,8},{12,... | collective-permute-start | bytes 18440 | tf_op jit(solution)/shard_map/ppermute | solution.py:44
  282.6 12.4 %collective-permute-start.25 = (bf16[512,1536]{1,0:T(8,128)(2,1)S(1)}, bf16[512,1536]{1,0:T(8,128)(2,1)S(1)}, u32[]{:S(2)}, u32[]{:S(2)}) collective-permute-start(bf16[512,1536]{1,0:T(8,128)(2,1)S(1)} %get-tuple-element.89), channel_id=1, source_target_pairs={{0,1},{1,0},{2,3},{3,2},{4,5},{5,4},{6,7},{7,6},{8,9},{9,8},{10,11... | collective-permute-start | bytes 4718600 | tf_op jit(solution)/shard_map/ppermute | solution.py:44
  289.0 20.1 %collective-permute-start.21 = (bf16[256,1536]{1,0:T(8,128)(2,1)S(1)}, bf16[256,1536]{1,0:T(8,128)(2,1)S(1)}, u32[]{:S(2)}, u32[]{:S(2)}) collective-permute-start(bf16[256,1536]{1,0:T(8,128)(2,1)S(1)} %slice.183), channel_id=1, source_target_pairs={{0,8},{8,0},{1,9},{9,1},{2,10},{10,2},{3,11},{11,3},{4,12},{12,4},... | collective-permute-start | bytes 2359304 | tf_op jit(solution)/shard_map/ppermute | solution.py:291
  (54 other events, 474.4 us)
Sparse Core Ops, SparseCore 0:
  10.1 39.7 all-gather.4
  52.1 35.9 all-gather.6
  91.0 59.0 reduce-scatter.2
  175.5 61.3 all-gather.8
  244.8 60.9 reduce-scatter.4

commit v4 on v3

--- a/solution.py
+++ b/solution.py
@@ -477,13 +477,18 @@
     for s, piece in zip(shifts, mixed_in):
         mixed_blocks.append(side_by_side(after(piece, gate_weight_grad, projected)))
         projected = projected + dot(mixed_blocks[-1], mixer_of[s])
-    sums = sum_over(sums, "col")
-    gain_sum = sum_over(gain_sum, "dp")
-    gain_pieces = exchange(
-        lambda j: lax.dynamic_index_in_dim(gain_sum, j, 0, keepdims=False), "col"
-    )
-    gain_col = sum(gain_pieces[1:], gain_pieces[0])
-    norm_gain_gradient = sum_over(after(gain_col, projected), "row")
+    small = exchange(
+        lambda j: jnp.concatenate(
+            [sums.reshape(-1), lax.dynamic_index_in_dim(gain_sum, j, 0, keepdims=False)]
+        ),
+        "col",
+    )
+    small = sum(small[1:], small[0])
+    sums, gain_col = small[: 2 * tokens].reshape(2, tokens), small[2 * tokens :]
+    gain_col = sum_over(gain_col, "dp")
+    gain_pieces = exchange(lambda j: gain_col, "row")
+    gain_pieces = [gain_pieces[0]] + [after(x, projected) for x in gain_pieces[1:]]
+    norm_gain_gradient = sum(gain_pieces[1:], gain_pieces[0])
     projected_blocks = [projected[k * tokens : (k + 1) * tokens] for k in range(n_row)]
     total = own.astype(F32) + projected_blocks[0]
     for s in shifts:
@@ -501,8 +506,10 @@
     )
     mixer_weight_grad = weight_grad(spread(mixed_rows), grad_cells)
 
-    kernel_sum = after(sum_over(after(kernel_rows, *part_in), "dp"), projected)
-    kernel_grad = jnp.concatenate(by_source(exchange(lambda j: kernel_sum, "row"), "row"), axis=1)
+    kernel_sum = sum_over(after(kernel_rows, *part_in), "dp")
+    kernel_pieces = exchange(lambda j: kernel_sum, "row")
+    kernel_pieces = [kernel_pieces[0]] + [after(x, projected) for x in kernel_pieces[1:]]
+    kernel_grad = jnp.concatenate(by_source(kernel_pieces, "row"), axis=1)
 
     normed_grad = summed.astype(F32)
     own_standard = (own.astype(F32) - mean) * inverse

time: 326 us -> 324 us (level)
  starting transfers between devices: 37.9 us -> 31.8 us
  waiting for transfers between devices: 98.7 us -> 103 us
    ppermute x18, waiting for transfers between devices: 74.7 us -> 81.8 us  [to_row(): return lax.ppermute(x, 'row', ring(n_row, s))]
    ppermute x15 -> x12, starting transfers between devices: 13.9 us -> 8.72 us  [exchange(): lax.ppermute(pick((me + s) % count), axis, ring(count, s))]
    unnamed x100 -> x101, local copies, waits for them, and re-layouts: 12.5 us -> 12 us
  transfers between devices with their start and end apart: 38 -> 35, of which waited for: 18 -> 15; matrix products, arithmetic and copies ran while one was open for 35% -> 35% of each run, Pallas kernels for 10% -> 10%
where the time goes in v4:
time: 324 us; the launch traced here: 317 us
  waiting for transfers between devices  103 us (32%)
  matrix products  58.6 us (18%)
  local copies, waits for them, and re-layouts  42.5 us (13%)
  Pallas kernels  39.9 us (12%)
  starting transfers between devices  31.8 us (10%)
  other arithmetic  26.5 us (8%)
  between operations  15.2 us (5%)
    ppermute x18, waiting for transfers between devices, to_row(): return lax.ppermute(x, 'row', ring(n_row, s))  81.8 us
    dot_general x3, matrix products, weight_grad(): lax.dot_general(left, right, CONTRACT_FIRST, preferred_element_type=F32)  28.5 us
    ppermute x18, starting transfers between devices, to_row(): return lax.ppermute(x, 'row', ring(n_row, s))  22.7 us
    dot_general x6, matrix products, dot(): return jnp.dot(a, b, preferred_element_type=F32)  19.4 us
    pallas_call x2, Pallas kernels, conv_block(): pl.pallas_call(functools.partial(conv_body, taps, frames, rows_in, len(be...  18.5 us
    pallas_call x2, Pallas kernels, back_block(): pl.pallas_call(back_body, grid=(depth // tile,), in_specs=[left, left, ri...  18.2 us
    unnamed x101, local copies, waits for them, and re-layouts  12 us
    dot_general x4, matrix products, dot_last(): return lax.dot_general(a, b, CONTRACT_LAST, preferred_element_type=F32)  10.6 us
  transfers between devices with their start and end apart: 35, of which 15 were waited for; matrix products, arithmetic and copies ran while one was open for 35% of the time, Pallas kernels for 10%

profile of v4, /device:TPU:0, one launch (start us, length us, event | category | flops | bytes accessed | tf_op | source)
XLA Modules:
  0.0 317.4 jit_solution(832396071940768409)
XLA Ops:
  9.3 3.0 collective-permute-start.7
  12.3 6.6 %constant_dynamic-slice_fusion.9 = (bf16[2,1,768,1536]{3,2,1,0:T(8,128)(2,1)S(1)}, bf16[2,1,768,1536]{3,2,1,0:T(8,128)(2,1)}) fusion(bf16[2,2,768,1536]{3,2,1,0:T(8,128)(2,1)} %bitcast.112, s32[]{:T(128)S(6)} %select_n.238, s32[]{:T(128)S(6)} %select_n.239), kind=kLoop, calls=%fused_computation.135 | loop fusion | bytes 18874376 | tf_op jit(solution)/shard_map/jit(dynamic_index_in_dim)/dynamic_slice | solution.py:311
  22.3 3.9 %fusion.28 = bf16[256,1536]{0,1:T(8,128)(2,1)S(1)} fusion(bf16[1536,1536]{1,0:T(8,128)(2,1)} %bitcast.120, bf16[1,256,1536]{2,1,0:T(8,128)(2,1)S(1)} %copy-done.17), kind=kOutput, calls=%fused_computation.41 | convolution fusion | flops 1208352768 | bytes 6291456 | tf_op jit(solution)/shard_map/dot_general | solution.py:57
  26.2 4.7 %collective-permute-done.7 = bf16[256,1536]{1,0:T(8,128)(2,1)S(1)} collective-permute-done((bf16[256,1536]{1,0:T(8,128)(2,1)}, bf16[256,1536]{1,0:T(8,128)(2,1)S(1)}, u32[]{:S(2)}, u32[]{:S(2)}) %collective-permute-start.7) | collective-permute-done | bytes 786464 | tf_op jit(solution)/shard_map/ppermute | solution.py:291
  35.6 3.8 %fusion.29 = bf16[256,1536]{0,1:T(8,128)(2,1)S(1)} fusion(bf16[1536,1536]{1,0:T(8,128)(2,1)} %bitcast.121, bf16[256,1536]{1,0:T(8,128)(2,1)S(1)} %collective-permute-done.7), kind=kOutput, calls=%fused_computation.42 | convolution fusion | flops 1208352768 | bytes 6291456 | tf_op jit(solution)/shard_map/dot_general | solution.py:57
  40.3 23.5 %collective-permute-done.8 = bf16[2,256,768]{1,2,0:T(8,128)(2,1)S(1)} collective-permute-done((bf16[2,256,768]{1,2,0:T(8,128)(2,1)S(1)}, bf16[2,256,768]{1,2,0:T(8,128)(2,1)S(1)}, u32[]{:S(2)}, u32[]{:S(2)}) %collective-permute-start.8) | collective-permute-done | bytes 786464 | tf_op jit(solution)/shard_map/ppermute | solution.py:291
  73.9 4.6 %copy.25 = bf16[4,512,768]{2,1,0:T(8,128)(2,1)} copy(bf16[4,512,768]{1,2,0:T(8,128)(2,1)} %pad_maximum_fusion) | data formatting | bytes 6291456 | tf_op jit(solution)/shard_map/concatenate | solution.py:330
  79.8 8.3 %all-gather.7.cloned.1.call-done.x_ref = bf16[4,128,1536]{2,1,0:T(8,128)(2,1)} async-done(((bf16[1,128,1536]{2,1,0:T(8,128)(2,1)}), bf16[4,128,1536]{2,1,0:T(8,128)(2,1)}) %all-gather.7.cloned.1.call-update) | async-done | bytes 1572880 | tf_op jit(solution)/shard_map/all_gather | solution.py:306
  93.6 6.4 %fusion.57.refs_4_ = f32[256,1536]{1,0:T(8,128)S(1)} fusion(bf16[256,3072]{1,0:T(8,128)(2,1)S(1)} %get-tuple-element.131, bf16[3072,1536]{1,0:T(8,128)(2,1)} %gate_weight_ref.3), kind=kOutput, calls=%fused_computation.157 | convolution fusion | flops 2415919104 | bytes 12582912 | tf_op jit(solution)/shard_map/dot_general | solution.py:53
  100.2 2.6 fusion.54.refs_0_
  107.7 3.9 %collective-permute-done.1 = bf16[128,3072]{1,0:T(8,128)(2,1)S(1)} collective-permute-done((bf16[128,3072]{1,0:T(8,128)(2,1)S(1)}, bf16[128,3072]{1,0:T(8,128)(2,1)S(1)}, u32[]{:S(2)}, u32[]{:S(2)}) %collective-permute-start.1) | collective-permute-done | bytes 786464 | tf_op jit(solution)/shard_map/ppermute | solution.py:291
  121.3 3.0 collective-permute-done.3.refs_7_
  124.3 11.4 %collective-permute-done.4.refs_2_ = bf16[256,384]{1,0:T(8,128)(2,1)S(1)} collective-permute-done((bf16[256,384]{1,0:T(8,128)(2,1)S(1)}, bf16[256,384]{1,0:T(8,128)(2,1)S(1)}, u32[]{:S(2)}, u32[]{:S(2)}) %collective-permute-start.4) | collective-permute-done | bytes 196640 | tf_op jit(solution)/shard_map/ppermute | solution.py:291
  142.8 7.3 %reduce-scatter.3.cloned.1.call-done.refs_8_ = bf16[512,768]{1,0:T(8,128)(2,1)} async-done(((bf16[2048,768]{1,0:T(8,128)(2,1)}), bf16[512,768]{1,0:T(8,128)(2,1)}) %reduce-scatter.3.cloned.1.call-update) | async-done | bytes 786448 | tf_op jit(solution)/shard_map/reduce_scatter | solution.py:348
  150.1 9.2 %conv_block.2 = (bf16[512,768]{1,0:T(8,128)(2,1)}, bf16[2,2,256,768]{3,2,1,0:T(8,128)(2,1)}, f32[31,768]{1,0:T(8,128)}) custom-call(s32[1]{0:T(128)} %bitcast.1.row_ref, f32[256,1536]{1,0:T(8,128)} %copy-done.8, f32[256,1536]{1,0:T(8,128)} %copy-done.9, bf16[256,384]{1,0:T(8,128)(2,1)} %copy-done.32, bf16[256,384]{1,0:T(8,128)(2,1)} %copy-done.31, ...), custom_call_target="tpu_custom_call" | custom-call | flops 36569088 | bytes 3932160 | tf_op jit(solution)/shard_map/conv_block/pallas_call | solution.py:161
  159.4 3.4 %collective-permute-done.12.refs_3_ = bf16[256,384]{1,0:T(8,128)(2,1)} collective-permute-done((bf16[256,384]{1,0:T(8,128)(2,1)}, bf16[256,384]{1,0:T(8,128)(2,1)}, u32[]{:S(2)}, u32[]{:S(2)}) %collective-permute-start.12) | collective-permute-done | bytes 196640 | tf_op jit(solution)/shard_map/ppermute | solution.py:291
  162.8 9.3 %conv_block.3 = (bf16[512,768]{1,0:T(8,128)(2,1)}, bf16[2,2,256,768]{3,2,1,0:T(8,128)(2,1)}, f32[31,768]{1,0:T(8,128)}) custom-call(s32[1]{0:T(128)} %bitcast.1.row_ref, f32[256,1536]{1,0:T(8,128)} %copy-done.8, f32[256,1536]{1,0:T(8,128)} %copy-done.9, ...), custom_call_target="tpu_custom_call", output_to_operand_aliasing={{0}: (11, {}), {1}: (12, {}), {2}: (13, {})} | custom-call | flops 36569088 | bytes 3932160 | tf_op jit(solution)/shard_map/conv_block/pallas_call | solution.py:161
  178.2 13.3 %collective-permute-done.15 = bf16[2,256,768]{2,1,0:T(8,128)(2,1)} collective-permute-done((bf16[2,256,768]{2,1,0:T(8,128)(2,1)S(1)}, bf16[2,256,768]{2,1,0:T(8,128)(2,1)}, u32[]{:S(2)}, u32[]{:S(2)}) %collective-permute-start.15) | collective-permute-done | bytes 786464 | tf_op jit(solution)/shard_map/ppermute | solution.py:291
  194.3 3.7 %copy-done = bf16[3072,1536]{1,0:T(8,128)(2,1)S(1)} copy-done((bf16[3072,1536]{1,0:T(8,128)(2,1)S(1)}, bf16[3072,1536]{1,0:T(8,128)(2,1)}, u32[]{:S(2)}) %copy-start) | copy-done | bytes 9437208
  198.1 9.6 %back_block.2 = bf16[2,256,1536]{2,1,0:T(8,128)(2,1)S(1)} custom-call(bf16[256,1536]{1,0:T(8,128)(2,1)S(1)} %get-tuple-element.151.value_ref, bf16[256,1536]{1,0:T(8,128)(2,1)S(1)} %get-tuple-element.152.gate_ref, bf16[3072,1536]{1,0:T(8,128)(2,1)S(1)} %copy-done, bf16[3072,1536]{1,0:T(8,128)(2,1)} %gate_weight_ref.3), custom_call_target="tpu_custom_call" | custom-call | flops 4831838208 | bytes 22020096 | tf_op jit(solution)/shard_map/back_block/pallas_call | solution.py:213
  212.9 8.7 %back_block.3 = bf16[2,256,1536]{2,1,0:T(8,128)(2,1)S(1)} custom-call(bf16[256,1536]{1,0:T(8,128)(2,1)S(1)} %pad_maximum_fusion.13.value_ref, bf16[256,1536]{1,0:T(8,128)(2,1)S(1)} %pad_maximum_fusion.14.gate_ref, bf16[3072,1536]{1,0:T(8,128)(2,1)S(1)} %bitcast.106, bf16[3072,1536]{1,0:T(8,128)(2,1)} %gate_weight_ref.3), custom_call_target="tpu_custom_call" | custom-call | flops 4831838208 | bytes 22020096 | tf_op jit(solution)/shard_map/back_block/pallas_call | solution.py:213
  224.8 8.6 %fusion.2 = f32[1536,1536]{1,0:T(8,128)} fusion(bf16[512,1536]{1,0:T(8,128)(2,1)S(1)} %collective-permute-done.17, bf16[256,768]{1,0:T(8,128)(2,1)S(1)} %get-tuple-element.111, bf16[256,768]{1,0:T(8,128)(2,1)S(1)} %get-tuple-element.113, bf16[256,768]{1,0:T(8,128)(2,1)S(1)} %get-tuple-element.107, bf16[256,768]{1,0:T(8,128)(2,1)S(1)} %get-tuple-element.109, ...), kind=kOutput, calls=%fused_computation.9 | convolution fusion | flops 4853858304 | bytes 15728640 | tf_op jit(solution)/shard_map/dot_general | solution.py:435
  233.4 3.5 %all-gather.9.cloned.1.call-done = bf16[2048,768]{1,0:T(8,128)(2,1)} async-done(((bf16[512,768]{1,0:T(8,128)(2,1)}), bf16[2048,768]{1,0:T(8,128)(2,1)}) %all-gather.9.cloned.1.call-update) | async-done | bytes 3145744 | tf_op jit(solution)/shard_map/all_gather | solution.py:414
  241.9 2.8 bitcast_dynamic-update-slice_fusion
  246.3 10.9 %fusion.12 = f32[1536,1536]{1,0:T(8,128)} fusion(bf16[1024,1536]{1,0:T(8,128)(2,1)} %pad_maximum_fusion.1, bf16[512,1536]{1,0:T(8,128)(2,1)} %collective-permute-done.20, bf16[256,768]{1,0:T(8,128)(2,1)S(1)} %get-tuple-element.112, bf16[256,768]{1,0:T(8,128)(2,1)S(1)} %get-tuple-element.110, bf16[256,768]{1,0:T(8,128)(2,1)S(1)} %get-tuple-element.108, ...), kind=kOutput, calls=%fused_computation.19 | convolution fusion | flops 4847566848 | bytes 15728640 | tf_op jit(solution)/shard_map/dot_general | solution.py:435
  257.2 5.6 %fusion.1 = (f32[4,1536]{1,0:T(4,128)S(1)}, f32[256]{0:T(256)S(1)}, f32[256]{0:T(256)S(1)}) fusion(bf16[4,256,1536]{2,1,0:T(8,128)(2,1)} %bitcast.39, f32[256]{0:T(256)S(1)} %bitcast.134, f32[256]{0:T(256)S(1)} %bitcast.132, bf16[4,128,1536]{2,1,0:T(8,128)(2,1)S(1)} %copy-done.4, bf16[4,128,1536]{2,1,0:T(8,128)(2,1)S(1)} %copy-done.2, f32[4,1536]{1,0:T(4,128)S(1)} %mul.91), kind=kLoop, calls=%fused_computation.4 | loop fusion | flops 20440576 | bytes 6344704 | tf_op jit(solution)/shard_map/reduce_sum | solution.py:475
  263.3 2.8 collective-permute-start.23
  271.7 7.0 %collective-permute-done.19 = bf16[2,512,768]{2,1,0:T(8,128)(2,1)S(1)} collective-permute-done((bf16[2,512,768]{2,1,0:T(8,128)(2,1)S(1)}, bf16[2,512,768]{2,1,0:T(8,128)(2,1)S(1)}, u32[]{:S(2)}, u32[]{:S(2)}) %collective-permute-start.19) | collective-permute-done | bytes 1572896 | tf_op jit(solution)/shard_map/ppermute | solution.py:291
  282.6 2.6 convolution_add_fusion
  289.4 9.0 %fusion.22 = f32[1536,1536]{1,0:T(8,128)} fusion(bf16[512,1536]{1,0:T(8,128)(2,1)S(1)} %collective-permute-done.25, bf16[512,1536]{1,0:T(8,128)(2,1)S(1)} %get-tuple-element.88, bf16[512,1536]{1,0:T(8,128)(2,1)} %collective-permute-done.11, bf16[256,1536]{1,0:T(8,128)(2,1)S(1)} %copy-done.25, bf16[256,1536]{1,0:T(8,128)(2,1)S(1)} %bitcast.129), kind=kOutput, calls=%fused_computation.31 | convolution fusion | flops 4847566848 | bytes 15728640 | tf_op jit(solution)/shard_map/dot_general | solution.py:435
  298.4 8.3 %collective-permute-done.21 = bf16[256,1536]{1,0:T(8,128)(2,1)S(1)} collective-permute-done((bf16[256,1536]{1,0:T(8,128)(2,1)S(1)}, bf16[256,1536]{1,0:T(8,128)(2,1)S(1)}, u32[]{:S(2)}, u32[]{:S(2)}) %collective-permute-start.21) | collective-permute-done | bytes 786464 | tf_op jit(solution)/shard_map/ppermute | solution.py:291
  306.7 3.7 %fusion.38 = (bf16[1,256,1536]{2,1,0:T(8,128)(2,1)}, bf16[1,256,1536]{2,1,0:T(8,128)(2,1)}) fusion(bf16[256,1536]{1,0:T(8,128)(2,1)} %reduce-scatter.5.cloned.1.call-done, bf16[1,256,1536]{2,1,0:T(8,128)(2,1)S(1)} %copy-done.16, f32[256]{0:T(256)S(1)} %get-tuple-element.147, f32[256]{0:T(256)S(1)} %bitcast.135, f32[256]{0:T(256)S(1)} %bitcast.133, ...), kind=kLoop, calls=%fused_computation.67 | loop fusion | flops 6291456 | bytes 6301696 | tf_op jit(solution)/shard_map/reshape | solution.py:522
  (231 shorter events, 87.1 us)
Async XLA Ops:
  7.2 57.9 %all-gather.5.cloned.1.call-start = ((), (), s32[]{:S(2)}) async-start(), calls=%async_computation.2 | async-start | bytes 1966080 | tf_op jit(solution)/shard_map/all_gather | solution.py:306
  9.3 78.8 %all-gather.7.cloned.1.call-start = ((), (), s32[]{:S(2)}) async-start(), calls=%async_computation.3 | async-start | bytes 1966080 | tf_op jit(solution)/shard_map/all_gather | solution.py:306
  9.3 21.6 %collective-permute-start.7 = (bf16[256,1536]{1,0:T(8,128)(2,1)}, bf16[256,1536]{1,0:T(8,128)(2,1)S(1)}, u32[]{:S(2)}, u32[]{:S(2)}) collective-permute-start(bf16[256,1536]{1,0:T(8,128)(2,1)} %bitcast.127), channel_id=1, source_target_pairs={{0,8},{8,0},{1,9},{9,1},{2,10},{10,2},{3,11},{11,3},{4,12},{12,4},... | collective-permute-start | bytes 2359304 | tf_op jit(solution)/shard_map/ppermute | solution.py:291
  22.2 41.7 %collective-permute-start.9 = (bf16[2,256,768]{1,2,0:T(8,128)(2,1)}, bf16[2,256,768]{1,2,0:T(8,128)(2,1)}, u32[]{:S(2)}, u32[]{:S(2)}) collective-permute-start(bf16[2,256,768]{1,2,0:T(8,128)(2,1)} %pad_maximum_fusion.10), channel_id=1, source_target_pairs={{0,8},{8,0},{1,9},{9,1},{2,10},{10,2},{3,11},{11,3},{4,12},{12,4},... | collective-permute-start | bytes 2359304 | tf_op jit(solution)/shard_map/ppermute | solution.py:291
  22.2 127.9 %reduce-scatter.3.cloned.1.call-start = ((), (), s32[]{:S(2)}) async-start(), calls=%async_computation.4 | async-start | bytes 3932160 | tf_op jit(solution)/shard_map/reduce_scatter | solution.py:348
  32.5 31.3 %collective-permute-start.8 = (bf16[2,256,768]{1,2,0:T(8,128)(2,1)S(1)}, bf16[2,256,768]{1,2,0:T(8,128)(2,1)S(1)}, u32[]{:S(2)}, u32[]{:S(2)}) collective-permute-start(bf16[2,256,768]{1,2,0:T(8,128)(2,1)S(1)} %pad_maximum_fusion.9), channel_id=1, source_target_pairs={{0,8},{8,0},{1,9},{9,1},{2,10},{10,2},{3,11},{11,3},{4,12},{12,4},... | collective-permute-start | bytes 2359304 | tf_op jit(solution)/shard_map/ppermute | solution.py:291
  68.1 20.0 %collective-permute-start = (bf16[128,3072]{1,0:T(8,128)(2,1)S(1)}, bf16[128,3072]{1,0:T(8,128)(2,1)}, u32[]{:S(2)}, u32[]{:S(2)}) collective-permute-start(bf16[128,3072]{1,0:T(8,128)(2,1)S(1)} %get-tuple-element.44), channel_id=1, source_target_pairs={{0,8},{8,0},{1,9},{9,1},{2,10},{10,2},{3,11},{11,3},{4,12},{12,4},... | collective-permute-start | bytes 2359304 | tf_op jit(solution)/shard_map/ppermute | solution.py:291
  78.5 158.4 %all-gather.9.cloned.1.call-start = ((), (), s32[]{:S(2)}) async-start(), calls=%async_computation.6 | async-start | bytes 3932160 | tf_op jit(solution)/shard_map/all_gather | solution.py:414
  91.1 20.5 %collective-permute-start.1 = (bf16[128,3072]{1,0:T(8,128)(2,1)S(1)}, bf16[128,3072]{1,0:T(8,128)(2,1)S(1)}, u32[]{:S(2)}, u32[]{:S(2)}) collective-permute-start(bf16[128,3072]{1,0:T(8,128)(2,1)S(1)} %get-tuple-element.47), channel_id=1, source_target_pairs={{0,8},{8,0},{1,9},{9,1},{2,10},{10,2},{3,11},{11,3},{4,12},{12,4},... | collective-permute-start | bytes 2359304 | tf_op jit(solution)/shard_map/ppermute | solution.py:291
  103.6 17.7 %collective-permute-start.5 = (bf16[256,384]{1,0:T(8,128)(2,1)S(1)}, bf16[256,384]{1,0:T(8,128)(2,1)S(1)}, u32[]{:S(2)}, u32[]{:S(2)}) collective-permute-start(bf16[256,384]{1,0:T(8,128)(2,1)S(1)} %get-tuple-element.121), channel_id=1, source_target_pairs={{0,8},{8,0},{1,9},{9,1},{2,10},{10,2},{3,11},{11,3},{4,12},{12,4},... | collective-permute-start | bytes 589832 | tf_op jit(solution)/shard_map/ppermute | solution.py:291
  105.0 19.3 %collective-permute-start.3 = (f32[256,384]{1,0:T(8,128)S(1)}, f32[256,384]{1,0:T(8,128)S(1)}, u32[]{:S(2)}, u32[]{:S(2)}) collective-permute-start(f32[256,384]{1,0:T(8,128)S(1)} %get-tuple-element.117), channel_id=1, source_target_pairs={{0,8},{8,0},{1,9},{9,1},{2,10},{10,2},{3,11},{11,3},{4,12},{12,4},... | collective-permute-start | bytes 1179656 | tf_op jit(solution)/shard_map/ppermute | solution.py:291
  112.0 27.7 %collective-permute-start.10 = (bf16[512,1536]{1,0:T(8,128)(2,1)S(1)}, bf16[512,1536]{1,0:T(8,128)(2,1)S(1)}, u32[]{:S(2)}, u32[]{:S(2)}) collective-permute-start(bf16[512,1536]{1,0:T(8,128)(2,1)S(1)} %get-tuple-element.97), channel_id=1, source_target_pairs={{0,1},{1,0},{2,3},{3,2},{4,5},{5,4},{6,7},{7,6},{8,9},{9,8},{10,11... | collective-permute-start | bytes 4718600 | tf_op jit(solution)/shard_map/ppermute | solution.py:44
  115.8 19.9 %collective-permute-start.2 = (f32[256,384]{1,0:T(8,128)S(1)}, f32[256,384]{1,0:T(8,128)S(1)}, u32[]{:S(2)}, u32[]{:S(2)}) collective-permute-start(f32[256,384]{1,0:T(8,128)S(1)} %get-tuple-element.119), channel_id=1, source_target_pairs={{0,8},{8,0},{1,9},{9,1},{2,10},{10,2},{3,11},{11,3},{4,12},{12,4},... | collective-permute-start | bytes 1179656 | tf_op jit(solution)/shard_map/ppermute | solution.py:291
  120.7 14.9 %collective-permute-start.4 = (bf16[256,384]{1,0:T(8,128)(2,1)S(1)}, bf16[256,384]{1,0:T(8,128)(2,1)S(1)}, u32[]{:S(2)}, u32[]{:S(2)}) collective-permute-start(bf16[256,384]{1,0:T(8,128)(2,1)S(1)} %get-tuple-element.122), channel_id=1, source_target_pairs={{0,8},{8,0},{1,9},{9,1},{2,10},{10,2},{3,11},{11,3},{4,12},{12,4},... | collective-permute-start | bytes 589832 | tf_op jit(solution)/shard_map/ppermute | solution.py:291
  135.6 23.7 %collective-permute-start.14 = (f32[256,384]{1,0:T(8,128)}, f32[256,384]{1,0:T(8,128)S(1)}, u32[]{:S(2)}, u32[]{:S(2)}) collective-permute-start(f32[256,384]{1,0:T(8,128)} %get-tuple-element.58), channel_id=1, source_target_pairs={{0,8},{8,0},{1,9},{9,1},{2,10},{10,2},{3,11},{11,3},{4,12},{12,4},... | collective-permute-start | bytes 1179656 | tf_op jit(solution)/shard_map/ppermute | solution.py:291
  137.2 22.2 %collective-permute-start.13 = (f32[256,384]{1,0:T(8,128)}, f32[256,384]{1,0:T(8,128)S(1)}, u32[]{:S(2)}, u32[]{:S(2)}) collective-permute-start(f32[256,384]{1,0:T(8,128)} %get-tuple-element.56), channel_id=1, source_target_pairs={{0,8},{8,0},{1,9},{9,1},{2,10},{10,2},{3,11},{11,3},{4,12},{12,4},... | collective-permute-start | bytes 1179656 | tf_op jit(solution)/shard_map/ppermute | solution.py:291
  137.7 25.1 %collective-permute-start.6 = (bf16[256,384]{1,0:T(8,128)(2,1)}, bf16[256,384]{1,0:T(8,128)(2,1)}, u32[]{:S(2)}, u32[]{:S(2)}) collective-permute-start(bf16[256,384]{1,0:T(8,128)(2,1)} %get-tuple-element.48), channel_id=1, source_target_pairs={{0,8},{8,0},{1,9},{9,1},{2,10},{10,2},{3,11},{11,3},{4,12},{12,4},... | collective-permute-start | bytes 589832 | tf_op jit(solution)/shard_map/ppermute | solution.py:291
  139.2 23.6 %collective-permute-start.12 = (bf16[256,384]{1,0:T(8,128)(2,1)}, bf16[256,384]{1,0:T(8,128)(2,1)}, u32[]{:S(2)}, u32[]{:S(2)}) collective-permute-start(bf16[256,384]{1,0:T(8,128)(2,1)} %get-tuple-element.54), channel_id=1, source_target_pairs={{0,8},{8,0},{1,9},{9,1},{2,10},{10,2},{3,11},{11,3},{4,12},{12,4},... | collective-permute-start | bytes 589832 | tf_op jit(solution)/shard_map/ppermute | solution.py:291
  173.7 17.8 %collective-permute-start.15 = (bf16[2,256,768]{2,1,0:T(8,128)(2,1)S(1)}, bf16[2,256,768]{2,1,0:T(8,128)(2,1)}, u32[]{:S(2)}, u32[]{:S(2)}) collective-permute-start(bf16[2,256,768]{2,1,0:T(8,128)(2,1)S(1)} %get-tuple-element.64), channel_id=1, source_target_pairs={{0,8},{8,0},{1,9},{9,1},{2,10},{10,2},{3,11},{11,3},{4,12},{12,4},... | collective-permute-start | bytes 2359304 | tf_op jit(solution)/shard_map/ppermute | solution.py:291
  175.4 131.4 %reduce-scatter.5.cloned.1.call-start = ((), (), s32[]{:S(2)}) async-start(), calls=%async_computation.5 | async-start | bytes 3932160 | tf_op jit(solution)/shard_map/reduce_scatter | solution.py:456
  177.9 111.4 %collective-permute-start.11 = (bf16[512,1536]{1,0:T(8,128)(2,1)}, bf16[512,1536]{1,0:T(8,128)(2,1)}, u32[]{:S(2)}, u32[]{:S(2)}) collective-permute-start(bf16[512,1536]{1,0:T(8,128)(2,1)} %pad_maximum_fusion.5), channel_id=1, source_target_pairs={{0,1},{1,0},{2,3},{3,2},{4,5},{5,4},{6,7},{7,6},{8,9},{9,8},{10,11... | collective-permute-start | bytes 4718600 | tf_op jit(solution)/shard_map/ppermute | solution.py:44
  191.5 17.8 %collective-permute-start.16 = (bf16[2,256,768]{2,1,0:T(8,128)(2,1)S(1)}, bf16[2,256,768]{2,1,0:T(8,128)(2,1)}, u32[]{:S(2)}, u32[]{:S(2)}) collective-permute-start(bf16[2,256,768]{2,1,0:T(8,128)(2,1)S(1)} %get-tuple-element.62), channel_id=1, source_target_pairs={{0,8},{8,0},{1,9},{9,1},{2,10},{10,2},{3,11},{11,3},{4,12},{12,4},... | collective-permute-start | bytes 2359304 | tf_op jit(solution)/shard_map/ppermute | solution.py:291
  207.6 34.3 %collective-permute-start.18 = (bf16[2,256,1536]{2,1,0:T(8,128)(2,1)S(1)}, bf16[2,256,1536]{2,1,0:T(8,128)(2,1)}, u32[]{:S(2)}, u32[]{:S(2)}) collective-permute-start(bf16[2,256,1536]{2,1,0:T(8,128)(2,1)S(1)} %back_block.2), channel_id=1, source_target_pairs={{0,8},{8,0},{1,9},{9,1},{2,10},{10,2},{3,11},{11,3},{4,12},{12,4},... | collective-permute-start | bytes 4718600 | tf_op jit(solution)/shard_map/ppermute | solution.py:291
  210.9 13.8 %collective-permute-start.17 = (bf16[512,1536]{1,0:T(8,128)(2,1)S(1)}, bf16[512,1536]{1,0:T(8,128)(2,1)S(1)}, u32[]{:S(2)}, u32[]{:S(2)}) collective-permute-start(bf16[512,1536]{1,0:T(8,128)(2,1)S(1)} %maximum_maximum_fusion.1), channel_id=1, source_target_pairs={{0,1},{1,0},{2,3},{3,2},{4,5},{5,4},{6,7},{7,6},{8,9},{9,8},{10,11... | collective-permute-start | bytes 4718600 | tf_op jit(solution)/shard_map/ppermute | solution.py:44
  212.2 34.1 %collective-permute-start.20 = (bf16[512,1536]{1,0:T(8,128)(2,1)}, bf16[512,1536]{1,0:T(8,128)(2,1)}, u32[]{:S(2)}, u32[]{:S(2)}) collective-permute-start(bf16[512,1536]{1,0:T(8,128)(2,1)} %maximum_maximum_fusion.2), channel_id=1, source_target_pairs={{0,1},{1,0},{2,3},{3,2},{4,5},{5,4},{6,7},{7,6},{8,9},{9,8},{10,11... | collective-permute-start | bytes 4718600 | tf_op jit(solution)/shard_map/ppermute | solution.py:44
  244.7 33.9 %collective-permute-start.19 = (bf16[2,512,768]{2,1,0:T(8,128)(2,1)S(1)}, bf16[2,512,768]{2,1,0:T(8,128)(2,1)S(1)}, u32[]{:S(2)}, u32[]{:S(2)}) collective-permute-start(bf16[2,512,768]{2,1,0:T(8,128)(2,1)S(1)} %copy-done.21), channel_id=1, source_target_pairs={{0,8},{8,0},{1,9},{9,1},{2,10},{10,2},{3,11},{11,3},{4,12},{12,4},... | collective-permute-start | bytes 4718600 | tf_op jit(solution)/shard_map/ppermute | solution.py:291
  263.0 8.0 %collective-permute-start.22 = (f32[2048]{0:T(1024)S(1)}, f32[2048]{0:T(1024)S(1)}, u32[]{:S(2)}, u32[]{:S(2)}) collective-permute-start(f32[2048]{0:T(1024)S(1)} %get-tuple-element.148), channel_id=1, source_target_pairs={{0,2},{2,4},{4,6},{6,0},{1,3},{3,5},{5,7},{7,1},{8,10},{10,12},{12... | collective-permute-start | bytes 24584 | tf_op jit(solution)/shard_map/ppermute | solution.py:44
  263.3 7.8 %collective-permute-start.23 = (f32[2048]{0:T(1024)S(1)}, f32[2048]{0:T(1024)S(1)}, u32[]{:S(2)}, u32[]{:S(2)}) collective-permute-start(f32[2048]{0:T(1024)S(1)} %get-tuple-element.149), channel_id=1, source_target_pairs={{0,4},{2,6},{4,0},{6,2},{1,5},{3,7},{5,1},{7,3},{8,12},{10,14},{12... | collective-permute-start | bytes 24584 | tf_op jit(solution)/shard_map/ppermute | solution.py:44
  271.0 11.2 %collective-permute-start.26 = (f32[31,768]{1,0:T(8,128)S(1)}, f32[31,768]{1,0:T(8,128)S(1)}, u32[]{:S(2)}, u32[]{:S(2)}) collective-permute-start(f32[31,768]{1,0:T(8,128)S(1)} %copy-done.26), channel_id=1, source_target_pairs={{0,1},{1,0},{2,3},{3,2},{4,5},{5,4},{6,7},{7,6},{8,9},{9,8},{10,11... | collective-permute-start | bytes 285704 | tf_op jit(solution)/shard_map/ppermute | solution.py:44
  271.1 9.3 %collective-permute-start.28 = (f32[1536]{0:T(1024)S(1)}, f32[1536]{0:T(1024)S(1)}, u32[]{:S(2)}, u32[]{:S(2)}) collective-permute-start(f32[1536]{0:T(1024)S(1)} %slice.158), channel_id=1, source_target_pairs={{0,1},{1,0},{2,3},{3,2},{4,5},{5,4},{6,7},{7,6},{8,9},{9,8},{10,11... | collective-permute-start | bytes 18440 | tf_op jit(solution)/shard_map/ppermute | solution.py:44
  280.3 9.0 %collective-permute-start.25 = (bf16[512,1536]{1,0:T(8,128)(2,1)S(1)}, bf16[512,1536]{1,0:T(8,128)(2,1)S(1)}, u32[]{:S(2)}, u32[]{:S(2)}) collective-permute-start(bf16[512,1536]{1,0:T(8,128)(2,1)S(1)} %get-tuple-element.89), channel_id=1, source_target_pairs={{0,1},{1,0},{2,3},{3,2},{4,5},{5,4},{6,7},{7,6},{8,9},{9,8},{10,11... | collective-permute-start | bytes 4718600 | tf_op jit(solution)/shard_map/ppermute | solution.py:44
  287.8 18.9 %collective-permute-start.21 = (bf16[256,1536]{1,0:T(8,128)(2,1)S(1)}, bf16[256,1536]{1,0:T(8,128)(2,1)S(1)}, u32[]{:S(2)}, u32[]{:S(2)}) collective-permute-start(bf16[256,1536]{1,0:T(8,128)(2,1)S(1)} %slice.194), channel_id=1, source_target_pairs={{0,8},{8,0},{1,9},{9,1},{2,10},{10,2},{3,11},{11,3},{4,12},{12,4},... | collective-permute-start | bytes 2359304 | tf_op jit(solution)/shard_map/ppermute | solution.py:291
  (51 other events, 460.8 us)
Sparse Core Ops, SparseCore 0:
  10.1 39.7 all-gather.4
  52.1 35.9 all-gather.6
  91.0 59.0 reduce-scatter.2
  175.5 61.3 all-gather.8
  244.8 60.9 reduce-scatter.4
